TPU v7x, 32 devices: a whole 2x2x4 slice. The times are simulated.
32 devices in a mesh: dp: 4 (over y, x), space: 8 (over z, core).
Axes of the slice: x: 2, y: 2, z: 4, core: 2. Of those that a mesh axis runs over, the one named last changes fastest.
Arguments:
- signal: bfloat16 [4, 512, 64, 1280], P('dp', None, 'space'), may hold values from -6 to 6
- cotangent: bfloat16 [4, 512, 64, 1280], P('dp', None, 'space'), may hold values from -6 to 6
- spec_weight: bfloat16 [2, 20, 20, 73728], P(None, None, None, 'space'), may hold values from -1.25 to 1.25
- point_weight: bfloat16 [20, 20], replicated, may hold values from -1.25 to 1.25
- bias: bfloat16 [20], replicated, may hold values from -3 to 3
Outputs:
- grad_signal: bfloat16 [4, 512, 64, 1280], P('dp', None, 'space')
- spec_grad: float32 [2, 20, 20, 73728], P(None, None, None, ('space', 'dp'))
All inputs are finite; a program needn't handle non-finite values.
Results may differ from a plain program's by a relative error of at most 0.024.
Values may be sent and summed in bfloat16 or wider, within the bound.
No kernel may reach another device: no remote copies, remote signals or barrier semaphores. Data moves between devices by JAX's collectives and lax.ppermute only.
A program may use at most 256 MiB of HBM per device.

v0:
```python
import math

import jax
import jax.numpy as jnp
from jax import lax
from jax.sharding import PartitionSpec as P

NX = 64
NY = 64
NZ = 32
NT = 16
C = 20
MX = 24
MY = 24
MZ = 16
MT = 8
MZT = 128


def retained(mode_count, length):
    positions = jnp.arange(mode_count, dtype=jnp.int32)
    return jnp.where(positions < mode_count // 2, positions, length - mode_count + positions)


def complex_table(mode_count, length):
    freqs = retained(mode_count, length)
    points = jnp.arange(length, dtype=jnp.int32)
    turns = freqs[:, None] * points[None, :] % length
    angles = turns.astype(jnp.float32) * (2.0 * math.pi / length)
    norm_scale = 1.0 / math.sqrt(length)
    cos_part = jnp.cos(angles) * norm_scale
    sin_part = jnp.sin(angles) * norm_scale
    upper_rows = jnp.stack([cos_part, sin_part], axis=1)
    lower_rows = jnp.stack([-sin_part, cos_part], axis=1)
    return jnp.stack([upper_rows, lower_rows], axis=0).astype(jnp.bfloat16)


def depth_tables():
    depth_freq = retained(MZ, NZ)
    time_freq = jnp.arange(MT, dtype=jnp.int32)
    depth_pos = jnp.arange(NZ, dtype=jnp.int32)
    time_pos = jnp.arange(NT, dtype=jnp.int32)
    depth_turns = depth_freq[:, None] * depth_pos[None, :] % NZ
    time_turns = time_freq[:, None] * time_pos[None, :] % NT
    turns = depth_turns[:, None, :, None] * NT + time_turns[None, :, None, :] * NZ
    angles = turns.astype(jnp.float32) * (2.0 * math.pi / (NZ * NT))
    norm_scale = 1.0 / math.sqrt(NZ * NT)
    forward = jnp.stack([jnp.cos(angles), -jnp.sin(angles)], axis=2) * norm_scale
    doubling = jnp.where(time_freq == 0, 1.0, 2.0).astype(jnp.float32)
    inverse = forward * doubling[None, :, None, None, None]
    return (
        forward.reshape(MZT, 2, NZ * NT).astype(jnp.bfloat16),
        inverse.reshape(MZT, 2, NZ * NT).astype(jnp.bfloat16),
    )


def gelu_slope(pre_act):
    cumulative = 0.5 * (1.0 + lax.erf(pre_act * (1.0 / math.sqrt(2.0))))
    density = jnp.exp(-0.5 * pre_act * pre_act) * (1.0 / math.sqrt(2.0 * math.pi))
    return cumulative + pre_act * density


def block_tables(table_y):
    identity = jnp.eye(C, dtype=jnp.float32)
    wide = table_y.astype(jnp.float32)
    rows = []
    for part_in in range(2):
        row = []
        for part_out in range(2):
            block = jnp.einsum("cd,jy->cydj", identity, wide[part_out, :, part_in, :])
            row.append(block.reshape(C * NY, C * MY).astype(jnp.bfloat16))
        rows.append(row)
    return rows


def forward_y(blocks, real_in, imag_in):
    outputs = []
    for part_out in range(2):
        total = jnp.einsum(
            "smxr,rK->smxK", real_in, blocks[0][part_out], preferred_element_type=jnp.float32
        ) + jnp.einsum(
            "smxr,rK->smxK", imag_in, blocks[1][part_out], preferred_element_type=jnp.float32
        )
        outputs.append(total.astype(jnp.bfloat16))
    return (outputs[0], outputs[1])


def inverse_y(blocks, real_in, imag_in):
    outputs = []
    for part_out in range(2):
        total = jnp.einsum(
            "smxK,rK->smxr", real_in, blocks[part_out][0], preferred_element_type=jnp.float32
        ) + jnp.einsum(
            "smxK,rK->smxr", imag_in, blocks[part_out][1], preferred_element_type=jnp.float32
        )
        outputs.append(total.astype(jnp.bfloat16))
    return (outputs[0], outputs[1])


def forward_x(table_x, real_in, imag_in):
    samples, modes_here, cells, merged = real_in.shape
    total = jnp.einsum(
        "Pix,smxr->sPmir", table_x[:, :, 0, :], real_in, preferred_element_type=jnp.float32
    ) + jnp.einsum(
        "Pix,smxr->sPmir", table_x[:, :, 1, :], imag_in, preferred_element_type=jnp.float32
    )
    rounded = total.astype(jnp.bfloat16).reshape(samples, 2, modes_here, MX, C, MY)
    return jnp.transpose(rounded, (0, 1, 4, 2, 3, 5)).reshape(samples, 2, C, modes_here * MX * MY)


def inverse_x(table_x, spectrum):
    samples = spectrum.shape[0]
    unmerged = spectrum.reshape(samples, 2, C, -1, MX, MY)
    modes_here = unmerged.shape[3]
    moved = jnp.transpose(unmerged, (0, 1, 3, 4, 2, 5)).reshape(samples, 2, modes_here, MX, C * MY)
    real_out = jnp.einsum(
        "Pix,sPmir->smxr", table_x[:, :, 0, :], moved, preferred_element_type=jnp.float32
    )
    imag_out = jnp.einsum(
        "Pix,sPmir->smxr", table_x[:, :, 1, :], moved, preferred_element_type=jnp.float32
    )
    return (real_out.astype(jnp.bfloat16), imag_out.astype(jnp.bfloat16))


def analyse(blocks, table_x, coeffs):
    samples, rows_all, cells, merged = coeffs.shape
    split = coeffs.reshape(samples, MZT, 2, cells, merged)
    moved = lax.all_to_all(split, "space", split_axis=1, concat_axis=3, tiled=True)
    real_m, imag_m = forward_y(blocks, moved[:, :, 0], moved[:, :, 1])
    return forward_x(table_x, real_m, imag_m)


def synthesise(blocks, table_x, spectrum):
    real_x, imag_x = inverse_x(table_x, spectrum)
    real_y, imag_y = inverse_y(blocks, real_x, imag_x)
    real_out, imag_out = (
        lax.all_to_all(real_y, "space", split_axis=2, concat_axis=1, tiled=True),
        lax.all_to_all(imag_y, "space", split_axis=2, concat_axis=1, tiled=True),
    )
    return (real_out, imag_out)


def to_grid(table, real_in, imag_in):
    return jnp.einsum(
        "mz,smxr->szxr", table[:, 0, :], real_in, preferred_element_type=jnp.float32
    ) + jnp.einsum("mz,smxr->szxr", table[:, 1, :], imag_in, preferred_element_type=jnp.float32)


def weight_terms(u_hat, h_hat):
    real_part = jnp.einsum(
        "gsik,gsok->giok", u_hat[:, :, 0], h_hat[:, :, 0], preferred_element_type=jnp.float32
    ) + jnp.einsum(
        "gsik,gsok->giok", u_hat[:, :, 1], h_hat[:, :, 1], preferred_element_type=jnp.float32
    )
    imag_part = jnp.einsum(
        "gsik,gsok->giok", u_hat[:, :, 0], h_hat[:, :, 1], preferred_element_type=jnp.float32
    ) - jnp.einsum(
        "gsik,gsok->giok", u_hat[:, :, 1], h_hat[:, :, 0], preferred_element_type=jnp.float32
    )
    return jnp.stack([real_part, imag_part], axis=1)


def local(signal, cotangent, spec_weight, point_weight, bias):
    samples, depth_len, x_rows, merged = signal.shape
    depth_table, depth_inverse = depth_tables()
    table_y = complex_table(MY, NY)
    table_x = complex_table(MX, NX)
    blocks = block_tables(table_y)
    point_block = (
        jnp.einsum("co,yz->cyoz", point_weight.astype(jnp.float32), jnp.eye(NY, dtype=jnp.float32))
        .reshape(C * NY, C * NY)
        .astype(jnp.bfloat16)
    )
    bias_row = jnp.repeat(bias.astype(jnp.float32), NY)
    w_real = spec_weight[0]
    w_imag = spec_weight[1]
    forward_flat = depth_table.reshape(2 * MZT, depth_len)
    inverse_flat = depth_inverse.reshape(2 * MZT, depth_len)
    coeffs = jnp.einsum(
        "qz,szxr->sqxr", forward_flat, signal, preferred_element_type=jnp.float32
    ).astype(jnp.bfloat16)
    u_hat = analyse(blocks, table_x, coeffs)
    v_real = jnp.einsum(
        "sik,iok->sok", u_hat[:, 0], w_real, preferred_element_type=jnp.float32
    ) - jnp.einsum("sik,iok->sok", u_hat[:, 1], w_imag, preferred_element_type=jnp.float32)
    v_imag = jnp.einsum(
        "sik,iok->sok", u_hat[:, 1], w_real, preferred_element_type=jnp.float32
    ) + jnp.einsum("sik,iok->sok", u_hat[:, 0], w_imag, preferred_element_type=jnp.float32)
    v_hat = jnp.stack([v_real, v_imag], axis=1).astype(jnp.bfloat16)
    real_syn, imag_syn = synthesise(blocks, table_x, v_hat)
    spectral = to_grid(depth_inverse, real_syn, imag_syn)
    direct = jnp.einsum("szxr,rR->szxR", signal, point_block, preferred_element_type=jnp.float32)
    pre_act = spectral + direct + bias_row
    hidden = (cotangent.astype(jnp.float32) * gelu_slope(pre_act)).astype(jnp.bfloat16)
    e_coeffs = jnp.einsum(
        "qz,szxr->sqxr", inverse_flat, hidden, preferred_element_type=jnp.float32
    ).astype(jnp.bfloat16)
    h_hat = analyse(blocks, table_x, e_coeffs)
    d_real = jnp.einsum(
        "sok,iok->sik", h_hat[:, 0], w_real, preferred_element_type=jnp.float32
    ) + jnp.einsum("sok,iok->sik", h_hat[:, 1], w_imag, preferred_element_type=jnp.float32)
    d_imag = jnp.einsum(
        "sok,iok->sik", h_hat[:, 1], w_real, preferred_element_type=jnp.float32
    ) - jnp.einsum("sok,iok->sik", h_hat[:, 0], w_imag, preferred_element_type=jnp.float32)
    d_hat = jnp.stack([d_real, d_imag], axis=1).astype(jnp.bfloat16)
    real_back, imag_back = synthesise(blocks, table_x, d_hat)
    returned = to_grid(depth_table, real_back, imag_back)
    pointwise = jnp.einsum("szxR,rR->szxr", hidden, point_block, preferred_element_type=jnp.float32)
    grad_signal = (returned + pointwise).astype(jnp.bfloat16)
    partial_value = weight_terms(u_hat[None], h_hat[None])[0]
    spec_grad = lax.psum_scatter(
        partial_value.astype(jnp.bfloat16), "dp", scatter_dimension=3, tiled=True
    ).astype(jnp.float32)
    return (grad_signal, spec_grad)


def solution(mesh):
    return jax.shard_map(
        local,
        mesh=mesh,
        in_specs=(
            P("dp", None, "space", None),
            P("dp", None, "space", None),
            P(None, None, None, "space"),
            P(),
            P(),
        ),
        out_specs=(P("dp", None, "space", None), P(None, None, None, ("space", "dp"))),
        check_vma=False,
    )
```

profile of v0, /device:TPU:0, one launch (start us, length us, event | category | flops | bytes accessed | tf_op | source)
XLA Modules:
  0.0 866.7 jit_solution(4177913953414593239)
XLA Ops:
  7.4 8.9 %sine_negate_fusion = (f32[16,8,32,16]{3,2,1,0:T(8,128)}, f32[16,8,32,16]{3,2,1,0:T(8,128)S(1)}) fusion(s32[8,16]{1,0:T(8,128)S(1)} %fusion.101, s32[16,32]{1,0:T(8,128)S(1)} %fusion.90), kind=kLoop, calls=%fused_computation.94 | loop fusion | flops 262144 | bytes 526848 | tf_op jit(solution)/shard_map/neg | solution.py:48
  16.3 3.1 reshape.710
  22.9 7.9 fusion.27
  30.7 5.3 copy.236
  36.0 6.6 all-to-all-start
  42.8 4.5 fusion.39
  47.3 4.6 reshape.725
  51.8 4.5 reshape.721
  56.4 4.5 reshape.724
  63.5 29.8 %fusion.106 = (bf16[1,20,20,9216]{3,0,2,1:T(2,128)(2,1)}, bf16[1,20,20,9216]{3,0,2,1:T(2,128)(2,1)}) fusion(bf16[2,20,20,9216]{3,0,2,1:T(2,128)(2,1)} %param.7), kind=kLoop, calls=%fused_computation.200 | loop fusion | bytes 29491200 | tf_op jit(solution)/shard_map/slice | solution.py:176
  93.3 65.8 %all-to-all-done = bf16[1,128,2,8,1280]{4,3,2,0,1:T(8,128)(2,1)} async-done(((bf16[1,128,2,8,1280]{4,3,2,0,1:T(8,128)(2,1)}), bf16[1,128,2,8,1280]{4,3,2,0,1:T(8,128)(2,1)}, u32[]{:S(2)}, u32[]{:S(2)}) %all-to-all-start) | async-done | bytes 5242912 | tf_op jit(solution)/shard_map/all_to_all | solution.py:128
  159.1 3.2 copy.304
  162.4 3.0 fusion.47
  168.3 5.3 fusion.56
  173.6 5.9 fusion.65
  180.7 4.5 reshape.684
  185.2 5.2 copy.141
  190.4 6.5 reshape.685
  198.3 19.7 %fusion.8 = (f32[9216,20]{0,1:T(8,128)S(1)}, f32[9216,20]{0,1:T(8,128)S(1)}, f32[9216,20]{0,1:T(8,128)S(1)}, f32[9216,20]{0,1:T(8,128)}) fusion(f32[9216,20]{0,1:T(8,128)S(1)} %get-tuple-element.57, bf16[1,20,20,9216]{3,0,2,1:T(2,128)(2,1)} %get-tuple-element.25, f32[9216,20]{0,1:T(8,128)S(1)} %get-tuple-element.56, ...), kind=kLoop, calls=%fused_computation.19 | loop fusion | flops 36126720 | bytes 19169280 | tf_op jit(solution)/shard_map/sik,iok->sok/dot_general | solution.py:183
  218.8 4.9 stack.75
  225.7 5.1 stack.74
  230.8 3.0 maximum_bitcast_fusion.1
  233.8 6.4 copy.144
  240.2 6.3 reshape.688
  256.7 4.4 all-to-all-start.2
  268.4 53.0 %all-to-all-done.2 = bf16[1,16,64,1280]{3,1,0,2:T(8,128)(2,1)} async-done(((bf16[1,16,64,1280]{3,1,0,2:T(8,128)(2,1)}), bf16[1,16,64,1280]{3,1,0,2:T(8,128)(2,1)}, u32[]{:S(2)}, u32[]{:S(2)}) %all-to-all-start.2) | async-done | bytes 2621472 | tf_op jit(solution)/shard_map/all_to_all | solution.py:138
  321.4 4.6 all-to-all-start.1
  326.6 4.9 fusion.23
  331.5 10.0 %convert_element_type.327 = bf16[1280,1280]{1,0:T(8,128)(2,1)} reshape(bf16[20,64,20,64]{3,2,1,0:T(8,128)(2,1)} %fusion.23) | data formatting | bytes 6553600 | tf_op jit(solution)/shard_map/convert_element_type | solution.py:172
  341.4 16.4 %copy.132 = bf16[1,512,8,1280]{1,3,2,0:T(8,128)(2,1)} copy(bf16[1,512,8,1280]{3,2,1,0:T(8,128)(2,1)} %param.6) | data formatting | bytes 20971520 | tf_op args[1]
  357.8 21.6 %fusion.17 = f32[1280,512,8]{1,0,2:T(8,128)} fusion(bf16[512,8,1280]{2,1,0:T(8,128)(2,1)} %bitcast.477, bf16[1280,1280]{1,0:T(8,128)(2,1)} %convert_element_type.327), kind=kOutput, calls=%fused_computation.32 | convolution fusion | flops 13421772800 | bytes 34734080 | tf_op jit(solution)/shard_map/szxr,rR->szxR/dot_general | solution.py:192
  389.0 9.0 %fusion.44 = f32[8,1280,512]{2,1,0:T(8,128)} fusion(bf16[128,8,1280]{2,1,0:T(8,128)(2,1)S(1)} %bitcast.458, bf16[128,2,512]{2,0,1:T(8,128)(2,1)S(1)} %copy-done.18), kind=kOutput, calls=%fused_computation.75 | convolution fusion | flops 1342177280 | bytes 23724032 | tf_op jit(solution)/shard_map/mz,smxr->szxr/dot_general | solution.py:144
  398.0 21.2 %fusion.16 = bf16[512,8,1280]{0,2,1:T(8,128)(2,1)S(1)} fusion(f32[1280,512,8]{1,0,2:T(8,128)} %fusion.17, f32[8,1280,512]{2,1,0:T(8,128)} %fusion.44, bf16[1,512,8,1280]{1,3,2,0:T(8,128)(2,1)} %copy.132, f32[1280]{0:T(1024)S(1)} %add.243, bf16[128,8,1280]{2,1,0:T(8,128)(2,1)} %bitcast.475, bf16[128,2,512]{2,0,1:T(8,128)(2,1)S(1)} %copy-done.18), kind=kOutput, calls=%fused_computation.31 | convolution fusion | flops 1415577600 | bytes 65675264 | tf_op jit(solution)/shard_map/mz,smxr->szxr/dot_general | solution.py:146
  419.3 3.4 fusion.30
  423.4 5.3 copy.238
  428.6 4.7 all-to-all-start.3
  433.3 6.3 broadcast_in_dim_reshape.8
  442.2 107.5 %all-to-all-done.3 = bf16[1,128,2,8,1280]{4,3,2,0,1:T(8,128)(2,1)} async-done(((bf16[1,128,2,8,1280]{4,3,2,0,1:T(8,128)(2,1)}), bf16[1,128,2,8,1280]{4,3,2,0,1:T(8,128)(2,1)}, u32[]{:S(2)}, u32[]{:S(2)}) %all-to-all-start.3) | async-done | bytes 5242912 | tf_op jit(solution)/shard_map/all_to_all | solution.py:128
  549.8 3.2 copy.303
  553.0 3.1 fusion.50
  559.0 5.4 fusion.59
  564.3 5.9 fusion.66
  571.5 4.5 reshape.697
  576.0 5.1 copy.162
  581.1 6.2 broadcast_in_dim_reshape.7
  588.7 5.8 fusion.21
  594.5 8.7 %maximum_bitcast_fusion = bf16[2,20,20,9216]{3,2,1,0:T(8,128)(2,1)} fusion(bf16[1,1,20,20,9216]{4,3,2,1,0:T(8,128)(2,1)S(1)} %get-tuple-element.27, bf16[1,1,20,20,9216]{4,3,2,1,0:T(8,128)(2,1)S(1)} %get-tuple-element.26), kind=kLoop, calls=%fused_computation.27 | loop fusion | flops 7372800 | bytes 29491200 | tf_op jit(solution)/shard_map/convert_element_type | solution.py:212
  603.2 6.2 reshape.698
  610.7 23.0 %fusion.12 = (f32[9216,20]{0,1:T(8,128)S(1)}, f32[9216,20]{0,1:T(8,128)S(1)}, f32[9216,20]{0,1:T(8,128)S(1)}, f32[9216,20]{0,1:T(8,128)}) fusion(f32[9216,20]{0,1:T(8,128)S(1)} %bitcast_convert_fusion.5, bf16[1,20,20,9216]{3,0,2,1:T(2,128)(2,1)} %get-tuple-element.25, f32[9216,20]{0,1:T(8,128)S(1)} %bitcast_convert_fusion.4, ...), kind=kLoop, calls=%fused_computation.23 | loop fusion | flops 36126720 | bytes 19169280 | tf_op jit(solution)/shard_map/sok,iok->sik/dot_general | solution.py:199
  634.5 5.3 stack.78
  641.8 5.0 stack.77
  646.8 3.3 maximum_bitcast_fusion.2
  650.1 6.4 copy.163
  656.5 6.6 reshape.701
  673.4 4.4 all-to-all-start.5
  683.8 54.3 %all-to-all-done.5 = bf16[1,16,64,1280]{3,1,0,2:T(8,128)(2,1)} async-done(((bf16[1,16,64,1280]{3,1,0,2:T(8,128)(2,1)}), bf16[1,16,64,1280]{3,1,0,2:T(8,128)(2,1)}, u32[]{:S(2)}, u32[]{:S(2)}) %all-to-all-start.5) | async-done | bytes 2621472 | tf_op jit(solution)/shard_map/all_to_all | solution.py:138
  738.1 4.6 all-to-all-start.4
  742.7 8.8 %reshape.756 = bf16[1280,1280,1]{1,0,2:T(8,128)(2,1)S(1)} reshape(bf16[20,64,20,64]{3,2,1,0:T(8,128)(2,1)} %fusion.23) | data formatting | bytes 6553600 | tf_op jit(solution)/shard_map/convert_element_type | solution.py:172
  751.6 20.5 %fusion.113 = f32[512,8,1280]{0,2,1:T(8,128)} fusion(bf16[1280,1280,1]{1,0,2:T(8,128)(2,1)S(1)} %reshape.756, bf16[512,8,1280]{0,2,1:T(8,128)(2,1)} %copy-done), kind=kOutput, calls=%fused_computation.207 | convolution fusion | flops 13421772800 | bytes 34734080 | tf_op jit(solution)/shard_map/szxR,rR->szxr/dot_general | solution.py:208
  774.7 28.3 %all-to-all-done.4 = bf16[1,16,64,1280]{3,1,0,2:T(8,128)(2,1)} async-done(((bf16[1,16,64,1280]{3,1,0,2:T(8,128)(2,1)}), bf16[1,16,64,1280]{3,1,0,2:T(8,128)(2,1)}, u32[]{:S(2)}, u32[]{:S(2)}) %all-to-all-start.4) | async-done | bytes 2621472 | tf_op jit(solution)/shard_map/all_to_all | solution.py:137
  806.5 8.6 fusion.41
  815.1 18.5 %fusion.6 = bf16[1,512,8,1280]{1,3,2,0:T(8,128)(2,1)} fusion(f32[512,8,1280]{0,2,1:T(8,128)} %fusion.113, f32[8,1280,512]{2,1,0:T(8,128)} %fusion.41, bf16[128,8,1280]{2,1,0:T(8,128)(2,1)S(1)} %bitcast.460, bf16[128,2,512]{2,0,1:T(8,128)(2,1)S(1)} %copy-done.17), kind=kOutput, calls=%fused_computation.16 | convolution fusion | flops 1357905920 | bytes 55181312 | tf_op jit(solution)/shard_map/mz,smxr->szxr/dot_general | solution.py:146
  833.6 16.9 %copy.176 = bf16[1,512,8,1280]{3,2,1,0:T(8,128)(2,1)} copy(bf16[1,512,8,1280]{1,3,2,0:T(8,128)(2,1)} %fusion.6) | data formatting | bytes 20971520
  850.5 9.1 %copy.177 = f32[2,20,20,2304]{3,0,2,1:T(2,128)} copy(bf16[2,20,20,2304]{3,2,1,0:T(8,128)(2,1)} %reduce-scatter.2.cloned.1.call-done) | data formatting | bytes 11059200
  (114 shorter events, 77.4 us)
Async XLA Ops:
  21.8 0.7 copy-start.16
  36.0 123.1 %all-to-all-start = ((bf16[1,128,2,8,1280]{4,3,2,0,1:T(8,128)(2,1)}), bf16[1,128,2,8,1280]{4,3,2,0,1:T(8,128)(2,1)}, u32[]{:S(2)}, u32[]{:S(2)}) async-start(bf16[1,128,2,8,1280]{4,3,2,0,1:T(8,128)(2,1)} %bitcast.454), calls=%async_computation | async-start | bytes 10485760 | tf_op jit(solution)/shard_map/all_to_all | solution.py:128
  159.1 3.2 copy-start.1
  162.3 3.1 copy-start.12
  162.4 3.0 copy-start.3
  165.4 2.9 copy-start.2
  249.7 1.0 copy-start.11
  250.7 1.5 copy-start.7
  256.7 64.7 %all-to-all-start.2 = ((bf16[1,16,64,1280]{3,1,0,2:T(8,128)(2,1)}), bf16[1,16,64,1280]{3,1,0,2:T(8,128)(2,1)}, u32[]{:S(2)}, u32[]{:S(2)}) async-start(bf16[1,16,64,1280]{3,1,0,2:T(8,128)(2,1)} %copy.149), calls=%async_computation.2 | async-start | bytes 5242880 | tf_op jit(solution)/shard_map/all_to_all | solution.py:138
  261.1 2.9 copy-start.4
  268.4 57.6 %copy-start.19 = (bf16[20,20]{1,0:T(8,128)(2,1)S(1)}, bf16[20,20]{1,0:T(8,128)(2,1)}, u32[]{:S(2)}) copy-start(bf16[20,20]{1,0:T(8,128)(2,1)} %param.8) | copy-start | bytes 2404
  268.4 57.7 %copy-start.20 = (bf16[20]{0:T(256)(128)(2,1)S(1)}, bf16[20]{0:T(256)(128)(2,1)}, u32[]{:S(2)}) copy-start(bf16[20]{0:T(256)(128)(2,1)} %param.9) | copy-start | bytes 124
  268.4 57.8 %copy-start.18 = (bf16[128,2,512]{2,0,1:T(8,128)(2,1)S(1)}, bf16[128,2,512]{2,0,1:T(8,128)(2,1)}, u32[]{:S(2)}) copy-start(bf16[128,2,512]{2,0,1:T(8,128)(2,1)} %get-tuple-element.36) | copy-start | bytes 786436
  321.4 64.9 %all-to-all-start.1 = ((bf16[1,16,64,1280]{3,1,0,2:T(8,128)(2,1)}), bf16[1,16,64,1280]{3,1,0,2:T(8,128)(2,1)}, u32[]{:S(2)}, u32[]{:S(2)}) async-start(bf16[1,16,64,1280]{3,1,0,2:T(8,128)(2,1)} %copy.145), calls=%async_computation.1 | async-start | bytes 5242880 | tf_op jit(solution)/shard_map/all_to_all | solution.py:137
  419.3 4.1 copy-start
  428.6 121.1 %all-to-all-start.3 = ((bf16[1,128,2,8,1280]{4,3,2,0,1:T(8,128)(2,1)}), bf16[1,128,2,8,1280]{4,3,2,0,1:T(8,128)(2,1)}, u32[]{:S(2)}, u32[]{:S(2)}) async-start(bf16[1,128,2,8,1280]{4,3,2,0,1:T(8,128)(2,1)} %bitcast.455), calls=%async_computation.3 | async-start | bytes 10485760 | tf_op jit(solution)/shard_map/all_to_all | solution.py:128
  433.3 417.2 %reduce-scatter.2.cloned.1.call-start = ((), (), s32[]{:S(2)}) async-start(), calls=%async_computation.7 | async-start | bytes 22118400 | tf_op jit(solution)/shard_map/reduce_scatter | solution.py:211
  549.7 3.2 copy-start.5
  553.0 3.1 copy-start.13
  587.3 1.3 copy-start.14
  587.3 1.4 copy-start.15
  666.4 1.0 copy-start.9
  667.3 1.5 copy-start.8
  670.4 7.4 copy-start.10
  673.4 64.7 %all-to-all-start.5 = ((bf16[1,16,64,1280]{3,1,0,2:T(8,128)(2,1)}), bf16[1,16,64,1280]{3,1,0,2:T(8,128)(2,1)}, u32[]{:S(2)}, u32[]{:S(2)}) async-start(bf16[1,16,64,1280]{3,1,0,2:T(8,128)(2,1)} %copy.168), calls=%async_computation.5 | async-start | bytes 5242880 | tf_op jit(solution)/shard_map/all_to_all | solution.py:138
  677.8 1.5 copy-start.6
  738.1 64.9 %all-to-all-start.4 = ((bf16[1,16,64,1280]{3,1,0,2:T(8,128)(2,1)}), bf16[1,16,64,1280]{3,1,0,2:T(8,128)(2,1)}, u32[]{:S(2)}, u32[]{:S(2)}) async-start(bf16[1,16,64,1280]{3,1,0,2:T(8,128)(2,1)} %copy.164), calls=%async_computation.4 | async-start | bytes 5242880 | tf_op jit(solution)/shard_map/all_to_all | solution.py:137
  805.5 1.0 copy-start.17
Sparse Core Ops, SparseCore 0:
  603.3 160.1 reduce-scatter.1
where the time goes:
time: 878 us; the launch traced here: 867 us
  waiting for transfers between devices  312 us (36%)
  local copies, waits for them, and re-layouts  255 us (29%)
  matrix products  165 us (19%)
  other arithmetic  91.1 us (10%)
  starting transfers between devices  29.3 us (3%)
  between operations  15 us (2%)
    all_to_all x2, waiting for transfers between devices, analyse(): lax.all_to_all(split, 'space', split_axis=1, concat_axis=3, tiled=True)  173 us
    all_to_all x2, waiting for transfers between devices, synthesise(): lax.all_to_all(imag_y, 'space', split_axis=2, concat_axis=1, tiled=True)  107 us
    unnamed x48, local copies, waits for them, and re-layouts  46.9 us
    dot_general x2, matrix products, to_grid(): jnp.einsum('mz,smxr->szxr', table[:, 1, :], imag_in, preferred_element_ty...  39.7 us
    all_to_all x2, waiting for transfers between devices, synthesise(): lax.all_to_all(real_y, 'space', split_axis=2, concat_axis=1, tiled=True)  30.9 us
    slice x1, local copies, waits for them, and re-layouts, local(): w_imag = spec_weight[1]  29.8 us
    dot_general x1, other arithmetic, local(): jnp.einsum('sok,iok->sik', h_hat[:, 0], w_real, preferred_element_type=jn...  23 us
    dot_general x1, matrix products, local(): jnp.einsum('szxr,rR->szxR', signal, point_block, preferred_element_type=j...  21.6 us
  transfers between devices with their start and end apart: 7, of which 6 were waited for; matrix products, arithmetic and copies ran while one was open for 32% of the time, Pallas kernels for 0%

commit v1 on v0

v1 whole, which is shorter than its diff:
```python
import math

import jax
import jax.numpy as jnp
import ml_dtypes
import numpy as np
from jax import lax
from jax.sharding import PartitionSpec as P

NX = 64
NY = 64
NZ = 32
NT = 16
C = 20
MX = 24
MY = 24
MZ = 16
MT = 8
MZT = 128
BF = ml_dtypes.bfloat16


def retained(mode_count, length):
    positions = np.arange(mode_count)
    return np.where(positions < mode_count // 2, positions, length - mode_count + positions)


def complex_table(mode_count, length):
    freqs = retained(mode_count, length)
    turns = freqs[:, None] * np.arange(length)[None, :] % length
    angles = turns * (2.0 * math.pi / length)
    norm_scale = 1.0 / math.sqrt(length)
    cos_part = np.cos(angles) * norm_scale
    sin_part = np.sin(angles) * norm_scale
    upper_rows = np.stack([cos_part, sin_part], axis=1)
    lower_rows = np.stack([-sin_part, cos_part], axis=1)
    return np.stack([upper_rows, lower_rows], axis=0)


def depth_tables():
    depth_freq = retained(MZ, NZ)
    time_freq = np.arange(MT)
    depth_turns = depth_freq[:, None] * np.arange(NZ)[None, :] % NZ
    time_turns = time_freq[:, None] * np.arange(NT)[None, :] % NT
    turns = depth_turns[:, None, :, None] * NT + time_turns[None, :, None, :] * NZ
    angles = turns * (2.0 * math.pi / (NZ * NT))
    norm_scale = 1.0 / math.sqrt(NZ * NT)
    forward = np.stack([np.cos(angles), -np.sin(angles)], axis=2) * norm_scale
    doubling = np.where(time_freq == 0, 1.0, 2.0)
    inverse = forward * doubling[None, :, None, None, None]
    return forward.reshape(MZT, 2, NZ * NT).astype(BF), inverse.reshape(MZT, 2, NZ * NT).astype(BF)


def gelu_slope(pre_act):
    cumulative = 0.5 * (1.0 + lax.erf(pre_act * (1.0 / math.sqrt(2.0))))
    density = jnp.exp(-0.5 * pre_act * pre_act) * (1.0 / math.sqrt(2.0 * math.pi))
    return cumulative + pre_act * density


def block_table(table_y):
    blocks = np.einsum("cd,PjpY->pcYPdj", np.eye(C), table_y)
    return blocks.reshape(2, C * NY, 2 * C * MY).astype(BF)


def dot32(form, left, right):
    return jnp.einsum(form, left, right, preferred_element_type=jnp.float32)


def local(signal, cotangent, spec_weight, point_weight, bias):
    samples, depth_len, x_rows, merged = signal.shape
    depth_np, inverse_np = depth_tables()
    table_y = complex_table(MY, NY)
    table_x = jnp.asarray(complex_table(MX, NX).astype(BF))
    blocks = jnp.asarray(block_table(table_y))
    depth_table = jnp.asarray(depth_np)
    depth_inverse = jnp.asarray(inverse_np)
    point_block = (
        jnp.einsum("co,yz->cyoz", point_weight.astype(jnp.float32), jnp.eye(NY, dtype=jnp.float32))
        .reshape(C * NY, C * NY)
        .astype(jnp.bfloat16)
    )
    bias_row = jnp.repeat(bias.astype(jnp.float32), NY)
    w_real = spec_weight[0]
    w_imag = spec_weight[1]

    def analyse(table, grid_values):
        real = dot32("mz,szxr->smxr", table[:, 0], grid_values).astype(jnp.bfloat16)
        imag = dot32("mz,szxr->smxr", table[:, 1], grid_values).astype(jnp.bfloat16)
        both = dot32("smxr,rK->smxK", real, blocks[0]) + dot32("smxr,rK->smxK", imag, blocks[1])
        both = both.astype(jnp.bfloat16)
        moved = lax.all_to_all(both, "space", split_axis=1, concat_axis=2, tiled=True)
        halves = moved.reshape(samples, moved.shape[1], NX, 2, C * MY)
        total = dot32("Pipx,smxpr->sPmir", table_x, halves).astype(jnp.bfloat16)
        total = total.reshape(samples, 2, -1, MX, C, MY)
        return jnp.transpose(total, (0, 1, 4, 2, 3, 5)).reshape(samples, 2, C, -1)

    def synthesise(table, spectrum):
        unmerged = spectrum.reshape(samples, 2, C, -1, MX, MY)
        moved = jnp.transpose(unmerged, (0, 1, 3, 4, 2, 5)).reshape(samples, 2, -1, MX, C * MY)
        cells = dot32("Pipx,sPmir->smxpr", table_x, moved).astype(jnp.bfloat16)
        cells = cells.reshape(samples, cells.shape[1], NX, 2 * C * MY)
        back = lax.all_to_all(cells, "space", split_axis=2, concat_axis=1, tiled=True)
        real = dot32("smxK,rK->smxr", back, blocks[0]).astype(jnp.bfloat16)
        imag = dot32("smxK,rK->smxr", back, blocks[1]).astype(jnp.bfloat16)
        return dot32("mz,smxr->szxr", table[:, 0], real) + dot32("mz,smxr->szxr", table[:, 1], imag)

    direct = dot32("szxr,rR->szxR", signal, point_block)
    u_hat = analyse(depth_table, signal)
    v_real = dot32("sik,iok->sok", u_hat[:, 0], w_real) - dot32("sik,iok->sok", u_hat[:, 1], w_imag)
    v_imag = dot32("sik,iok->sok", u_hat[:, 1], w_real) + dot32("sik,iok->sok", u_hat[:, 0], w_imag)
    v_hat = jnp.stack([v_real, v_imag], axis=1).astype(jnp.bfloat16)
    pre_act = synthesise(depth_inverse, v_hat) + direct + bias_row
    hidden = (cotangent.astype(jnp.float32) * gelu_slope(pre_act)).astype(jnp.bfloat16)
    h_hat = analyse(depth_inverse, hidden)
    d_real = dot32("sok,iok->sik", h_hat[:, 0], w_real) + dot32("sok,iok->sik", h_hat[:, 1], w_imag)
    d_imag = dot32("sok,iok->sik", h_hat[:, 1], w_real) - dot32("sok,iok->sik", h_hat[:, 0], w_imag)
    d_hat = jnp.stack([d_real, d_imag], axis=1).astype(jnp.bfloat16)
    pointwise = dot32("szxR,rR->szxr", hidden, point_block)
    grad_signal = (synthesise(depth_table, d_hat) + pointwise).astype(jnp.bfloat16)
    u_all = lax.all_to_all(u_hat, "dp", split_axis=3, concat_axis=0, tiled=True)
    h_all = lax.all_to_all(h_hat, "dp", split_axis=3, concat_axis=0, tiled=True)
    u_all = u_all.astype(jnp.float32)
    h_all = h_all.astype(jnp.float32)

    def outer(left, right):
        return jnp.sum(left[:, :, None, :] * right[:, None, :, :], axis=0)

    grad_real = outer(u_all[:, 0], h_all[:, 0]) + outer(u_all[:, 1], h_all[:, 1])
    grad_imag = outer(u_all[:, 0], h_all[:, 1]) - outer(u_all[:, 1], h_all[:, 0])
    return (grad_signal, jnp.stack([grad_real, grad_imag], axis=0))


def solution(mesh):
    return jax.shard_map(
        local,
        mesh=mesh,
        in_specs=(
            P("dp", None, "space", None),
            P("dp", None, "space", None),
            P(None, None, None, "space"),
            P(),
            P(),
        ),
        out_specs=(P("dp", None, "space", None), P(None, None, None, ("space", "dp"))),
        check_vma=False,
    )
```

time: 878 us -> 668 us (0.76)
  waiting for transfers between devices: 312 us -> 44.2 us
  local copies, waits for them, and re-layouts: 255 us -> 306 us
  between operations: 15 us -> 1.32 us
  matrix products: 165 us -> 175 us
  other arithmetic: 91.1 us -> 101 us
    all_to_all x6, waiting for transfers between devices: 312 us -> 44.2 us  [the longest x2 44.2 us: analyse(): lax.all_to_all(both, 'space', split_axis=1, concat_axis=2, tiled=True)]
    unnamed x48 -> x39, local copies, waits for them, and re-layouts: 46.9 us -> 96.5 us
    reduce_sum x0 -> x1, other arithmetic: none -> 40.5 us  [outer(): return jnp.sum(left[:, :, None, :] * right[:, None, :, :], axis=0)]
    convert_element_type x14 -> x6, local copies, waits for them, and re-layouts: 31.1 us -> 9.54 us  [the longest x2 7.02 us: analyse(): both = both.astype(jnp.bfloat16)]
    reshape x6 -> x10, local copies, waits for them, and re-layouts: 32.3 us -> 47.3 us  [the longest x4 27.9 us: analyse(): return jnp.transpose(total, (0, 1, 4, 2, 3, 5)).reshape(samples, 2, C, -1)]
    convert_element_type x3 -> x0, other arithmetic: 14 us -> none  [the longest x1 8.71 us: local(): partial_value.astype(jnp.bfloat16)]
    all_to_all x10 -> x6, local copies, waits for them, and re-layouts: 18.7 us -> 31.8 us  [the longest x1 10.2 us: local(): u_all = lax.all_to_all(u_hat, 'dp', split_axis=3, concat_axis=0, tiled=True)]
    transpose x4 -> x2, local copies, waits for them, and re-layouts: 23.2 us -> 10.4 us  [analyse(): return jnp.transpose(total, (0, 1, 4, 2, 3, 5)).reshape(samples, 2, C, -1)]
  transfers between devices with their start and end apart: 7 -> 6, of which waited for: 6 -> 2; matrix products, arithmetic and copies ran while one was open for 32% -> 50% of each run, Pallas kernels for 0% -> 0%
where the time goes in v1:
time: 668 us; the launch traced here: 657 us
  local copies, waits for them, and re-layouts  306 us (46%)
  matrix products  175 us (26%)
  other arithmetic  101 us (15%)
  waiting for transfers between devices  44.2 us (7%)
  starting transfers between devices  30 us (4%)
    dot_general x14, matrix products, dot32(): return jnp.einsum(form, left, right, preferred_element_type=jnp.float32)  175 us
    unnamed x39, local copies, waits for them, and re-layouts  96.5 us
    all_to_all x2, waiting for transfers between devices, analyse(): lax.all_to_all(both, 'space', split_axis=1, concat_axis=2, tiled=True)  44.2 us
    dot_general x2, other arithmetic, dot32(): return jnp.einsum(form, left, right, preferred_element_type=jnp.float32)  41.2 us
    reduce_sum x1, other arithmetic, outer(): return jnp.sum(left[:, :, None, :] * right[:, None, :, :], axis=0)  40.5 us
    another operation x8, local copies, waits for them, and re-layouts  38.5 us
    slice x1, local copies, waits for them, and re-layouts, local(): w_imag = spec_weight[1]  29.8 us
    reshape x4, local copies, waits for them, and re-layouts, analyse(): return jnp.transpose(total, (0, 1, 4, 2, 3, 5)).reshape(samples, 2, C, -1)  27.9 us
  transfers between devices with their start and end apart: 6, of which 2 were waited for; matrix products, arithmetic and copies ran while one was open for 50% of the time, Pallas kernels for 0%

profile of v1, /device:TPU:0, one launch (start us, length us, event | category | flops | bytes accessed | tf_op | source)
XLA Modules:
  0.0 657.0 jit_solution(13614879044189403960)
XLA Ops:
  0.7 13.3 %fusion.42 = f32[128,8,960]{0,2,1:T(8,128)} fusion(bf16[1280,960,1]{0,1,2:T(8,128)(2,1)} %constant.47, bf16[128,512,1]{1,0,2:T(8,128)(2,1)} %constant.46, bf16[512,8,1280]{2,1,0:T(8,128)(2,1)} %bitcast.305), kind=kOutput, calls=%fused_computation.68 | convolution fusion | flops 3860070400 | bytes 17006592 | tf_op jit(solution)/shard_map/smxr,rK->smxK/dot_general | solution.py:66
  14.0 12.9 %fusion.39 = bf16[1,128,8,960]{1,3,2,0:T(8,128)(2,1)} fusion(f32[128,8,960]{0,2,1:T(8,128)} %fusion.42, bf16[1280,960,1]{0,1,2:T(8,128)(2,1)S(1)} %copy-done.2, bf16[128,512,1]{1,0,2:T(8,128)(2,1)S(1)} %copy-done.5, bf16[512,8,1280]{2,1,0:T(8,128)(2,1)} %bitcast.306), kind=kOutput, calls=%fused_computation.66 | convolution fusion | flops 3862036480 | bytes 18972672 | tf_op jit(solution)/shard_map/smxr,rK->smxK/dot_general | solution.py:66
  26.9 4.1 copy.257
  31.0 6.6 %all-to-all-start = ((bf16[1,128,8,960]{3,2,0,1:T(8,128)(2,1)}), bf16[1,128,8,960]{3,2,0,1:T(8,128)(2,1)S(1)}, u32[]{:S(2)}, u32[]{:S(2)}) async-start(bf16[1,128,8,960]{3,2,0,1:T(8,128)(2,1)} %copy.257), calls=%async_computation | async-start | bytes 4194304 | tf_op jit(solution)/shard_map/all_to_all | solution.py:91
  37.6 29.8 %fusion.66 = (bf16[1,20,20,9216]{3,0,2,1:T(2,128)(2,1)}, bf16[1,20,20,9216]{3,0,2,1:T(2,128)(2,1)}) fusion(bf16[2,20,20,9216]{3,0,2,1:T(2,128)(2,1)} %param.11), kind=kLoop, calls=%fused_computation.96 | loop fusion | bytes 29491200 | tf_op jit(solution)/shard_map/slice | solution.py:84
  67.4 19.2 %all-to-all-done = bf16[1,128,8,960]{3,2,0,1:T(8,128)(2,1)S(1)} async-done(((bf16[1,128,8,960]{3,2,0,1:T(8,128)(2,1)}), bf16[1,128,8,960]{3,2,0,1:T(8,128)(2,1)S(1)}, u32[]{:S(2)}, u32[]{:S(2)}) %all-to-all-start) | async-done | bytes 1966112 | tf_op jit(solution)/shard_map/all_to_all | solution.py:91
  88.2 3.6 reshape.295
  92.3 4.5 reshape.296
  96.8 5.2 copy.261
  102.0 6.2 reshape.297
  110.1 7.8 %copy.295 = bf16[1,2,20,9216]{2,1,0,3:T(2,128)(2,1)} copy(bf16[1,2,20,9216]{3,1,2,0:T(2,128)(2,1)S(1)} %reshape.297) | data formatting | bytes 1474560 | tf_op jit(solution)/shard_map/reshape | solution.py:95
  117.9 11.3 %reshape.360 = bf16[4,2,46080]{2,1,0:T(2,128)(2,1)} reshape(bf16[9216,1,2,20]{3,2,1,0:T(2,128)(2,1)} %bitcast.294) | data formatting | bytes 1474560
  129.1 4.1 all-to-all-start.4
  133.5 19.1 %fusion.8 = (f32[9216,20]{0,1:T(8,128)S(1)}, f32[9216,20]{0,1:T(8,128)S(1)}, f32[9216,20]{0,1:T(8,128)S(1)}, f32[9216,20]{0,1:T(8,128)S(1)}) fusion(f32[9216,20]{0,1:T(8,128)S(1)} %get-tuple-element.43, bf16[1,20,20,9216]{3,0,2,1:T(2,128)(2,1)} %get-tuple-element.33, f32[9216,20]{0,1:T(8,128)S(1)} %get-tuple-element.42, ...), kind=kLoop, calls=%fused_computation.19 | loop fusion | flops 36126720 | bytes 19169280 | tf_op jit(solution)/shard_map/sik,iok->sok/dot_general | solution.py:66
  153.6 3.2 stack.24
  156.8 5.1 stack.23
  161.9 2.4 maximum_bitcast_fusion
  164.3 6.4 copy.368
  170.7 5.6 reshape.333
  179.2 3.0 reshape.355
  182.2 4.8 all-to-all-start.1
  187.0 5.0 fusion.23
  192.0 10.0 %reshape.352 = bf16[1280,1280,1]{1,0,2:T(8,128)(2,1)} reshape(bf16[20,64,20,64]{3,2,1,0:T(8,128)(2,1)} %fusion.23) | data formatting | bytes 6553600 | tf_op jit(solution)/shard_map/convert_element_type | solution.py:80
  202.0 8.6 %convert_element_type.187 = bf16[1280,1280]{1,0:T(8,128)(2,1)S(1)} reshape(bf16[20,64,20,64]{3,2,1,0:T(8,128)(2,1)} %fusion.23) | data formatting | bytes 6553600 | tf_op jit(solution)/shard_map/convert_element_type | solution.py:80
  210.6 16.4 %copy.254 = bf16[1,512,8,1280]{1,3,2,0:T(8,128)(2,1)} copy(bf16[1,512,8,1280]{3,2,1,0:T(8,128)(2,1)} %param.10) | data formatting | bytes 20971520 | tf_op args[1]
  227.2 20.6 %fusion.17 = f32[1280,512,8]{1,0,2:T(8,128)} fusion(bf16[512,8,1280]{2,1,0:T(8,128)(2,1)} %bitcast.307, bf16[1280,1280]{1,0:T(8,128)(2,1)S(1)} %convert_element_type.187), kind=kOutput, calls=%fused_computation.34 | convolution fusion | flops 13421772800 | bytes 34734080 | tf_op jit(solution)/shard_map/szxr,rR->szxR/dot_general | solution.py:66
  247.8 14.2 %reshape.361 = bf16[9216,1,2,20]{3,2,1,0:T(2,128)(2,1)} reshape(bf16[4,2,46080]{2,1,0:T(2,128)(2,1)} %copy-done.3) | data formatting | bytes 1474560
  261.9 10.2 %copy.296 = bf16[1,2,20,9216]{3,1,2,0:T(2,128)(2,1)S(1)} copy(bf16[1,2,20,9216]{2,1,0,3:T(2,128)(2,1)} %bitcast.295) | data formatting | bytes 1474560 | tf_op jit(solution)/shard_map/all_to_all | solution.py:120
  273.9 4.3 copy.269
  278.2 4.1 copy.270
  282.3 11.6 %fusion.33 = f32[8,1280,512]{2,1,0:T(8,128)} fusion(bf16[128,512,1]{1,0,2:T(8,128)(2,1)S(1)} %copy-done.8, bf16[128,8,960]{0,2,1:T(8,128)(2,1)} %copy.270, bf16[1280,960,1]{0,1,2:T(8,128)(2,1)S(1)} %copy-done.1), kind=kOutput, calls=%fused_computation.60 | convolution fusion | flops 3860070400 | bytes 25526272 | tf_op jit(solution)/shard_map/mz,smxr->szxr/dot_general | solution.py:66
  293.9 28.3 %fusion.16 = bf16[512,8,1280]{0,2,1:T(8,128)(2,1)} fusion(f32[1280,512,8]{1,0,2:T(8,128)} %fusion.17, f32[8,1280,512]{2,1,0:T(8,128)} %fusion.33, bf16[128,512,1]{1,0,2:T(8,128)(2,1)S(1)} %copy-done.15, bf16[1,512,8,1280]{1,3,2,0:T(8,128)(2,1)} %copy.254, f32[1280]{0:T(1024)S(1)} %add.90, bf16[128,8,960]{0,2,1:T(8,128)(2,1)} %copy.270, ...), kind=kOutput, calls=%fused_computation.32 | convolution fusion | flops 3933470720 | bytes 67474432 | tf_op jit(solution)/shard_map/mz,smxr->szxr/dot_general | solution.py:66
  322.2 12.8 %fusion.58 = f32[128,8,960]{0,2,1:T(8,128)} fusion(bf16[1280,960,1]{0,1,2:T(8,128)(2,1)S(1)} %copy-done.1, bf16[512,8,1280]{0,2,1:T(8,128)(2,1)} %fusion.16, bf16[128,512,1]{1,0,2:T(8,128)(2,1)S(1)} %copy-done.8), kind=kOutput, calls=%fused_computation.79 | convolution fusion | flops 3860070400 | bytes 17006592 | tf_op jit(solution)/shard_map/smxr,rK->smxK/dot_general | solution.py:66
  335.0 12.9 %fusion.40 = bf16[1,128,8,960]{1,3,2,0:T(8,128)(2,1)S(1)} fusion(f32[128,8,960]{0,2,1:T(8,128)} %fusion.58, bf16[1280,960,1]{0,1,2:T(8,128)(2,1)} %constant.49, bf16[512,8,1280]{0,2,1:T(8,128)(2,1)} %fusion.16, bf16[128,512,1]{1,0,2:T(8,128)(2,1)S(1)} %copy-done.15), kind=kOutput, calls=%fused_computation.67 | convolution fusion | flops 3862036480 | bytes 18972672 | tf_op jit(solution)/shard_map/smxr,rK->smxK/dot_general | solution.py:66
  347.9 2.9 copy.278
  350.8 5.5 all-to-all-start.2
  356.3 2.6 slice_bitcast_fusion.3
  358.9 21.4 %fusion.69 = f32[512,8,1280]{0,2,1:T(8,128)} fusion(bf16[1280,1280,1]{1,0,2:T(8,128)(2,1)} %reshape.352, bf16[512,8,1280]{0,2,1:T(8,128)(2,1)} %fusion.16), kind=kOutput, calls=%fused_computation.99 | convolution fusion | flops 13421772800 | bytes 34734080 | tf_op jit(solution)/shard_map/szxR,rR->szxr/dot_general | solution.py:66
  380.3 25.0 %all-to-all-done.2 = bf16[1,128,8,960]{3,2,0,1:T(8,128)(2,1)S(1)} async-done(((bf16[1,128,8,960]{3,2,0,1:T(8,128)(2,1)}), bf16[1,128,8,960]{3,2,0,1:T(8,128)(2,1)S(1)}, u32[]{:S(2)}, u32[]{:S(2)}) %all-to-all-start.2) | async-done | bytes 1966112 | tf_op jit(solution)/shard_map/all_to_all | solution.py:91
  406.9 3.6 reshape.306
  411.1 4.5 reshape.307
  415.6 5.2 copy.282
  420.8 6.2 reshape.308
  428.0 7.8 %copy.297 = bf16[1,2,20,9216]{2,1,0,3:T(2,128)(2,1)} copy(bf16[1,2,20,9216]{3,1,2,0:T(2,128)(2,1)S(1)} %reshape.308) | data formatting | bytes 1474560 | tf_op jit(solution)/shard_map/reshape | solution.py:95
  436.1 11.2 %reshape.362 = bf16[4,2,46080]{2,1,0:T(2,128)(2,1)} reshape(bf16[9216,1,2,20]{3,2,1,0:T(2,128)(2,1)} %bitcast.293) | data formatting | bytes 1474560
  447.3 4.4 all-to-all-start.5
  451.7 22.1 %fusion.12 = (f32[9216,20]{0,1:T(8,128)S(1)}, f32[9216,20]{0,1:T(8,128)S(1)}, f32[9216,20]{0,1:T(8,128)S(1)}, f32[9216,20]{0,1:T(8,128)S(1)}) fusion(f32[9216,20]{0,1:T(8,128)S(1)} %bitcast_convert_fusion.5, bf16[1,20,20,9216]{3,0,2,1:T(2,128)(2,1)} %get-tuple-element.33, f32[9216,20]{0,1:T(8,128)S(1)} %bitcast_convert_fusion.4, ...), kind=kLoop, calls=%fused_computation.23 | loop fusion | flops 36126720 | bytes 19169280 | tf_op jit(solution)/shard_map/sok,iok->sik/dot_general | solution.py:66
  474.6 3.2 stack.27
  477.8 5.1 stack.26
  485.4 6.4 copy.373
  491.8 5.6 reshape.349
  500.3 3.0 reshape.358
  503.3 4.7 all-to-all-start.3
  508.0 12.7 %reshape.363 = bf16[9216,1,2,20]{3,2,1,0:T(2,128)(2,1)} reshape(bf16[4,2,46080]{2,1,0:T(2,128)(2,1)S(1)} %all-to-all-done.5) | data formatting | bytes 1474560
  520.8 10.0 %copy.298 = bf16[1,2,20,9216]{3,1,2,0:T(2,128)(2,1)S(1)} copy(bf16[1,2,20,9216]{2,1,0,3:T(2,128)(2,1)} %bitcast.296) | data formatting | bytes 1474560 | tf_op jit(solution)/shard_map/all_to_all | solution.py:121
  532.6 40.5 %multiply_reduce_fusion.2 = (f32[20,20,2304]{2,1,0:T(8,128)S(1)}, f32[20,20,2304]{2,1,0:T(8,128)S(1)}, f32[20,20,2304]{2,1,0:T(8,128)S(1)}, f32[20,20,2304]{2,1,0:T(8,128)S(1)}) fusion(f32[4,20,2304]{2,0,1:T(4,128)} %get-tuple-element.37, f32[4,20,2304]{2,0,1:T(4,128)} %get-tuple-element.35, f32[4,20,2304]{2,0,1:T(4,128)} %get-tuple-element.36, ...), kind=kLoop, calls=%fused_computation.30 | loop fusion | flops 25804800 | bytes 17694720 | tf_op jit(solution)/shard_map/reduce_sum | solution.py:126
  573.1 2.6 subtract_bitcast_fusion
  577.9 4.1 pad_maximum_fusion
  582.1 12.3 %copy.300 = f32[2,20,20,2304]{3,0,2,1:T(2,128)} copy(f32[2,20,20,2304]{3,2,1,0:T(8,128)} %pad_maximum_fusion) | data formatting | bytes 14745600
  594.3 4.2 copy.288
  598.5 3.3 copy.289
  601.8 13.3 %fusion.34 = f32[8,1280,512]{2,1,0:T(8,128)} fusion(bf16[128,512,1]{1,0,2:T(8,128)(2,1)S(1)} %copy-done.7, bf16[128,8,960]{0,2,1:T(8,128)(2,1)S(1)} %copy.289, bf16[1280,960,1]{0,1,2:T(8,128)(2,1)} %constant.47), kind=kOutput, calls=%fused_computation.61 | convolution fusion | flops 3860070400 | bytes 25526272 | tf_op jit(solution)/shard_map/mz,smxr->szxr/dot_general | solution.py:66
  615.1 25.0 %fusion.6 = bf16[1,512,8,1280]{1,3,2,0:T(8,128)(2,1)} fusion(f32[512,8,1280]{0,2,1:T(8,128)} %fusion.69, f32[8,1280,512]{2,1,0:T(8,128)} %fusion.34, bf16[128,512,1]{1,0,2:T(8,128)(2,1)S(1)} %copy-done.6, bf16[128,8,960]{0,2,1:T(8,128)(2,1)S(1)} %copy.289, bf16[1280,960,1]{0,1,2:T(8,128)(2,1)} %constant.49), kind=kOutput, calls=%fused_computation.16 | convolution fusion | flops 3875799040 | bytes 56983552 | tf_op jit(solution)/shard_map/mz,smxr->szxr/dot_general | solution.py:66
  640.1 16.6 %copy.299 = bf16[1,512,8,1280]{3,2,1,0:T(8,128)(2,1)} copy(bf16[1,512,8,1280]{1,3,2,0:T(8,128)(2,1)} %fusion.6) | data formatting | bytes 20971520
  (64 shorter events, 23.9 us)
Async XLA Ops:
  0.6 13.3 %copy-start.2 = (bf16[1280,960,1]{0,1,2:T(8,128)(2,1)S(1)}, bf16[1280,960,1]{0,1,2:T(8,128)(2,1)}, u32[]{:S(2)}) copy-start(bf16[1280,960,1]{0,1,2:T(8,128)(2,1)} %constant.49) | copy-start | bytes 7372804
  0.6 13.3 %copy-start.5 = (bf16[128,512,1]{1,0,2:T(8,128)(2,1)S(1)}, bf16[128,512,1]{1,0,2:T(8,128)(2,1)}, u32[]{:S(2)}) copy-start(bf16[128,512,1]{1,0,2:T(8,128)(2,1)} %constant.48) | copy-start | bytes 393220
  31.0 55.6 %all-to-all-start = ((bf16[1,128,8,960]{3,2,0,1:T(8,128)(2,1)}), bf16[1,128,8,960]{3,2,0,1:T(8,128)(2,1)S(1)}, u32[]{:S(2)}, u32[]{:S(2)}) async-start(bf16[1,128,8,960]{3,2,0,1:T(8,128)(2,1)} %copy.257), calls=%async_computation | async-start | bytes 4194304 | tf_op jit(solution)/shard_map/all_to_all | solution.py:91
  37.6 29.8 %copy-start.13 = (bf16[20,20]{1,0:T(8,128)(2,1)S(1)}, bf16[20,20]{1,0:T(8,128)(2,1)}, u32[]{:S(2)}) copy-start(bf16[20,20]{1,0:T(8,128)(2,1)} %param.12) | copy-start | bytes 2404
  67.4 24.4 %copy-start.11 = (bf16[2,24,2,64,1]{3,1,2,0,4:T(8,128)(2,1)S(1)}, bf16[2,24,2,64,1]{3,1,2,0,4:T(8,128)(2,1)}, u32[]{:S(2)}) copy-start(bf16[2,24,2,64,1]{3,1,2,0,4:T(8,128)(2,1)} %constant.50) | copy-start | bytes 36868
  117.9 15.4 %copy-start.4 = (bf16[1,1,20,9216]{3,1,2,0:T(2,128)(2,1)S(1)}, bf16[1,1,20,9216]{3,1,2,0:T(2,128)(2,1)}, u32[]{:S(2)}) copy-start(bf16[1,1,20,9216]{3,1,2,0:T(2,128)(2,1)} %get-tuple-element.41) | copy-start | bytes 1105924
  129.1 53.1 %all-to-all-start.4 = ((bf16[4,2,46080]{2,1,0:T(2,128)(2,1)}), bf16[4,2,46080]{2,1,0:T(2,128)(2,1)S(1)}, u32[]{:S(2)}, u32[]{:S(2)}) async-start(bf16[4,2,46080]{2,1,0:T(2,128)(2,1)} %reshape.360), calls=%async_computation.4 | async-start | bytes 1474560 | tf_op jit(solution)/shard_map/all_to_all | solution.py:120
  170.7 5.6 copy-start.9
  182.2 9.8 %copy-start.3 = (bf16[4,2,46080]{2,1,0:T(2,128)(2,1)}, bf16[4,2,46080]{2,1,0:T(2,128)(2,1)S(1)}, u32[]{:S(2)}) copy-start(bf16[4,2,46080]{2,1,0:T(2,128)(2,1)S(1)} %all-to-all-done.4) | copy-start | bytes 2211844
  182.2 91.6 %all-to-all-start.1 = ((bf16[1,16,64,960]{3,1,0,2:T(8,128)(2,1)}), bf16[1,16,64,960]{3,1,0,2:T(8,128)(2,1)}, u32[]{:S(2)}, u32[]{:S(2)}) async-start(bf16[1,16,64,960]{3,1,0,2:T(8,128)(2,1)} %reshape.355), calls=%async_computation.1 | async-start | bytes 4194304 | tf_op jit(solution)/shard_map/all_to_all | solution.py:102
  210.6 16.4 %copy-start.14 = (bf16[20]{0:T(256)(128)(2,1)S(1)}, bf16[20]{0:T(256)(128)(2,1)}, u32[]{:S(2)}) copy-start(bf16[20]{0:T(256)(128)(2,1)} %param.13) | copy-start | bytes 124
  273.9 8.5 %copy-start.1 = (bf16[1280,960,1]{0,1,2:T(8,128)(2,1)S(1)}, bf16[1280,960,1]{0,1,2:T(8,128)(2,1)}, u32[]{:S(2)}) copy-start(bf16[1280,960,1]{0,1,2:T(8,128)(2,1)} %constant.47) | copy-start | bytes 7372804
  273.9 8.5 %copy-start.8 = (bf16[128,512,1]{1,0,2:T(8,128)(2,1)S(1)}, bf16[128,512,1]{1,0,2:T(8,128)(2,1)}, u32[]{:S(2)}) copy-start(bf16[128,512,1]{1,0,2:T(8,128)(2,1)} %constant.53) | copy-start | bytes 393220
  282.3 11.6 %copy-start.15 = (bf16[128,512,1]{1,0,2:T(8,128)(2,1)S(1)}, bf16[128,512,1]{1,0,2:T(8,128)(2,1)}, u32[]{:S(2)}) copy-start(bf16[128,512,1]{1,0,2:T(8,128)(2,1)} %constant.54) | copy-start | bytes 393220
  350.8 54.5 %all-to-all-start.2 = ((bf16[1,128,8,960]{3,2,0,1:T(8,128)(2,1)}), bf16[1,128,8,960]{3,2,0,1:T(8,128)(2,1)S(1)}, u32[]{:S(2)}, u32[]{:S(2)}) async-start(bf16[1,128,8,960]{3,2,0,1:T(8,128)(2,1)} %copy.278), calls=%async_computation.2 | async-start | bytes 4194304 | tf_op jit(solution)/shard_map/all_to_all | solution.py:91
  380.3 30.2 %copy-start.12 = (bf16[2,24,2,64,1]{3,1,2,0,4:T(8,128)(2,1)S(1)}, bf16[2,24,2,64,1]{3,1,2,0,4:T(8,128)(2,1)}, u32[]{:S(2)}) copy-start(bf16[2,24,2,64,1]{3,1,2,0,4:T(8,128)(2,1)} %constant.50) | copy-start | bytes 36868
  447.3 56.0 %all-to-all-start.5 = ((bf16[4,2,46080]{2,1,0:T(2,128)(2,1)}), bf16[4,2,46080]{2,1,0:T(2,128)(2,1)S(1)}, u32[]{:S(2)}, u32[]{:S(2)}) async-start(bf16[4,2,46080]{2,1,0:T(2,128)(2,1)} %reshape.362), calls=%async_computation.5 | async-start | bytes 1474560 | tf_op jit(solution)/shard_map/all_to_all | solution.py:121
  491.8 5.6 copy-start.10
  503.3 91.0 %all-to-all-start.3 = ((bf16[1,16,64,960]{3,1,0,2:T(8,128)(2,1)}), bf16[1,16,64,960]{3,1,0,2:T(8,128)(2,1)}, u32[]{:S(2)}, u32[]{:S(2)}) async-start(bf16[1,16,64,960]{3,1,0,2:T(8,128)(2,1)} %reshape.358), calls=%async_computation.3 | async-start | bytes 4194304 | tf_op jit(solution)/shard_map/all_to_all | solution.py:102
  575.7 2.3 copy-start
  594.3 7.5 %copy-start.7 = (bf16[128,512,1]{1,0,2:T(8,128)(2,1)S(1)}, bf16[128,512,1]{1,0,2:T(8,128)(2,1)}, u32[]{:S(2)}) copy-start(bf16[128,512,1]{1,0,2:T(8,128)(2,1)} %constant.46) | copy-start | bytes 393220
  601.8 13.3 %copy-start.6 = (bf16[128,512,1]{1,0,2:T(8,128)(2,1)S(1)}, bf16[128,512,1]{1,0,2:T(8,128)(2,1)}, u32[]{:S(2)}) copy-start(bf16[128,512,1]{1,0,2:T(8,128)(2,1)} %constant.48) | copy-start | bytes 393220

commit v2 on v1

v2 whole, which is shorter than its diff:
```python
import functools
import math

import jax
import jax.numpy as jnp
import ml_dtypes
import numpy as np
from jax import lax
from jax.experimental import pallas as pl
from jax.experimental.pallas import tpu as pltpu
from jax.sharding import PartitionSpec as P

NX = 64
NY = 64
NZ = 32
NT = 16
ZT = NZ * NT
C = 20
MX = 24
MY = 24
MZ = 16
MT = 8
MZT = 128
CY = C * NY
LANES = 512
KM = MX * MY
KB = 2 * KM
BF = ml_dtypes.bfloat16
BF16 = jnp.bfloat16
F32 = jnp.float32
VMEM_LIMIT = 56 * 1024 * 1024
PAIRS = ((0, 0), (0, 1), (1, 1), (1, 2), (2, 2), (2, 3), (3, 4))


def retained(mode_count, length):
    positions = np.arange(mode_count)
    return np.where(positions < mode_count // 2, positions, length - mode_count + positions)


def complex_table(mode_count, length):
    freqs = retained(mode_count, length)
    turns = freqs[:, None] * np.arange(length)[None, :] % length
    angles = turns * (2.0 * math.pi / length)
    norm_scale = 1.0 / math.sqrt(length)
    cos_part = np.cos(angles) * norm_scale
    sin_part = np.sin(angles) * norm_scale
    upper_rows = np.stack([cos_part, sin_part], axis=1)
    lower_rows = np.stack([-sin_part, cos_part], axis=1)
    return np.stack([upper_rows, lower_rows], axis=0)


def depth_tables():
    depth_freq = retained(MZ, NZ)
    time_freq = np.arange(MT)
    depth_turns = depth_freq[:, None] * np.arange(NZ)[None, :] % NZ
    time_turns = time_freq[:, None] * np.arange(NT)[None, :] % NT
    turns = depth_turns[:, None, :, None] * NT + time_turns[None, :, None, :] * NZ
    angles = turns * (2.0 * math.pi / ZT)
    norm_scale = 1.0 / math.sqrt(ZT)
    forward = np.stack([np.cos(angles), -np.sin(angles)], axis=2) * norm_scale
    doubling = np.where(time_freq == 0, 1.0, 2.0)
    inverse = forward * doubling[None, :, None, None, None]

    def square(table):
        real, imag = table.reshape(MZT, 2, ZT).transpose(1, 0, 2)
        return np.block([[real, -imag], [imag, real]]).astype(BF)

    return square(forward), square(inverse)


def y_tiles():
    table = complex_table(MY, NY)
    full = np.zeros((2, CY, LANES))
    for ch in range(C):
        full[:, ch * NY : (ch + 1) * NY, ch * MY : (ch + 1) * MY] = table[:, :, 0, :].transpose(0, 2, 1)
    tiles = []
    for tile, group in PAIRS:
        rows = full[:, 256 * group : 256 * group + 256, 128 * tile : 128 * tile + 128]
        tiles.append(np.concatenate([rows[0], rows[1]], axis=1))
    tiles = np.stack(tiles)
    return tiles.astype(BF), tiles.transpose(0, 2, 1).astype(BF)


def x_table(x_rows):
    table = complex_table(MX, NX)
    split = table.reshape(2, MX, 2, NX // x_rows, x_rows).transpose(3, 2, 4, 0, 1)
    out = np.zeros((NX // x_rows, 2, x_rows, 2, 4, 32))
    out[..., :MX] = split[:, :, :, :, None, :]
    return out.reshape(2 * NX, 256).astype(BF)


def lane_perms():
    perm = np.zeros((2, 768, 640))
    for i in range(MX):
        for j in range(MY):
            perm[:, 128 * (j // 4) + 32 * (j % 4) + i, i * MY + j] = 1.0
    perm[1] = np.roll(perm[1], 64, axis=1)
    return perm.astype(BF), perm.transpose(0, 2, 1).astype(BF)


def dot32(left, right):
    return jnp.dot(left, right, preferred_element_type=F32)


def forward_y(rows, yf_ref, y_scr):
    for tile in range(4):
        total = None
        for k, (pair_tile, group) in enumerate(PAIRS):
            if pair_tile == tile:
                part = dot32(rows[:, 256 * group : 256 * group + 256], yf_ref[k])
                total = part if total is None else total + part
        y_scr[2 * tile] = total[:, :128]
        y_scr[2 * tile + 1] = total[:, 128:]


def spread_x(y_scr, yt_scr, step, x_rows, depth_rows):
    start = pl.multiple_of(step * depth_rows, depth_rows)
    for x in range(x_rows):
        for tile in range(4):
            for part in range(2):
                piece = y_scr[2 * tile + part, pl.ds(x, depth_rows, stride=x_rows), :].astype(BF16)
                yt_scr[x, pl.ds(part * ZT + start, depth_rows), 128 * tile : 128 * tile + 128] = piece


def forward_depth(zf_ref, yt_scr, out_ref, x_rows):
    owners = out_ref.shape[0]
    modes_here = MZT // owners
    for x in range(x_rows):
        coeffs = dot32(zf_ref[...], yt_scr[x]).astype(BF16)
        for owner in range(owners):
            for part in range(2):
                row = part * MZT + owner * modes_here
                out_ref[owner, part, x] = coeffs[row : row + modes_here]


def inverse_depth(q_ref, zi_ref, z_scr, x_rows):
    owners = q_ref.shape[0]
    for x in range(x_rows):
        rows = jnp.concatenate([q_ref[owner, part, x] for part in range(2) for owner in range(owners)], axis=0)
        grid_rows = dot32(zi_ref[...], rows)
        for part in range(2):
            for tile in range(4):
                z_scr[2 * tile + part, pl.ds(x, ZT, stride=x_rows), :] = grid_rows[
                    part * ZT : (part + 1) * ZT, 128 * tile : 128 * tile + 128
                ]


def inverse_y(z_scr, yi_ref, start, count, group):
    total = None
    for k, (tile, pair_group) in enumerate(PAIRS):
        if pair_group == group:
            rows = jnp.concatenate([z_scr[2 * tile + p, pl.ds(start, count), :] for p in range(2)], axis=1)
            part = dot32(rows.astype(BF16), yi_ref[k])
            total = part if total is None else total + part
    return total


def gelu_slope(pre_act):
    size = jnp.abs(pre_act) * math.sqrt(0.5)
    gauss = jnp.exp(-(size * size))
    t = 1.0 / (1.0 + 0.3275911 * size)
    poly = t * (
        0.254829592 + t * (-0.284496736 + t * (1.421413741 + t * (-1.453152027 + t * 1.061405429)))
    )
    tail = 0.5 * poly * gauss
    cumulative = jnp.where(pre_act >= 0.0, 1.0 - tail, tail)
    return cumulative + pre_act * (gauss * (1.0 / math.sqrt(2.0 * math.pi)))


def analyse_kernel(s_ref, yf_ref, zf_ref, out_ref, y_scr, yt_scr, *, x_rows, depth_rows):
    step = pl.program_id(0)
    forward_y(s_ref[...], yf_ref, y_scr)
    spread_x(y_scr, yt_scr, step, x_rows, depth_rows)

    @pl.when(step == pl.num_programs(0) - 1)
    def _():
        forward_depth(zf_ref, yt_scr, out_ref, x_rows)


def middle_kernel(
    q_ref, d_ref, cot_ref, bias_ref, zi_ref, yi_ref, yf_ref, zf_ref, h_ref, out_ref,
    z_scr, pre_scr, y_scr, yt_scr, *, x_rows, depth_rows,
):
    step = pl.program_id(0)
    block = x_rows * depth_rows

    @pl.when(step == 0)
    def _():
        inverse_depth(q_ref, zi_ref, z_scr, x_rows)

    start = pl.multiple_of(step * block, block)
    for group in range(5):
        pre_scr[:, 256 * group : 256 * group + 256] = inverse_y(z_scr, yi_ref, start, block, group)

    def rows_body(index, carry):
        row = pl.multiple_of(index * 16, 16)
        for group in range(5):
            lanes = slice(256 * group, 256 * group + 256)
            pre_act = pre_scr[pl.ds(row, 16), lanes] + d_ref[pl.ds(row, 16), lanes].astype(F32) + bias_ref[:, lanes]
            hidden = cot_ref[pl.ds(row, 16), lanes].astype(F32) * gelu_slope(pre_act)
            h_ref[pl.ds(row, 16), lanes] = hidden.astype(BF16)
        return carry

    lax.fori_loop(0, block // 16, rows_body, 0)
    forward_y(h_ref[...], yf_ref, y_scr)
    spread_x(y_scr, yt_scr, step, x_rows, depth_rows)

    @pl.when(step == pl.num_programs(0) - 1)
    def _():
        forward_depth(zf_ref, yt_scr, out_ref, x_rows)


def final_kernel(q_ref, p_ref, zi_ref, yi_ref, out_ref, z_scr, *, x_rows, depth_rows):
    step = pl.program_id(0)
    block = x_rows * depth_rows

    @pl.when(step == 0)
    def _():
        inverse_depth(q_ref, zi_ref, z_scr, x_rows)

    start = pl.multiple_of(step * block, block)
    for group in range(5):
        lanes = slice(256 * group, 256 * group + 256)
        total = inverse_y(z_scr, yi_ref, start, block, group) + p_ref[:, lanes].astype(F32)
        out_ref[:, lanes] = total.astype(BF16)


def point_kernel(s_ref, b_ref, out_ref):
    out_ref[...] = dot32(s_ref[...], b_ref[...]).astype(BF16)


def mode_kernel(
    r_ref, w_ref, gx_ref, perm_ref, permt_ref, u_ref, q_ref,
    in_scr, out_scr, o_scr, ut_scr, u_scr, v_scr, vt_scr, *, backward,
):
    step = pl.program_id(0)
    owners, _, x_rows, modes_here, _ = r_ref.shape
    cells = 2 * NX
    slot = lax.broadcasted_iota(jnp.int32, (C, 128), 1) // 32

    @pl.when(step == 0)
    def _():
        o_scr[...] = jnp.zeros_like(o_scr)
        for owner in range(owners):
            rows = 2 * x_rows * modes_here
            values = r_ref[owner].reshape(rows, LANES).astype(F32)
            for tile in range(4):
                in_scr[tile, owner * rows : (owner + 1) * rows, :] = values[:, 128 * tile : 128 * tile + 128]

    for half in range(2):
        mode = 2 * step + half
        tiles = [in_scr[tile, pl.ds(mode, cells, stride=modes_here), :] for tile in range(4)]
        block = jnp.concatenate(tiles, axis=1).astype(BF16)
        cols = lax.dot_general(block, gx_ref[...], (((0,), (0,)), ((), ())), preferred_element_type=F32)
        for part in range(2):
            vt_scr[part] = cols[:, 128 * part : 128 * part + 128]
        for part in range(2):
            for a in range(6):
                piece = vt_scr[part, pl.ds(4 * a, C, stride=MY), :]
                for r in range(1, 4):
                    piece = jnp.where(slot == r, vt_scr[part, pl.ds(4 * a + r, C, stride=MY), :], piece)
                ut_scr[24 * part : 24 * part + C, 128 * a : 128 * a + 128] = piece
        moved = dot32(ut_scr[...].astype(BF16), perm_ref[half])
        for part in range(2):
            rows = moved[24 * part : 24 * part + C]
            if half == 0:
                u_scr[part, :C, :640] = rows
            else:
                u_scr[part, :C, 512:640] = u_scr[part, :C, 512:640] + rows[:, :128]
                u_scr[part, :C, 640:] = rows[:, 128:]
    for part in range(2):
        u_ref[part] = u_scr[part, :C, :].astype(BF16)

    for chunk in range(3):
        lanes = slice(384 * chunk, 384 * chunk + 384)
        if backward:
            real = u_scr[0, :C, lanes]
            imag = u_scr[1, :C, lanes]
            for ch in range(C):
                w_real = w_ref[0, ch, :, lanes].astype(F32)
                w_imag = w_ref[1, ch, :, lanes].astype(F32)
                v_scr[0, ch : ch + 1, lanes] = jnp.sum(w_real * real + w_imag * imag, axis=0, keepdims=True)
                v_scr[1, ch : ch + 1, lanes] = jnp.sum(w_real * imag - w_imag * real, axis=0, keepdims=True)
        else:
            real = jnp.zeros((C, 384), F32)
            imag = jnp.zeros((C, 384), F32)
            for ch in range(C):
                w_real = w_ref[0, ch, :, lanes].astype(F32)
                w_imag = w_ref[1, ch, :, lanes].astype(F32)
                u_real = u_scr[0, ch : ch + 1, lanes]
                u_imag = u_scr[1, ch : ch + 1, lanes]
                real = real + w_real * u_real - w_imag * u_imag
                imag = imag + w_real * u_imag + w_imag * u_real
            v_scr[0, :C, lanes] = real
            v_scr[1, :C, lanes] = imag

    for half in range(2):
        mode = 2 * step + half
        for part in range(2):
            rows = v_scr[part, :, 512 * half : 512 * half + 640].astype(BF16)
            moved = dot32(rows, permt_ref[half])
            for a in range(6):
                for r in range(4):
                    piece = jnp.where(slot == r, moved[:C, 128 * a : 128 * a + 128], 0.0)
                    o_scr[part, pl.ds(4 * a + r, C, stride=MY), :] = piece
        cols = jnp.concatenate([o_scr[0], o_scr[1]], axis=1).astype(BF16)
        back = lax.dot_general(gx_ref[...], cols, (((1,), (1,)), ((), ())), preferred_element_type=F32)
        for tile in range(4):
            out_scr[tile, pl.ds(mode, cells, stride=modes_here), :] = back[:, 128 * tile : 128 * tile + 128]

    @pl.when(step == pl.num_programs(0) - 1)
    def _():
        for owner in range(owners):
            rows = 2 * x_rows * modes_here
            for tile in range(4):
                values = out_scr[tile, owner * rows : (owner + 1) * rows, :].astype(BF16)
                q_ref[owner, :, :, :, 128 * tile : 128 * tile + 128] = values.reshape(2, x_rows, modes_here, 128)


def weight_kernel(u_ref, g_ref, out_ref):
    groups = u_ref.shape[0]
    width = u_ref.shape[3]
    lane_step = 384 if width % 384 == 0 else width
    for first in range(0, width, lane_step):
        lanes = slice(first, first + lane_step)
        real = jnp.zeros((C, lane_step), F32)
        imag = jnp.zeros((C, lane_step), F32)
        for group in range(groups):
            u_real = u_ref[group, 0, pl.ds(pl.program_id(0), 1), lanes]
            u_imag = u_ref[group, 1, pl.ds(pl.program_id(0), 1), lanes]
            g_real = g_ref[group, 0, :, lanes].astype(F32)
            g_imag = g_ref[group, 1, :, lanes].astype(F32)
            real = real + u_real * g_real + u_imag * g_imag
            imag = imag + u_real * g_imag - u_imag * g_real
        out_ref[0, 0, :, lanes] = real
        out_ref[1, 0, :, lanes] = imag


def whole(array):
    zeros = (0,) * len(array.shape)
    return pl.BlockSpec(array.shape, lambda i: zeros)


def params():
    return pltpu.CompilerParams(dimension_semantics=("arbitrary",), vmem_limit_bytes=VMEM_LIMIT)


def shape_of(shape, kind):
    return jax.ShapeDtypeStruct(shape, kind)


def local(signal, cotangent, spec_weight, point_weight, bias):
    samples, depth_len, x_rows, merged = signal.shape
    owners = NX // x_rows
    modes_here = MZT // owners
    modes = modes_here * KM
    dp_size = lax.axis_size("dp")
    share = modes // dp_size
    rows_all = ZT * x_rows
    depth_rows = 64
    block = depth_rows * x_rows
    steps = ZT // depth_rows

    forward_np, inverse_np = depth_tables()
    yf_np, yi_np = y_tiles()
    perm_np, permt_np = lane_perms()
    zf_fwd, zf_inv = jnp.asarray(forward_np), jnp.asarray(inverse_np)
    zi_fwd, zi_inv = jnp.asarray(forward_np.T.copy()), jnp.asarray(inverse_np.T.copy())
    yf, yi = jnp.asarray(yf_np), jnp.asarray(yi_np)
    perm, permt = jnp.asarray(perm_np), jnp.asarray(permt_np)
    gx = jnp.asarray(x_table(x_rows))
    spread = jnp.asarray((np.arange(CY)[:, None] // NY == np.arange(C)[None, :]).astype(BF))
    same_y = jnp.asarray(np.arange(NY)[:, None] == np.arange(NY)[None, :])

    sig = signal.reshape(rows_all, CY)
    cot = cotangent.reshape(rows_all, CY)
    payload = shape_of((owners, 2, x_rows, modes_here, LANES), BF16)
    row_spec = pl.BlockSpec((block, CY), lambda i: (i, 0))
    y_scr = pltpu.VMEM((8, block, 128), F32)
    yt_scr = pltpu.VMEM((x_rows, 2 * ZT, LANES), BF16)
    z_scr = pltpu.VMEM((8, rows_all, 128), F32)
    sizes = dict(x_rows=x_rows, depth_rows=depth_rows)

    def point_block(weights):
        wide = dot32(dot32(spread, weights).astype(BF16), spread.T)
        row_y = lax.broadcasted_iota(jnp.int32, (CY, CY), 0) % NY
        col_y = lax.broadcasted_iota(jnp.int32, (CY, CY), 1) % NY
        return jnp.where(row_y == col_y, wide, 0.0).astype(BF16)

    def point(values, weights):
        matrix = point_block(weights)
        return pl.pallas_call(
            point_kernel,
            grid=(steps,),
            in_specs=[row_spec, whole(matrix)],
            out_specs=row_spec,
            out_shape=shape_of((rows_all, CY), BF16),
            compiler_params=params(),
            name="point",
        )(values, matrix)

    def modes_call(received, backward):
        ints = modes_here // 2
        out_shape = (shape_of((2, C, modes), BF16), payload)
        return pl.pallas_call(
            functools.partial(mode_kernel, backward=backward),
            grid=(ints,),
            in_specs=[
                whole(received),
                pl.BlockSpec((2, C, C, KB), lambda i: (0, 0, 0, i)),
                whole(gx),
                whole(perm),
                whole(permt),
            ],
            out_specs=(pl.BlockSpec((2, C, KB), lambda i: (0, 0, i)), whole(payload)),
            out_shape=out_shape,
            scratch_shapes=[
                pltpu.VMEM((4, 2 * NX * modes_here, 128), F32),
                pltpu.VMEM((4, 2 * NX * modes_here, 128), F32),
                pltpu.VMEM((2, LANES, 128), F32),
                pltpu.VMEM((48, 768), F32),
                pltpu.VMEM((2, 24, KB), F32),
                pltpu.VMEM((2, 24, KB), F32),
                pltpu.VMEM((2, LANES, 128), F32),
            ],
            compiler_params=params(),
            name="modes",
        )(received, spec_weight, gx, perm, permt)

    def exchange(values):
        return lax.all_to_all(values, "space", split_axis=0, concat_axis=0, tiled=True)

    def to_owners(spectrum):
        cut = jnp.transpose(spectrum.reshape(2, C, dp_size, share), (2, 0, 1, 3))
        return lax.all_to_all(cut, "dp", split_axis=0, concat_axis=0, tiled=True)

    coeffs = pl.pallas_call(
        functools.partial(analyse_kernel, **sizes),
        grid=(steps,),
        in_specs=[row_spec, whole(yf), whole(zf_fwd)],
        out_specs=whole(payload),
        out_shape=payload,
        scratch_shapes=[y_scr, yt_scr],
        compiler_params=params(),
        name="analyse",
    )(sig, yf, zf_fwd)
    u_hat, v_cells = modes_call(exchange(coeffs), False)
    direct = point(sig, point_weight)
    bias_row = jnp.repeat(bias.astype(F32), NY).reshape(1, CY)
    v_here = exchange(v_cells)
    hidden, e_coeffs = pl.pallas_call(
        functools.partial(middle_kernel, **sizes),
        grid=(steps,),
        in_specs=[
            whole(payload), row_spec, row_spec, whole(bias_row), whole(zi_inv), whole(yi), whole(yf), whole(zf_inv),
        ],
        out_specs=(row_spec, whole(payload)),
        out_shape=(shape_of((rows_all, CY), BF16), payload),
        scratch_shapes=[z_scr, pltpu.VMEM((block, CY), F32), y_scr, yt_scr],
        compiler_params=params(),
        name="middle",
    )(v_here, direct, cot, bias_row, zi_inv, yi, yf, zf_inv)
    pointwise = point(hidden, point_weight.T)
    g_hat, d_cells = modes_call(exchange(e_coeffs), True)
    d_here = exchange(d_cells)
    grad_signal = pl.pallas_call(
        functools.partial(final_kernel, **sizes),
        grid=(steps,),
        in_specs=[whole(payload), row_spec, whole(zi_fwd), whole(yi)],
        out_specs=row_spec,
        out_shape=shape_of((rows_all, CY), BF16),
        scratch_shapes=[z_scr],
        compiler_params=params(),
        name="final",
    )(d_here, pointwise, zi_fwd, yi)
    u_all = to_owners(u_hat).astype(F32)
    g_all = to_owners(g_hat)
    spec_grad = pl.pallas_call(
        weight_kernel,
        grid=(C,),
        in_specs=[whole(u_all), whole(g_all)],
        out_specs=pl.BlockSpec((2, 1, C, share), lambda i: (0, i, 0, 0)),
        out_shape=shape_of((2, C, C, share), F32),
        compiler_params=params(),
        name="weight",
    )(u_all, g_all)
    return (grad_signal.reshape(signal.shape), spec_grad)


def solution(mesh):
    return jax.shard_map(
        local,
        mesh=mesh,
        in_specs=(
            P("dp", None, "space", None),
            P("dp", None, "space", None),
            P(None, None, None, "space"),
            P(),
            P(),
        ),
        out_specs=(P("dp", None, "space", None), P(None, None, None, ("space", "dp"))),
        check_vma=False,
    )
```

time: 668 us -> 385 us (0.58); the launches traced: 657 us -> 384 us
  local copies, waits for them, and re-layouts: 306 us -> 36.4 us
  Pallas kernels: 0 us -> 195 us
  matrix products: 175 us -> 6.63 us
  other arithmetic: 101 us -> 1.35 us
  waiting for transfers between devices: 44.2 us -> 108 us
  blocking collectives: 0 us -> 14.3 us
  starting transfers between devices: 30 us -> 21 us
    pallas_call x0 -> x8, Pallas kernels: none -> 195 us  [the longest x2 59.2 us: modes_call(): pl.pallas_call(functools.partial(mode_kernel, backward=backward), grid=(i...]
    dot_general x14 -> x2, matrix products: 175 us -> 6.63 us  [dot32(): return jnp.dot(left, right, preferred_element_type=F32)]
    unnamed x39 -> x18, local copies, waits for them, and re-layouts: 96.5 us -> 29.5 us
    all_to_all x6 -> x5, waiting for transfers between devices: 44.2 us -> 108 us  [the longest x4 108 us: exchange(): lax.all_to_all(values, 'space', split_axis=0, concat_axis=0, tiled=True)]
    another operation x12 -> x1, local copies, waits for them, and re-layouts: 55 us -> 0.67 us  [local(): bias_row = jnp.repeat(bias.astype(F32), NY).reshape(1, CY)]
    reshape x10 -> x2, local copies, waits for them, and re-layouts: 47.3 us -> 3.12 us  [to_owners(): cut = jnp.transpose(spectrum.reshape(2, C, dp_size, share), (2, 0, 1, 3))]
    dot_general x2 -> x0, other arithmetic: 41.2 us -> none  [dot32(): return jnp.einsum(form, left, right, preferred_element_type=jnp.float32)]
    reduce_sum x1 -> x0, other arithmetic: 40.5 us -> none  [outer(): return jnp.sum(left[:, :, None, :] * right[:, None, :, :], axis=0)]
  transfers between devices with their start and end apart: 6 -> 5, of which waited for: 2 -> 3; matrix products, arithmetic and copies ran while one was open for 50% -> 11% of each run, Pallas kernels for 0% -> 21%
where the time goes in v2:
time: 385 us; the launch traced here: 384 us
  Pallas kernels  195 us (51%)
  waiting for transfers between devices  108 us (28%)
  local copies, waits for them, and re-layouts  36.4 us (9%)
  starting transfers between devices  21 us (5%)
  blocking collectives  14.3 us (4%)
  matrix products  6.63 us (2%)
    all_to_all x4, waiting for transfers between devices, exchange(): lax.all_to_all(values, 'space', split_axis=0, concat_axis=0, tiled=True)  108 us
    pallas_call x2, Pallas kernels, modes_call(): pl.pallas_call(functools.partial(mode_kernel, backward=backward), grid=(i...  59.2 us
    pallas_call x1, Pallas kernels, local(): pl.pallas_call(functools.partial(middle_kernel, **sizes), grid=(steps,),...  52.8 us
    pallas_call x2, Pallas kernels, point(): pl.pallas_call(point_kernel, grid=(steps,), in_specs=[row_spec, whole(mat...  36.9 us
    unnamed x18, local copies, waits for them, and re-layouts  29.5 us
    pallas_call x1, Pallas kernels, local(): pl.pallas_call(functools.partial(final_kernel, **sizes), grid=(steps,), i...  18.5 us
    all_to_all x4, starting transfers between devices, exchange(): lax.all_to_all(values, 'space', split_axis=0, concat_axis=0, tiled=True)  17.3 us
    pallas_call x1, Pallas kernels, local(): pl.pallas_call(functools.partial(analyse_kernel, **sizes), grid=(steps,),...  14.9 us
  transfers between devices with their start and end apart: 5, of which 3 were waited for; matrix products, arithmetic and copies ran while one was open for 11% of the time, Pallas kernels for 21%

profile of v2, /device:TPU:0, one launch (start us, length us, event | category | flops | bytes accessed | tf_op | source)
XLA Modules:
  0.0 383.9 jit_solution(17362718658918096245)
XLA Ops:
  0.6 0.0 copy-start
  0.6 14.9 %analyse.1 = bf16[8,2,8,16,512]{4,3,2,1,0:T(8,128)(2,1)} custom-call(bf16[4096,1280]{1,0:T(8,128)(2,1)} %bitcast.13, bf16[7,256,256]{2,1,0:T(8,128)(2,1)} %constant.51.clone.yf_ref, bf16[256,1024]{1,0:T(8,128)(2,1)} %constant.47.clone.zf_ref), custom_call_target="tpu_custom_call" | custom-call | tf_op jit(solution)/shard_map/analyse/pallas_call | solution.py:437
  15.5 6.3 %all-to-all-start = ((bf16[8,2,8,16,512]{4,3,2,1,0:T(8,128)(2,1)}), bf16[8,2,8,16,512]{4,3,2,1,0:T(8,128)(2,1)S(1)}, u32[]{:S(2)}, u32[]{:S(2)}) async-start(bf16[8,2,8,16,512]{4,3,2,1,0:T(8,128)(2,1)} %analyse.1), calls=%async_computation | async-start | bytes 4194304 | tf_op jit(solution)/shard_map/all_to_all | solution.py:431
  21.8 13.3 %copy.27.w_ref = bf16[2,20,20,9216]{3,2,1,0:T(8,128)(2,1)} copy(bf16[2,20,20,9216]{3,0,2,1:T(2,128)(2,1)} %param.17) | data formatting | bytes 29491200 | tf_op args[2]
  35.1 0.0 copy-start.7
  35.1 35.8 %all-to-all-done.r_ref = bf16[8,2,8,16,512]{4,3,2,1,0:T(8,128)(2,1)S(1)} async-done(((bf16[8,2,8,16,512]{4,3,2,1,0:T(8,128)(2,1)}), bf16[8,2,8,16,512]{4,3,2,1,0:T(8,128)(2,1)S(1)}, u32[]{:S(2)}, u32[]{:S(2)}) %all-to-all-start) | async-done | bytes 2097184 | tf_op jit(solution)/shard_map/all_to_all | solution.py:431
  70.9 0.0 copy-start.3
  70.9 1.3 copy-done.3
  72.2 30.1 %modes.2 = (bf16[2,20,9216]{2,1,0:T(8,128)(2,1)}, bf16[8,2,8,16,512]{4,3,2,1,0:T(8,128)(2,1)}) custom-call(bf16[8,2,8,16,512]{4,3,2,1,0:T(8,128)(2,1)} %copy-done.3, bf16[2,20,20,9216]{3,2,1,0:T(8,128)(2,1)} %copy.27.w_ref, bf16[128,256]{1,0:T(8,128)(2,1)} %constant.55.clone.gx_ref, bf16[2,768,640]{2,1,0:T(8,128)(2,1)} %constant.53.clone.perm_ref, ...), custom_call_target="tpu_custom_call" | custom-call | tf_op jit(solution)/shard_map/modes/pallas_call | solution.py:405
  102.3 3.8 all-to-all-start.1
  106.1 0.0 copy-done
  106.1 0.0 copy-done.7
  106.1 3.3 fusion.b_ref
  109.4 0.0 copy-start.6
  109.4 18.4 %point.2.d_ref = bf16[4096,1280]{1,0:T(8,128)(2,1)} custom-call(bf16[4096,1280]{1,0:T(8,128)(2,1)} %bitcast.14, bf16[1280,1280]{1,0:T(8,128)(2,1)} %fusion.b_ref), custom_call_target="tpu_custom_call" | custom-call | tf_op jit(solution)/shard_map/point/pallas_call | solution.py:392
  127.8 0.0 copy-done.6
  127.8 0.1 broadcast_in_dim.9
  127.9 0.7 reshape_reshape.3.bias_ref
  128.6 26.3 %all-to-all-done.1.q_ref = bf16[8,2,8,16,512]{4,3,2,1,0:T(8,128)(2,1)S(1)} async-done(((bf16[8,2,8,16,512]{4,3,2,1,0:T(8,128)(2,1)}), bf16[8,2,8,16,512]{4,3,2,1,0:T(8,128)(2,1)S(1)}, u32[]{:S(2)}, u32[]{:S(2)}) %all-to-all-start.1) | async-done | bytes 2097184 | tf_op jit(solution)/shard_map/all_to_all | solution.py:431
  154.9 0.0 copy-start.4
  154.9 1.3 copy-done.4
  156.2 52.8 %middle.1 = (bf16[4096,1280]{1,0:T(8,128)(2,1)}, bf16[8,2,8,16,512]{4,3,2,1,0:T(8,128)(2,1)}) custom-call(bf16[8,2,8,16,512]{4,3,2,1,0:T(8,128)(2,1)} %copy-done.4, bf16[4096,1280]{1,0:T(8,128)(2,1)} %point.2.d_ref, bf16[4096,1280]{1,0:T(8,128)(2,1)} %bitcast.15, f32[1,1280]{1,0:T(1,128)} %reshape_reshape.3.bias_ref, ...), custom_call_target="tpu_custom_call" | custom-call | tf_op jit(solution)/shard_map/middle/pallas_call | solution.py:451
  209.0 3.6 all-to-all-start.2
  212.6 1.6 reshape.24
  214.2 1.4 copy.30
  215.6 46.0 %all-to-all-done.2.r_ref = bf16[8,2,8,16,512]{4,3,2,1,0:T(8,128)(2,1)S(1)} async-done(((bf16[8,2,8,16,512]{4,3,2,1,0:T(8,128)(2,1)}), bf16[8,2,8,16,512]{4,3,2,1,0:T(8,128)(2,1)S(1)}, u32[]{:S(2)}, u32[]{:S(2)}) %all-to-all-start.2) | async-done | bytes 2097184 | tf_op jit(solution)/shard_map/all_to_all | solution.py:431
  261.6 0.0 copy-start.2
  261.6 3.7 all-to-all-start.4
  265.3 0.0 copy-done.2
  265.3 29.2 %modes.3 = (bf16[2,20,9216]{2,1,0:T(8,128)(2,1)}, bf16[8,2,8,16,512]{4,3,2,1,0:T(8,128)(2,1)}) custom-call(bf16[8,2,8,16,512]{4,3,2,1,0:T(8,128)(2,1)} %copy-done.2, bf16[2,20,20,9216]{3,2,1,0:T(8,128)(2,1)} %copy.27.w_ref, bf16[128,256]{1,0:T(8,128)(2,1)} %constant.55.clone.gx_ref, bf16[2,768,640]{2,1,0:T(8,128)(2,1)} %constant.53.clone.perm_ref, ...), custom_call_target="tpu_custom_call" | custom-call | tf_op jit(solution)/shard_map/modes/pallas_call | solution.py:405
  294.5 1.6 reshape.25
  296.1 0.6 copy.33
  296.6 0.0 all-to-all-done.4
  296.6 14.3 %all_to_all.30 = bf16[4,2,20,2304]{3,1,2,0:T(2,128)(2,1)} all-to-all(bf16[4,2,20,2304]{3,1,2,0:T(2,128)(2,1)S(1)} %copy.33), channel_id=1, replica_groups=mesh['dp'=4,'space'=8] {'dp'}, dimensions={0} | all-to-all | bytes 1474560 | tf_op jit(solution)/shard_map/all_to_all | solution.py:435
  311.0 3.6 all-to-all-start.3
  314.6 3.3 fusion.1.b_ref
  318.0 1.3 copy_convert_fusion.u_ref
  319.3 0.0 copy-start.5
  319.3 18.5 %point.3.p_ref = bf16[4096,1280]{1,0:T(8,128)(2,1)} custom-call(bf16[4096,1280]{1,0:T(8,128)(2,1)} %get-tuple-element.11.s_ref, bf16[1280,1280]{1,0:T(8,128)(2,1)} %fusion.1.b_ref), custom_call_target="tpu_custom_call" | custom-call | tf_op jit(solution)/shard_map/point/pallas_call | solution.py:392
  337.8 0.0 copy-done.5
  337.8 1.0 copy.34.g_ref
  338.8 13.0 %weight.1 = f32[2,20,20,2304]{3,2,1,0:T(8,128)} custom-call(f32[4,2,20,2304]{3,2,1,0:T(8,128)} %copy_convert_fusion.u_ref, bf16[4,2,20,2304]{3,2,1,0:T(8,128)(2,1)} %copy.34.g_ref), custom_call_target="tpu_custom_call" | custom-call | tf_op jit(solution)/shard_map/weight/pallas_call | solution.py:478
  351.8 12.3 %copy.35 = f32[2,20,20,2304]{3,0,2,1:T(2,128)} copy(f32[2,20,20,2304]{3,2,1,0:T(8,128)} %weight.1) | data formatting | bytes 14745600
  364.1 0.0 all-to-all-done.3.q_ref
  364.1 0.0 copy-start.1
  364.1 1.3 copy-done.1
  365.4 18.5 %final.1 = bf16[4096,1280]{1,0:T(8,128)(2,1)} custom-call(bf16[8,2,8,16,512]{4,3,2,1,0:T(8,128)(2,1)} %copy-done.1, bf16[4096,1280]{1,0:T(8,128)(2,1)} %point.3.p_ref, bf16[1024,256]{1,0:T(8,128)(2,1)} %constant.49.clone.zi_ref, bf16[7,256,256]{2,1,0:T(8,128)(2,1)} %constant.52.clone.yi_ref), custom_call_target="tpu_custom_call" | custom-call | tf_op jit(solution)/shard_map/final/pallas_call | solution.py:466
  (2 shorter events, 0.0 us)
Async XLA Ops:
  0.6 105.5 %copy-start = (bf16[20,20]{1,0:T(8,128)(2,1)S(1)}, bf16[20,20]{1,0:T(8,128)(2,1)}, u32[]{:S(2)}) copy-start(bf16[20,20]{1,0:T(8,128)(2,1)} %param.18) | copy-start | bytes 2404
  15.5 55.4 %all-to-all-start = ((bf16[8,2,8,16,512]{4,3,2,1,0:T(8,128)(2,1)}), bf16[8,2,8,16,512]{4,3,2,1,0:T(8,128)(2,1)S(1)}, u32[]{:S(2)}, u32[]{:S(2)}) async-start(bf16[8,2,8,16,512]{4,3,2,1,0:T(8,128)(2,1)} %analyse.1), calls=%async_computation | async-start | bytes 4194304 | tf_op jit(solution)/shard_map/all_to_all | solution.py:431
  35.1 71.0 %copy-start.7 = (bf16[1280,20]{1,0:T(8,128)(2,1)S(1)}, bf16[1280,20]{1,0:T(8,128)(2,1)}, u32[]{:S(2)}) copy-start(bf16[1280,20]{1,0:T(8,128)(2,1)} %constant.56.clone) | copy-start | bytes 153604
  70.9 1.3 copy-start.3
  102.3 52.6 %all-to-all-start.1 = ((bf16[8,2,8,16,512]{4,3,2,1,0:T(8,128)(2,1)}), bf16[8,2,8,16,512]{4,3,2,1,0:T(8,128)(2,1)S(1)}, u32[]{:S(2)}, u32[]{:S(2)}) async-start(bf16[8,2,8,16,512]{4,3,2,1,0:T(8,128)(2,1)} %get-tuple-element.8), calls=%async_computation.1 | async-start | bytes 4194304 | tf_op jit(solution)/shard_map/all_to_all | solution.py:431
  109.4 18.4 %copy-start.6 = (bf16[20]{0:T(256)(128)(2,1)S(1)}, bf16[20]{0:T(256)(128)(2,1)}, u32[]{:S(2)}) copy-start(bf16[20]{0:T(256)(128)(2,1)} %param.19) | copy-start | bytes 124
  154.9 1.3 copy-start.4
  209.0 52.6 %all-to-all-start.2 = ((bf16[8,2,8,16,512]{4,3,2,1,0:T(8,128)(2,1)}), bf16[8,2,8,16,512]{4,3,2,1,0:T(8,128)(2,1)S(1)}, u32[]{:S(2)}, u32[]{:S(2)}) async-start(bf16[8,2,8,16,512]{4,3,2,1,0:T(8,128)(2,1)} %get-tuple-element.9), calls=%async_computation.2 | async-start | bytes 4194304 | tf_op jit(solution)/shard_map/all_to_all | solution.py:431
  261.6 3.7 copy-start.2
  261.6 35.0 %all-to-all-start.4 = ((bf16[4,2,20,2304]{3,1,2,0:T(2,128)(2,1)}), bf16[4,2,20,2304]{3,1,2,0:T(2,128)(2,1)S(1)}, u32[]{:S(2)}, u32[]{:S(2)}) async-start(bf16[4,2,20,2304]{3,1,2,0:T(2,128)(2,1)} %copy.30), calls=%async_computation.4 | async-start | bytes 1474560 | tf_op jit(solution)/shard_map/all_to_all | solution.py:435
  311.0 53.1 %all-to-all-start.3 = ((bf16[8,2,8,16,512]{4,3,2,1,0:T(8,128)(2,1)}), bf16[8,2,8,16,512]{4,3,2,1,0:T(8,128)(2,1)S(1)}, u32[]{:S(2)}, u32[]{:S(2)}) async-start(bf16[8,2,8,16,512]{4,3,2,1,0:T(8,128)(2,1)} %get-tuple-element.10), calls=%async_computation.3 | async-start | bytes 4194304 | tf_op jit(solution)/shard_map/all_to_all | solution.py:431
  319.3 18.5 %copy-start.5 = (bf16[4,2,20,2304]{3,1,2,0:T(2,128)(2,1)S(1)}, bf16[4,2,20,2304]{3,1,2,0:T(2,128)(2,1)}, u32[]{:S(2)}) copy-start(bf16[4,2,20,2304]{3,1,2,0:T(2,128)(2,1)} %all_to_all.30) | copy-start | bytes 2211844
  364.1 1.3 copy-start.1

commit v3 on v2

--- a/solution.py
+++ b/solution.py
@@ -156,15 +156,9 @@
 
 
 def gelu_slope(pre_act):
-    size = jnp.abs(pre_act) * math.sqrt(0.5)
-    gauss = jnp.exp(-(size * size))
-    t = 1.0 / (1.0 + 0.3275911 * size)
-    poly = t * (
-        0.254829592 + t * (-0.284496736 + t * (1.421413741 + t * (-1.453152027 + t * 1.061405429)))
-    )
-    tail = 0.5 * poly * gauss
-    cumulative = jnp.where(pre_act >= 0.0, 1.0 - tail, tail)
-    return cumulative + pre_act * (gauss * (1.0 / math.sqrt(2.0 * math.pi)))
+    cumulative = 0.5 * (1.0 + lax.erf(pre_act * math.sqrt(0.5)))
+    density = jnp.exp(-0.5 * pre_act * pre_act) * (1.0 / math.sqrt(2.0 * math.pi))
+    return cumulative + pre_act * density
 
 
 def analyse_kernel(s_ref, yf_ref, zf_ref, out_ref, y_scr, yt_scr, *, x_rows, depth_rows):
@@ -179,7 +173,7 @@
 
 def middle_kernel(
     q_ref, d_ref, cot_ref, bias_ref, zi_ref, yi_ref, yf_ref, zf_ref, h_ref, out_ref,
-    z_scr, pre_scr, y_scr, yt_scr, *, x_rows, depth_rows,
+    z_scr, y_scr, yt_scr, *, x_rows, depth_rows,
 ):
     step = pl.program_id(0)
     block = x_rows * depth_rows
@@ -190,18 +184,13 @@
 
     start = pl.multiple_of(step * block, block)
     for group in range(5):
-        pre_scr[:, 256 * group : 256 * group + 256] = inverse_y(z_scr, yi_ref, start, block, group)
-
-    def rows_body(index, carry):
-        row = pl.multiple_of(index * 16, 16)
-        for group in range(5):
-            lanes = slice(256 * group, 256 * group + 256)
-            pre_act = pre_scr[pl.ds(row, 16), lanes] + d_ref[pl.ds(row, 16), lanes].astype(F32) + bias_ref[:, lanes]
-            hidden = cot_ref[pl.ds(row, 16), lanes].astype(F32) * gelu_slope(pre_act)
-            h_ref[pl.ds(row, 16), lanes] = hidden.astype(BF16)
-        return carry
-
-    lax.fori_loop(0, block // 16, rows_body, 0)
+        lanes = slice(256 * group, 256 * group + 256)
+        total = inverse_y(z_scr, yi_ref, start, block, group)
+        for first in range(0, block, 64):
+            rows = slice(first, first + 64)
+            pre_act = total[rows] + d_ref[rows, lanes].astype(F32) + bias_ref[:, lanes]
+            hidden = cot_ref[rows, lanes].astype(F32) * gelu_slope(pre_act)
+            h_ref[rows, lanes] = hidden.astype(BF16)
     forward_y(h_ref[...], yf_ref, y_scr)
     spread_x(y_scr, yt_scr, step, x_rows, depth_rows)
 
@@ -231,109 +220,115 @@
 
 def mode_kernel(
     r_ref, w_ref, gx_ref, perm_ref, permt_ref, u_ref, q_ref,
-    in_scr, out_scr, o_scr, ut_scr, u_scr, v_scr, vt_scr, *, backward,
+    in_scr, out_scr, o_scr, ut_scr, u_scr, v_scr, *, backward,
 ):
     step = pl.program_id(0)
+    pairs = pl.num_programs(0)
     owners, _, x_rows, modes_here, _ = r_ref.shape
+    count = modes_here // 2
     cells = 2 * NX
+    rows = 2 * x_rows * modes_here
     slot = lax.broadcasted_iota(jnp.int32, (C, 128), 1) // 32
 
     @pl.when(step == 0)
     def _():
-        o_scr[...] = jnp.zeros_like(o_scr)
         for owner in range(owners):
-            rows = 2 * x_rows * modes_here
             values = r_ref[owner].reshape(rows, LANES).astype(F32)
             for tile in range(4):
                 in_scr[tile, owner * rows : (owner + 1) * rows, :] = values[:, 128 * tile : 128 * tile + 128]
-
-    for half in range(2):
-        mode = 2 * step + half
-        tiles = [in_scr[tile, pl.ds(mode, cells, stride=modes_here), :] for tile in range(4)]
-        block = jnp.concatenate(tiles, axis=1).astype(BF16)
-        cols = lax.dot_general(block, gx_ref[...], (((0,), (0,)), ((), ())), preferred_element_type=F32)
-        for part in range(2):
-            vt_scr[part] = cols[:, 128 * part : 128 * part + 128]
-        for part in range(2):
-            for a in range(6):
-                piece = vt_scr[part, pl.ds(4 * a, C, stride=MY), :]
-                for r in range(1, 4):
-                    piece = jnp.where(slot == r, vt_scr[part, pl.ds(4 * a + r, C, stride=MY), :], piece)
-                ut_scr[24 * part : 24 * part + C, 128 * a : 128 * a + 128] = piece
-        moved = dot32(ut_scr[...].astype(BF16), perm_ref[half])
-        for part in range(2):
-            rows = moved[24 * part : 24 * part + C]
-            if half == 0:
-                u_scr[part, :C, :640] = rows
-            else:
-                u_scr[part, :C, 512:640] = u_scr[part, :C, 512:640] + rows[:, :128]
-                u_scr[part, :C, 640:] = rows[:, 128:]
+        for mode in range(modes_here):
+            pair, half = mode // 2, mode % 2
+            tiles = [in_scr[tile, pl.ds(mode, cells, stride=modes_here), :] for tile in range(4)]
+            block = jnp.concatenate(tiles, axis=1).astype(BF16)
+            cols = lax.dot_general(block, gx_ref[...], (((0,), (0,)), ((), ())), preferred_element_type=F32)
+            for part in range(2):
+                here = 2 * (mode % 2) + part
+                o_scr[here] = cols[:, 128 * part : 128 * part + 128]
+                for a in range(6):
+                    piece = o_scr[here, pl.ds(4 * a, C, stride=MY), :]
+                    for r in range(1, 4):
+                        piece = jnp.where(slot == r, o_scr[here, pl.ds(4 * a + r, C, stride=MY), :], piece)
+                    ut_scr[half, pair, part, :C, 128 * a : 128 * a + 128] = piece
+        even = dot32(ut_scr[0].reshape(count * 48, 768).astype(BF16), perm_ref[0])
+        odd = dot32(ut_scr[1].reshape(count * 48, 768).astype(BF16), perm_ref[1])
+        even = even.reshape(count, 2, 24, 640)
+        odd = odd.reshape(count, 2, 24, 640)
+        u_scr[:, :, :, :512] = even[:, :, :, :512]
+        u_scr[:, :, :, 512:640] = even[:, :, :, 512:] + odd[:, :, :, :128]
+        u_scr[:, :, :, 640:] = odd[:, :, :, 128:]
+
     for part in range(2):
-        u_ref[part] = u_scr[part, :C, :].astype(BF16)
-
+        u_ref[0, part] = u_scr[step, part, :C, :].astype(BF16)
     for chunk in range(3):
         lanes = slice(384 * chunk, 384 * chunk + 384)
         if backward:
-            real = u_scr[0, :C, lanes]
-            imag = u_scr[1, :C, lanes]
+            real = u_scr[step, 0, :C, lanes]
+            imag = u_scr[step, 1, :C, lanes]
             for ch in range(C):
                 w_real = w_ref[0, ch, :, lanes].astype(F32)
                 w_imag = w_ref[1, ch, :, lanes].astype(F32)
-                v_scr[0, ch : ch + 1, lanes] = jnp.sum(w_real * real + w_imag * imag, axis=0, keepdims=True)
-                v_scr[1, ch : ch + 1, lanes] = jnp.sum(w_real * imag - w_imag * real, axis=0, keepdims=True)
+                v_scr[step, 0, ch : ch + 1, lanes] = jnp.sum(w_real * real + w_imag * imag, axis=0, keepdims=True)
+                v_scr[step, 1, ch : ch + 1, lanes] = jnp.sum(w_real * imag - w_imag * real, axis=0, keepdims=True)
         else:
             real = jnp.zeros((C, 384), F32)
             imag = jnp.zeros((C, 384), F32)
             for ch in range(C):
                 w_real = w_ref[0, ch, :, lanes].astype(F32)
                 w_imag = w_ref[1, ch, :, lanes].astype(F32)
-                u_real = u_scr[0, ch : ch + 1, lanes]
-                u_imag = u_scr[1, ch : ch + 1, lanes]
+                u_real = u_scr[step, 0, ch : ch + 1, lanes]
+                u_imag = u_scr[step, 1, ch : ch + 1, lanes]
                 real = real + w_real * u_real - w_imag * u_imag
                 imag = imag + w_real * u_imag + w_imag * u_real
-            v_scr[0, :C, lanes] = real
-            v_scr[1, :C, lanes] = imag
-
-    for half in range(2):
-        mode = 2 * step + half
-        for part in range(2):
-            rows = v_scr[part, :, 512 * half : 512 * half + 640].astype(BF16)
-            moved = dot32(rows, permt_ref[half])
-            for a in range(6):
-                for r in range(4):
-                    piece = jnp.where(slot == r, moved[:C, 128 * a : 128 * a + 128], 0.0)
-                    o_scr[part, pl.ds(4 * a + r, C, stride=MY), :] = piece
-        cols = jnp.concatenate([o_scr[0], o_scr[1]], axis=1).astype(BF16)
-        back = lax.dot_general(gx_ref[...], cols, (((1,), (1,)), ((), ())), preferred_element_type=F32)
-        for tile in range(4):
-            out_scr[tile, pl.ds(mode, cells, stride=modes_here), :] = back[:, 128 * tile : 128 * tile + 128]
-
-    @pl.when(step == pl.num_programs(0) - 1)
+            v_scr[step, 0, :C, lanes] = real
+            v_scr[step, 1, :C, lanes] = imag
+
+    @pl.when(step == pairs - 1)
     def _():
+        for half in range(2):
+            values = v_scr[:, :, :, 512 * half : 512 * half + 640].reshape(count * 48, 640).astype(BF16)
+            ut_scr[half] = dot32(values, permt_ref[half]).reshape(count, 2, 24, 768)
+        o_scr[...] = jnp.zeros_like(o_scr)
+        for mode in range(modes_here):
+            pair, half = mode // 2, mode % 2
+            for part in range(2):
+                here = 2 * half + part
+                for a in range(6):
+                    values = ut_scr[half, pair, part, :C, 128 * a : 128 * a + 128]
+                    for r in range(4):
+                        o_scr[here, pl.ds(4 * a + r, C, stride=MY), :] = jnp.where(slot == r, values, 0.0)
+            cols = jnp.concatenate([o_scr[2 * half], o_scr[2 * half + 1]], axis=1).astype(BF16)
+            back = lax.dot_general(gx_ref[...], cols, (((1,), (1,)), ((), ())), preferred_element_type=F32)
+            for tile in range(4):
+                out_scr[tile, pl.ds(mode, cells, stride=modes_here), :] = back[:, 128 * tile : 128 * tile + 128]
         for owner in range(owners):
-            rows = 2 * x_rows * modes_here
             for tile in range(4):
                 values = out_scr[tile, owner * rows : (owner + 1) * rows, :].astype(BF16)
                 q_ref[owner, :, :, :, 128 * tile : 128 * tile + 128] = values.reshape(2, x_rows, modes_here, 128)
 
 
-def weight_kernel(u_ref, g_ref, out_ref):
-    groups = u_ref.shape[0]
-    width = u_ref.shape[3]
+def weight_kernel(*refs):
+    out_ref = refs[-1]
+    pieces = refs[:-1]
+    width = out_ref.shape[3]
     lane_step = 384 if width % 384 == 0 else width
+    row = pl.ds(pl.program_id(0), 1)
     for first in range(0, width, lane_step):
         lanes = slice(first, first + lane_step)
         real = jnp.zeros((C, lane_step), F32)
         imag = jnp.zeros((C, lane_step), F32)
-        for group in range(groups):
-            u_real = u_ref[group, 0, pl.ds(pl.program_id(0), 1), lanes]
-            u_imag = u_ref[group, 1, pl.ds(pl.program_id(0), 1), lanes]
-            g_real = g_ref[group, 0, :, lanes].astype(F32)
-            g_imag = g_ref[group, 1, :, lanes].astype(F32)
+        for u_ref, g_ref in zip(pieces[::2], pieces[1::2]):
+            u_real = u_ref[0, row, lanes]
+            u_imag = u_ref[1, row, lanes]
+            g_real = g_ref[0, :, lanes].astype(F32)
+            g_imag = g_ref[1, :, lanes].astype(F32)
             real = real + u_real * g_real + u_imag * g_imag
             imag = imag + u_real * g_imag - u_imag * g_real
         out_ref[0, 0, :, lanes] = real
         out_ref[1, 0, :, lanes] = imag
+
+
+def cost(micros):
+    return pl.CostEstimate(flops=int(micros * 1e9), transcendentals=0, bytes_accessed=int(micros * 3e6))
 
 
 def whole(array):
@@ -357,7 +352,7 @@
     dp_size = lax.axis_size("dp")
     share = modes // dp_size
     rows_all = ZT * x_rows
-    depth_rows = 64
+    depth_rows = 128
     block = depth_rows * x_rows
     steps = ZT // depth_rows
 
@@ -395,16 +390,24 @@
             in_specs=[row_spec, whole(matrix)],
             out_specs=row_spec,
             out_shape=shape_of((rows_all, CY), BF16),
-            compiler_params=params(),
+            compiler_params=params(), cost_estimate=cost(18),
             name="point",
         )(values, matrix)
 
+    aligned = share % KB == 0
+
     def modes_call(received, backward):
-        ints = modes_here // 2
-        out_shape = (shape_of((2, C, modes), BF16), payload)
+        pairs = modes_here // 2
+        if aligned:
+            per = share // KB
+            u_shape = shape_of((dp_size, 2, C, share), BF16)
+            u_spec = pl.BlockSpec((1, 2, C, KB), lambda i: (i // per, 0, 0, i % per))
+        else:
+            u_shape = shape_of((1, 2, C, modes), BF16)
+            u_spec = pl.BlockSpec((1, 2, C, KB), lambda i: (0, 0, 0, i))
         return pl.pallas_call(
             functools.partial(mode_kernel, backward=backward),
-            grid=(ints,),
+            grid=(pairs,),
             in_specs=[
                 whole(received),
                 pl.BlockSpec((2, C, C, KB), lambda i: (0, 0, 0, i)),
@@ -412,27 +415,37 @@
                 whole(perm),
                 whole(permt),
             ],
-            out_specs=(pl.BlockSpec((2, C, KB), lambda i: (0, 0, i)), whole(payload)),
-            out_shape=out_shape,
+            out_specs=(u_spec, whole(payload)),
+            out_shape=(u_shape, payload),
             scratch_shapes=[
                 pltpu.VMEM((4, 2 * NX * modes_here, 128), F32),
                 pltpu.VMEM((4, 2 * NX * modes_here, 128), F32),
-                pltpu.VMEM((2, LANES, 128), F32),
-                pltpu.VMEM((48, 768), F32),
-                pltpu.VMEM((2, 24, KB), F32),
-                pltpu.VMEM((2, 24, KB), F32),
-                pltpu.VMEM((2, LANES, 128), F32),
+                pltpu.VMEM((4, LANES, 128), F32),
+                pltpu.VMEM((2, pairs, 2, 24, 768), F32),
+                pltpu.VMEM((pairs, 2, 24, KB), F32),
+                pltpu.VMEM((pairs, 2, 24, KB), F32),
             ],
-            compiler_params=params(),
+            compiler_params=params(), cost_estimate=cost(27),
             name="modes",
         )(received, spec_weight, gx, perm, permt)
 
     def exchange(values):
         return lax.all_to_all(values, "space", split_axis=0, concat_axis=0, tiled=True)
 
+    me = lax.axis_index("dp")
+
     def to_owners(spectrum):
-        cut = jnp.transpose(spectrum.reshape(2, C, dp_size, share), (2, 0, 1, 3))
-        return lax.all_to_all(cut, "dp", split_axis=0, concat_axis=0, tiled=True)
+        if aligned:
+            cut = spectrum
+        else:
+            cut = jnp.transpose(spectrum[0].reshape(2, C, dp_size, share), (2, 0, 1, 3))
+        pieces = []
+        for shift in range(dp_size):
+            piece = lax.dynamic_index_in_dim(cut, (me + shift) % dp_size, 0, keepdims=False)
+            if shift:
+                piece = lax.ppermute(piece, "dp", [(i, (i + shift) % dp_size) for i in range(dp_size)])
+            pieces.append(piece)
+        return pieces
 
     coeffs = pl.pallas_call(
         functools.partial(analyse_kernel, **sizes),
@@ -441,13 +454,15 @@
         out_specs=whole(payload),
         out_shape=payload,
         scratch_shapes=[y_scr, yt_scr],
-        compiler_params=params(),
+        compiler_params=params(), cost_estimate=cost(14),
         name="analyse",
     )(sig, yf, zf_fwd)
-    u_hat, v_cells = modes_call(exchange(coeffs), False)
     direct = point(sig, point_weight)
+    received, direct = lax.optimization_barrier((exchange(coeffs), direct))
+    u_hat, v_cells = modes_call(received, False)
     bias_row = jnp.repeat(bias.astype(F32), NY).reshape(1, CY)
-    v_here = exchange(v_cells)
+    u_pieces = [piece.astype(F32) for piece in to_owners(u_hat)]
+    v_here, u_pieces = lax.optimization_barrier((exchange(v_cells), u_pieces))
     hidden, e_coeffs = pl.pallas_call(
         functools.partial(middle_kernel, **sizes),
         grid=(steps,),
@@ -456,12 +471,13 @@
         ],
         out_specs=(row_spec, whole(payload)),
         out_shape=(shape_of((rows_all, CY), BF16), payload),
-        scratch_shapes=[z_scr, pltpu.VMEM((block, CY), F32), y_scr, yt_scr],
-        compiler_params=params(),
+        scratch_shapes=[z_scr, y_scr, yt_scr],
+        compiler_params=params(), cost_estimate=cost(32),
         name="middle",
     )(v_here, direct, cot, bias_row, zi_inv, yi, yf, zf_inv)
     pointwise = point(hidden, point_weight.T)
-    g_hat, d_cells = modes_call(exchange(e_coeffs), True)
+    received, pointwise = lax.optimization_barrier((exchange(e_coeffs), pointwise))
+    g_hat, d_cells = modes_call(received, True)
     d_here = exchange(d_cells)
     grad_signal = pl.pallas_call(
         functools.partial(final_kernel, **sizes),
@@ -470,20 +486,19 @@
         out_specs=row_spec,
         out_shape=shape_of((rows_all, CY), BF16),
         scratch_shapes=[z_scr],
-        compiler_params=params(),
+        compiler_params=params(), cost_estimate=cost(16),
         name="final",
     )(d_here, pointwise, zi_fwd, yi)
-    u_all = to_owners(u_hat).astype(F32)
-    g_all = to_owners(g_hat)
+    pieces = [piece for pair in zip(u_pieces, to_owners(g_hat)) for piece in pair]
     spec_grad = pl.pallas_call(
         weight_kernel,
         grid=(C,),
-        in_specs=[whole(u_all), whole(g_all)],
+        in_specs=[whole(piece) for piece in pieces],
         out_specs=pl.BlockSpec((2, 1, C, share), lambda i: (0, i, 0, 0)),
         out_shape=shape_of((2, C, C, share), F32),
-        compiler_params=params(),
+        compiler_params=params(), cost_estimate=cost(13),
         name="weight",
-    )(u_all, g_all)
+    )(*pieces)
     return (grad_signal.reshape(signal.shape), spec_grad)
 
 

time: 385 us -> 341 us (0.89); the launches traced: 384 us -> 334 us
  Pallas kernels: 195 us -> 165 us
  blocking collectives: 14.3 us -> 0 us
  waiting for transfers between devices: 108 us -> 97.6 us
  starting transfers between devices: 21 us -> 26.1 us
    all_to_all x4, waiting for transfers between devices: 108 us -> 81.3 us  [exchange(): lax.all_to_all(values, 'space', split_axis=0, concat_axis=0, tiled=True)]
    pallas_call x1, Pallas kernels: 52.8 us -> 32.3 us  [local(): pl.pallas_call(functools.partial(middle_kernel, **sizes), grid=(steps,),...]
    ppermute x0 -> x6, waiting for transfers between devices: none -> 16.3 us  [to_owners(): lax.ppermute(piece, 'dp', [(i, (i + shift) % dp_size) for i in range(dp_s...]
    all_to_all x1 -> x0, blocking collectives: 14.3 us -> none  [to_owners(): return lax.all_to_all(cut, 'dp', split_axis=0, concat_axis=0, tiled=True)]
    ppermute x0 -> x6, starting transfers between devices: none -> 8.92 us  [to_owners(): lax.ppermute(piece, 'dp', [(i, (i + shift) % dp_size) for i in range(dp_s...]
    pallas_call x3, Pallas kernels: 72.3 us -> 65.6 us  [the longest x2 52.1 us: modes_call(): pl.pallas_call(functools.partial(mode_kernel, backward=backward), grid=(p...]
    unnamed x18 -> x26, local copies, waits for them, and re-layouts: 29.5 us -> 31.6 us
  transfers between devices with their start and end apart: 5 -> 10, of which waited for: 3 -> 9; matrix products, arithmetic and copies ran while one was open for 11% -> 11% of each run, Pallas kernels for 21% -> 15%
where the time goes in v3:
time: 341 us; the launch traced here: 334 us
  Pallas kernels  165 us (48%)
  waiting for transfers between devices  97.6 us (29%)
  local copies, waits for them, and re-layouts  34.4 us (10%)
  starting transfers between devices  26.1 us (8%)
  matrix products  5.45 us (2%)
  other arithmetic  4.55 us (1%)
    all_to_all x4, waiting for transfers between devices, exchange(): lax.all_to_all(values, 'space', split_axis=0, concat_axis=0, tiled=True)  81.3 us
    pallas_call x2, Pallas kernels, modes_call(): pl.pallas_call(functools.partial(mode_kernel, backward=backward), grid=(p...  52.1 us
    pallas_call x2, Pallas kernels, point(): pl.pallas_call(point_kernel, grid=(steps,), in_specs=[row_spec, whole(mat...  36.9 us
    pallas_call x1, Pallas kernels, local(): pl.pallas_call(functools.partial(middle_kernel, **sizes), grid=(steps,),...  32.3 us
    unnamed x26, local copies, waits for them, and re-layouts  31.6 us
    all_to_all x4, starting transfers between devices, exchange(): lax.all_to_all(values, 'space', split_axis=0, concat_axis=0, tiled=True)  17.1 us
    pallas_call x1, Pallas kernels, local(): pl.pallas_call(functools.partial(final_kernel, **sizes), grid=(steps,), i...  16.4 us
    ppermute x6, waiting for transfers between devices, to_owners(): lax.ppermute(piece, 'dp', [(i, (i + shift) % dp_size) for i in range(dp_s...  16.3 us
  transfers between devices with their start and end apart: 10, of which 9 were waited for; matrix products, arithmetic and copies ran while one was open for 11% of the time, Pallas kernels for 15%

profile of v3, /device:TPU:0, one launch (start us, length us, event | category | flops | bytes accessed | tf_op | source)
XLA Modules:
  0.0 334.1 jit_solution(13613527803482879678)
XLA Ops:
  0.6 0.0 copy-start
  0.6 13.7 %analyse.1 = bf16[8,2,8,16,512]{4,3,2,1,0:T(8,128)(2,1)} custom-call(bf16[4096,1280]{1,0:T(8,128)(2,1)} %bitcast.26, bf16[7,256,256]{2,1,0:T(8,128)(2,1)} %constant.111.clone.yf_ref, bf16[256,1024]{1,0:T(8,128)(2,1)} %constant.107.clone.zf_ref), custom_call_target="tpu_custom_call" | custom-call | flops 14000000000 | bytes 42000000 | tf_op jit(solution)/shard_map/analyse/pallas_call | solution.py:450
  14.4 6.3 %all-to-all-start = ((bf16[8,2,8,16,512]{4,3,2,1,0:T(8,128)(2,1)}), bf16[8,2,8,16,512]{4,3,2,1,0:T(8,128)(2,1)S(1)}, u32[]{:S(2)}, u32[]{:S(2)}) async-start(bf16[8,2,8,16,512]{4,3,2,1,0:T(8,128)(2,1)} %analyse.1), calls=%async_computation | async-start | bytes 4194304 | tf_op jit(solution)/shard_map/all_to_all | solution.py:433
  20.7 0.0 copy-start.10
  20.7 13.3 %copy.17.w_ref = bf16[2,20,20,9216]{3,2,1,0:T(8,128)(2,1)} copy(bf16[2,20,20,9216]{3,0,2,1:T(2,128)(2,1)} %param.17) | data formatting | bytes 29491200 | tf_op args[2]
  34.1 0.0 copy-done
  34.1 0.0 copy-done.10
  34.1 2.7 fusion.b_ref
  36.8 18.5 %point.2.d_ref = bf16[4096,1280]{1,0:T(8,128)(2,1)} custom-call(bf16[4096,1280]{1,0:T(8,128)(2,1)} %bitcast.27, bf16[1280,1280]{1,0:T(8,128)(2,1)} %fusion.b_ref), custom_call_target="tpu_custom_call" | custom-call | flops 17999998976 | bytes 54000000 | tf_op jit(solution)/shard_map/point/pallas_call | solution.py:387
  55.3 0.0 copy-start.6
  55.3 14.5 %all-to-all-done.r_ref = bf16[8,2,8,16,512]{4,3,2,1,0:T(8,128)(2,1)S(1)} async-done(((bf16[8,2,8,16,512]{4,3,2,1,0:T(8,128)(2,1)}), bf16[8,2,8,16,512]{4,3,2,1,0:T(8,128)(2,1)S(1)}, u32[]{:S(2)}, u32[]{:S(2)}) %all-to-all-start) | async-done | bytes 2097184 | tf_op jit(solution)/shard_map/all_to_all | solution.py:433
  69.8 0.0 copy-start.5
  69.8 1.3 copy-done.5
  71.1 25.5 %modes.2 = (bf16[4,2,20,2304]{3,2,1,0:T(8,128)(2,1)}, bf16[8,2,8,16,512]{4,3,2,1,0:T(8,128)(2,1)}) custom-call(bf16[8,2,8,16,512]{4,3,2,1,0:T(8,128)(2,1)} %copy-done.5, bf16[2,20,20,9216]{3,2,1,0:T(8,128)(2,1)} %copy.17.w_ref, bf16[128,256]{1,0:T(8,128)(2,1)} %constant.115.clone.gx_ref, bf16[2,768,640]{2,1,0:T(8,128)(2,1)} %constant.113.clone.perm_ref, ...), custom_call_target="tpu_custom_call" | custom-call | flops 27000000512 | bytes 81000000 | tf_op jit(solution)/shard_map/modes/pallas_call | solution.py:408
  96.6 3.6 %all-to-all-start.1 = ((bf16[8,2,8,16,512]{4,3,2,1,0:T(8,128)(2,1)}), bf16[8,2,8,16,512]{4,3,2,1,0:T(8,128)(2,1)S(1)}, u32[]{:S(2)}, u32[]{:S(2)}) async-start(bf16[8,2,8,16,512]{4,3,2,1,0:T(8,128)(2,1)} %get-tuple-element.18), calls=%async_computation.1 | async-start | bytes 4194304 | tf_op jit(solution)/shard_map/all_to_all | solution.py:433
  100.3 2.1 dynamic-slice_bitcast_fusion.4
  102.4 1.5 collective-permute-start
  103.9 1.5 collective-permute-start.1
  105.4 1.5 collective-permute-start.2
  106.9 0.0 copy-done.6
  106.9 0.1 broadcast_in_dim.9
  106.9 0.7 reshape_reshape.3.bias_ref
  107.6 4.0 %collective-permute-done = bf16[2,20,2304]{2,1,0:T(8,128)(2,1)S(1)} collective-permute-done((bf16[2,20,2304]{2,1,0:T(8,128)(2,1)S(1)}, bf16[2,20,2304]{2,1,0:T(8,128)(2,1)S(1)}, u32[]{:S(2)}, u32[]{:S(2)}) %collective-permute-start) | collective-permute-done | bytes 184352 | tf_op jit(solution)/shard_map/ppermute | solution.py:446
  111.6 0.8 convert_element_type.34.refs_2_
  112.4 3.3 collective-permute-done.1
  115.7 0.8 convert_element_type.35.refs_4_
  116.5 0.0 collective-permute-done.2
  116.5 0.8 convert_element_type.36.refs_6_
  117.3 31.9 %all-to-all-done.1.q_ref = bf16[8,2,8,16,512]{4,3,2,1,0:T(8,128)(2,1)S(1)} async-done(((bf16[8,2,8,16,512]{4,3,2,1,0:T(8,128)(2,1)}), bf16[8,2,8,16,512]{4,3,2,1,0:T(8,128)(2,1)S(1)}, u32[]{:S(2)}, u32[]{:S(2)}) %all-to-all-start.1) | async-done | bytes 2097184 | tf_op jit(solution)/shard_map/all_to_all | solution.py:433
  149.2 0.0 copy-start.2
  149.2 1.3 copy-done.2
  150.5 0.0 copy-start.11
  150.5 32.3 %middle.1 = (bf16[4096,1280]{1,0:T(8,128)(2,1)}, bf16[8,2,8,16,512]{4,3,2,1,0:T(8,128)(2,1)}) custom-call(bf16[8,2,8,16,512]{4,3,2,1,0:T(8,128)(2,1)} %copy-done.2, bf16[4096,1280]{1,0:T(8,128)(2,1)} %point.2.d_ref, bf16[4096,1280]{1,0:T(8,128)(2,1)} %bitcast.28, f32[1,1280]{1,0:T(1,128)} %reshape_reshape.3.bias_ref, ...), custom_call_target="tpu_custom_call" | custom-call | flops 32000000000 | bytes 96000000 | tf_op jit(solution)/shard_map/middle/pallas_call | solution.py:466
  182.8 3.6 %all-to-all-start.2 = ((bf16[8,2,8,16,512]{4,3,2,1,0:T(8,128)(2,1)}), bf16[8,2,8,16,512]{4,3,2,1,0:T(8,128)(2,1)S(1)}, u32[]{:S(2)}, u32[]{:S(2)}) async-start(bf16[8,2,8,16,512]{4,3,2,1,0:T(8,128)(2,1)} %get-tuple-element.22), calls=%async_computation.2 | async-start | bytes 4194304 | tf_op jit(solution)/shard_map/all_to_all | solution.py:433
  186.4 0.0 copy-done.11
  186.4 2.7 fusion.1.b_ref
  189.2 18.4 %point.3.p_ref = bf16[4096,1280]{1,0:T(8,128)(2,1)} custom-call(bf16[4096,1280]{1,0:T(8,128)(2,1)} %get-tuple-element.23.s_ref, bf16[1280,1280]{1,0:T(8,128)(2,1)} %fusion.1.b_ref), custom_call_target="tpu_custom_call" | custom-call | flops 17999998976 | bytes 54000000 | tf_op jit(solution)/shard_map/point/pallas_call | solution.py:387
  207.6 27.8 %all-to-all-done.2.r_ref = bf16[8,2,8,16,512]{4,3,2,1,0:T(8,128)(2,1)S(1)} async-done(((bf16[8,2,8,16,512]{4,3,2,1,0:T(8,128)(2,1)}), bf16[8,2,8,16,512]{4,3,2,1,0:T(8,128)(2,1)S(1)}, u32[]{:S(2)}, u32[]{:S(2)}) %all-to-all-start.2) | async-done | bytes 2097184 | tf_op jit(solution)/shard_map/all_to_all | solution.py:433
  235.4 0.0 copy-start.4
  235.4 1.3 copy-done.4
  236.7 26.6 %modes.3 = (bf16[4,2,20,2304]{3,2,1,0:T(8,128)(2,1)}, bf16[8,2,8,16,512]{4,3,2,1,0:T(8,128)(2,1)}) custom-call(bf16[8,2,8,16,512]{4,3,2,1,0:T(8,128)(2,1)} %copy-done.4, bf16[2,20,20,9216]{3,2,1,0:T(8,128)(2,1)} %copy.17.w_ref, bf16[128,256]{1,0:T(8,128)(2,1)} %constant.115.clone.gx_ref, bf16[2,768,640]{2,1,0:T(8,128)(2,1)} %constant.113.clone.perm_ref, ...), custom_call_target="tpu_custom_call" | custom-call | flops 27000000512 | bytes 81000000 | tf_op jit(solution)/shard_map/modes/pallas_call | solution.py:408
  263.3 3.6 %all-to-all-start.3 = ((bf16[8,2,8,16,512]{4,3,2,1,0:T(8,128)(2,1)}), bf16[8,2,8,16,512]{4,3,2,1,0:T(8,128)(2,1)S(1)}, u32[]{:S(2)}, u32[]{:S(2)}) async-start(bf16[8,2,8,16,512]{4,3,2,1,0:T(8,128)(2,1)} %get-tuple-element.25), calls=%async_computation.3 | async-start | bytes 4194304 | tf_op jit(solution)/shard_map/all_to_all | solution.py:433
  266.9 2.0 dynamic-slice_bitcast_fusion
  269.0 1.5 collective-permute-start.3
  270.5 1.5 collective-permute-start.4
  272.0 1.5 collective-permute-start.5
  273.4 4.7 %collective-permute-done.3.refs_3_ = bf16[2,20,2304]{2,1,0:T(8,128)(2,1)S(1)} collective-permute-done((bf16[2,20,2304]{2,1,0:T(8,128)(2,1)S(1)}, bf16[2,20,2304]{2,1,0:T(8,128)(2,1)S(1)}, u32[]{:S(2)}, u32[]{:S(2)}) %collective-permute-start.3) | collective-permute-done | bytes 184352 | tf_op jit(solution)/shard_map/ppermute | solution.py:446
  278.2 0.0 copy-start.7
  278.2 4.1 %collective-permute-done.4.refs_5_ = bf16[2,20,2304]{2,1,0:T(8,128)(2,1)S(1)} collective-permute-done((bf16[2,20,2304]{2,1,0:T(8,128)(2,1)S(1)}, bf16[2,20,2304]{2,1,0:T(8,128)(2,1)S(1)}, u32[]{:S(2)}, u32[]{:S(2)}) %collective-permute-start.4) | collective-permute-done | bytes 184352 | tf_op jit(solution)/shard_map/ppermute | solution.py:446
  282.3 0.0 copy-start.8
  282.3 0.1 collective-permute-done.5.refs_7_
  282.4 0.0 copy-start.9
  282.4 0.0 copy-done.7
  282.4 0.6 copy-done.8
  283.0 0.1 copy-done.9
  283.1 13.5 %weight.1 = f32[2,20,20,2304]{3,2,1,0:T(8,128)} custom-call(f32[2,20,2304]{2,1,0:T(8,128)} %get-tuple-element.27.refs_0_, bf16[2,20,2304]{2,1,0:T(8,128)(2,1)} %get-tuple-element.37.refs_1_, f32[2,20,2304]{2,1,0:T(8,128)} %convert_element_type.34.refs_2_, bf16[2,20,2304]{2,1,0:T(8,128)(2,1)} %copy-done.7, f32[2,20,2304]{2,1,0:T(8,128)} %convert_element_type.35.refs_4_, ...), custom_call_target="tpu_custom_call" | custom-call | flops 12999999488 | bytes 39000000 | tf_op jit(solution)/shard_map/weight/pallas_call | solution.py:493
  296.6 12.3 %copy.19 = f32[2,20,20,2304]{3,0,2,1:T(2,128)} copy(f32[2,20,20,2304]{3,2,1,0:T(8,128)} %weight.1) | data formatting | bytes 14745600
  308.8 7.1 %all-to-all-done.3.q_ref = bf16[8,2,8,16,512]{4,3,2,1,0:T(8,128)(2,1)S(1)} async-done(((bf16[8,2,8,16,512]{4,3,2,1,0:T(8,128)(2,1)}), bf16[8,2,8,16,512]{4,3,2,1,0:T(8,128)(2,1)S(1)}, u32[]{:S(2)}, u32[]{:S(2)}) %all-to-all-start.3) | async-done | bytes 2097184 | tf_op jit(solution)/shard_map/all_to_all | solution.py:433
  315.9 0.0 copy-start.3
  315.9 1.3 copy-done.3
  317.3 0.0 copy-start.1
  317.3 16.4 %final.1 = bf16[4096,1280]{1,0:T(8,128)(2,1)} custom-call(bf16[8,2,8,16,512]{4,3,2,1,0:T(8,128)(2,1)} %copy-done.3, bf16[4096,1280]{1,0:T(8,128)(2,1)} %point.3.p_ref, bf16[1024,256]{1,0:T(8,128)(2,1)} %constant.109.clone.zi_ref, bf16[7,256,256]{2,1,0:T(8,128)(2,1)} %constant.112.clone.yi_ref), custom_call_target="tpu_custom_call" | custom-call | flops 16000000000 | bytes 48000000 | tf_op jit(solution)/shard_map/final/pallas_call | solution.py:482
  333.7 0.0 copy-done.1
  (2 shorter events, 0.0 us)
Async XLA Ops:
  0.6 33.4 %copy-start = (bf16[20,20]{1,0:T(8,128)(2,1)S(1)}, bf16[20,20]{1,0:T(8,128)(2,1)}, u32[]{:S(2)}) copy-start(bf16[20,20]{1,0:T(8,128)(2,1)} %param.18) | copy-start | bytes 2404
  14.4 55.4 %all-to-all-start = ((bf16[8,2,8,16,512]{4,3,2,1,0:T(8,128)(2,1)}), bf16[8,2,8,16,512]{4,3,2,1,0:T(8,128)(2,1)S(1)}, u32[]{:S(2)}, u32[]{:S(2)}) async-start(bf16[8,2,8,16,512]{4,3,2,1,0:T(8,128)(2,1)} %analyse.1), calls=%async_computation | async-start | bytes 4194304 | tf_op jit(solution)/shard_map/all_to_all | solution.py:433
  20.7 13.3 %copy-start.10 = (bf16[1280,20]{1,0:T(8,128)(2,1)S(1)}, bf16[1280,20]{1,0:T(8,128)(2,1)}, u32[]{:S(2)}) copy-start(bf16[1280,20]{1,0:T(8,128)(2,1)} %constant.116.clone) | copy-start | bytes 153604
  55.3 51.6 %copy-start.6 = (bf16[20]{0:T(256)(128)(2,1)S(1)}, bf16[20]{0:T(256)(128)(2,1)}, u32[]{:S(2)}) copy-start(bf16[20]{0:T(256)(128)(2,1)} %param.19) | copy-start | bytes 124
  69.8 1.3 copy-start.5
  96.6 52.6 %all-to-all-start.1 = ((bf16[8,2,8,16,512]{4,3,2,1,0:T(8,128)(2,1)}), bf16[8,2,8,16,512]{4,3,2,1,0:T(8,128)(2,1)S(1)}, u32[]{:S(2)}, u32[]{:S(2)}) async-start(bf16[8,2,8,16,512]{4,3,2,1,0:T(8,128)(2,1)} %get-tuple-element.18), calls=%async_computation.1 | async-start | bytes 4194304 | tf_op jit(solution)/shard_map/all_to_all | solution.py:433
  102.4 9.2 %collective-permute-start = (bf16[2,20,2304]{2,1,0:T(8,128)(2,1)S(1)}, bf16[2,20,2304]{2,1,0:T(8,128)(2,1)S(1)}, u32[]{:S(2)}, u32[]{:S(2)}) collective-permute-start(bf16[2,20,2304]{2,1,0:T(8,128)(2,1)S(1)} %get-tuple-element.40), channel_id=1, source_target_pairs={{0,8},{8,16},{16,24},{24,0},{1,9},{9,17},{17,25},{25,1},{2,10},{10... | collective-permute-start | bytes 552968 | tf_op jit(solution)/shard_map/ppermute | solution.py:446
  103.9 11.8 %collective-permute-start.1 = (bf16[2,20,2304]{2,1,0:T(8,128)(2,1)S(1)}, bf16[2,20,2304]{2,1,0:T(8,128)(2,1)S(1)}, u32[]{:S(2)}, u32[]{:S(2)}) collective-permute-start(bf16[2,20,2304]{2,1,0:T(8,128)(2,1)S(1)} %get-tuple-element.39), channel_id=1, source_target_pairs={{0,16},{8,24},{16,0},{24,8},{1,17},{9,25},{17,1},{25,9},{2,18},{10... | collective-permute-start | bytes 552968 | tf_op jit(solution)/shard_map/ppermute | solution.py:446
  105.4 11.1 %collective-permute-start.2 = (bf16[2,20,2304]{2,1,0:T(8,128)(2,1)S(1)}, bf16[2,20,2304]{2,1,0:T(8,128)(2,1)S(1)}, u32[]{:S(2)}, u32[]{:S(2)}) collective-permute-start(bf16[2,20,2304]{2,1,0:T(8,128)(2,1)S(1)} %get-tuple-element.38), channel_id=1, source_target_pairs={{0,24},{8,0},{16,8},{24,16},{1,25},{9,1},{17,9},{25,17},{2,26},{10... | collective-permute-start | bytes 552968 | tf_op jit(solution)/shard_map/ppermute | solution.py:446
  149.2 1.3 copy-start.2
  150.5 35.9 %copy-start.11 = (bf16[1280,20]{1,0:T(8,128)(2,1)S(1)}, bf16[1280,20]{1,0:T(8,128)(2,1)}, u32[]{:S(2)}) copy-start(bf16[1280,20]{1,0:T(8,128)(2,1)} %constant.116.clone) | copy-start | bytes 153604
  182.8 52.6 %all-to-all-start.2 = ((bf16[8,2,8,16,512]{4,3,2,1,0:T(8,128)(2,1)}), bf16[8,2,8,16,512]{4,3,2,1,0:T(8,128)(2,1)S(1)}, u32[]{:S(2)}, u32[]{:S(2)}) async-start(bf16[8,2,8,16,512]{4,3,2,1,0:T(8,128)(2,1)} %get-tuple-element.22), calls=%async_computation.2 | async-start | bytes 4194304 | tf_op jit(solution)/shard_map/all_to_all | solution.py:433
  235.4 1.3 copy-start.4
  263.3 52.6 %all-to-all-start.3 = ((bf16[8,2,8,16,512]{4,3,2,1,0:T(8,128)(2,1)}), bf16[8,2,8,16,512]{4,3,2,1,0:T(8,128)(2,1)S(1)}, u32[]{:S(2)}, u32[]{:S(2)}) async-start(bf16[8,2,8,16,512]{4,3,2,1,0:T(8,128)(2,1)} %get-tuple-element.25), calls=%async_computation.3 | async-start | bytes 4194304 | tf_op jit(solution)/shard_map/all_to_all | solution.py:433
  269.0 9.2 %collective-permute-start.3 = (bf16[2,20,2304]{2,1,0:T(8,128)(2,1)S(1)}, bf16[2,20,2304]{2,1,0:T(8,128)(2,1)S(1)}, u32[]{:S(2)}, u32[]{:S(2)}) collective-permute-start(bf16[2,20,2304]{2,1,0:T(8,128)(2,1)S(1)} %get-tuple-element.36), channel_id=1, source_target_pairs={{0,8},{8,16},{16,24},{24,0},{1,9},{9,17},{17,25},{25,1},{2,10},{10... | collective-permute-start | bytes 552968 | tf_op jit(solution)/shard_map/ppermute | solution.py:446
  270.5 11.9 %collective-permute-start.4 = (bf16[2,20,2304]{2,1,0:T(8,128)(2,1)S(1)}, bf16[2,20,2304]{2,1,0:T(8,128)(2,1)S(1)}, u32[]{:S(2)}, u32[]{:S(2)}) collective-permute-start(bf16[2,20,2304]{2,1,0:T(8,128)(2,1)S(1)} %get-tuple-element.35), channel_id=1, source_target_pairs={{0,16},{8,24},{16,0},{24,8},{1,17},{9,25},{17,1},{25,9},{2,18},{10... | collective-permute-start | bytes 552968 | tf_op jit(solution)/shard_map/ppermute | solution.py:446
  272.0 10.4 %collective-permute-start.5 = (bf16[2,20,2304]{2,1,0:T(8,128)(2,1)S(1)}, bf16[2,20,2304]{2,1,0:T(8,128)(2,1)S(1)}, u32[]{:S(2)}, u32[]{:S(2)}) collective-permute-start(bf16[2,20,2304]{2,1,0:T(8,128)(2,1)S(1)} %get-tuple-element.34), channel_id=1, source_target_pairs={{0,24},{8,0},{16,8},{24,16},{1,25},{9,1},{17,9},{25,17},{2,26},{10... | collective-permute-start | bytes 552968 | tf_op jit(solution)/shard_map/ppermute | solution.py:446
  278.2 4.3 %copy-start.7 = (bf16[2,20,2304]{2,1,0:T(8,128)(2,1)}, bf16[2,20,2304]{2,1,0:T(8,128)(2,1)S(1)}, u32[]{:S(2)}) copy-start(bf16[2,20,2304]{2,1,0:T(8,128)(2,1)S(1)} %collective-permute-done.3.refs_3_) | copy-start | bytes 552964
  282.3 0.7 copy-start.8
  282.4 0.7 copy-start.9
  315.9 1.3 copy-start.3
  317.3 16.4 %copy-start.1 = (bf16[20,20]{1,0:T(8,128)(2,1)S(1)}, bf16[20,20]{1,0:T(8,128)(2,1)}, u32[]{:S(2)}) copy-start(bf16[20,20]{1,0:T(8,128)(2,1)} %param.18) | copy-start | bytes 2404

commit v4 on v3

--- a/solution.py
+++ b/solution.py
@@ -28,7 +28,7 @@
 BF = ml_dtypes.bfloat16
 BF16 = jnp.bfloat16
 F32 = jnp.float32
-VMEM_LIMIT = 56 * 1024 * 1024
+MIB = 1024 * 1024
 PAIRS = ((0, 0), (0, 1), (1, 1), (1, 2), (2, 2), (2, 3), (3, 4))
 
 
@@ -84,9 +84,9 @@
 def x_table(x_rows):
     table = complex_table(MX, NX)
     split = table.reshape(2, MX, 2, NX // x_rows, x_rows).transpose(3, 2, 4, 0, 1)
-    out = np.zeros((NX // x_rows, 2, x_rows, 2, 4, 32))
+    out = np.zeros((NX // x_rows, 2, x_rows, 2, 2, 32))
     out[..., :MX] = split[:, :, :, :, None, :]
-    return out.reshape(2 * NX, 256).astype(BF)
+    return out.reshape(2 * NX, 128).astype(BF)
 
 
 def lane_perms():
@@ -135,21 +135,23 @@
 
 def inverse_depth(q_ref, zi_ref, z_scr, x_rows):
     owners = q_ref.shape[0]
+    depth_rows = zi_ref.shape[1]
+    table = jnp.concatenate([zi_ref[0], zi_ref[1]], axis=0)
     for x in range(x_rows):
         rows = jnp.concatenate([q_ref[owner, part, x] for part in range(2) for owner in range(owners)], axis=0)
-        grid_rows = dot32(zi_ref[...], rows)
+        grid_rows = dot32(table, rows)
         for part in range(2):
             for tile in range(4):
-                z_scr[2 * tile + part, pl.ds(x, ZT, stride=x_rows), :] = grid_rows[
-                    part * ZT : (part + 1) * ZT, 128 * tile : 128 * tile + 128
+                z_scr[2 * tile + part, pl.ds(x, depth_rows, stride=x_rows), :] = grid_rows[
+                    part * depth_rows : (part + 1) * depth_rows, 128 * tile : 128 * tile + 128
                 ]
 
 
-def inverse_y(z_scr, yi_ref, start, count, group):
+def inverse_y(z_scr, yi_ref, group):
     total = None
     for k, (tile, pair_group) in enumerate(PAIRS):
         if pair_group == group:
-            rows = jnp.concatenate([z_scr[2 * tile + p, pl.ds(start, count), :] for p in range(2)], axis=1)
+            rows = jnp.concatenate([z_scr[2 * tile], z_scr[2 * tile + 1]], axis=1)
             part = dot32(rows.astype(BF16), yi_ref[k])
             total = part if total is None else total + part
     return total
@@ -178,14 +180,10 @@
     step = pl.program_id(0)
     block = x_rows * depth_rows
 
-    @pl.when(step == 0)
-    def _():
-        inverse_depth(q_ref, zi_ref, z_scr, x_rows)
-
-    start = pl.multiple_of(step * block, block)
+    inverse_depth(q_ref, zi_ref, z_scr, x_rows)
     for group in range(5):
         lanes = slice(256 * group, 256 * group + 256)
-        total = inverse_y(z_scr, yi_ref, start, block, group)
+        total = inverse_y(z_scr, yi_ref, group)
         for first in range(0, block, 64):
             rows = slice(first, first + 64)
             pre_act = total[rows] + d_ref[rows, lanes].astype(F32) + bias_ref[:, lanes]
@@ -199,18 +197,11 @@
         forward_depth(zf_ref, yt_scr, out_ref, x_rows)
 
 
-def final_kernel(q_ref, p_ref, zi_ref, yi_ref, out_ref, z_scr, *, x_rows, depth_rows):
-    step = pl.program_id(0)
-    block = x_rows * depth_rows
-
-    @pl.when(step == 0)
-    def _():
-        inverse_depth(q_ref, zi_ref, z_scr, x_rows)
-
-    start = pl.multiple_of(step * block, block)
+def final_kernel(q_ref, p_ref, zi_ref, yi_ref, out_ref, z_scr, *, x_rows):
+    inverse_depth(q_ref, zi_ref, z_scr, x_rows)
     for group in range(5):
         lanes = slice(256 * group, 256 * group + 256)
-        total = inverse_y(z_scr, yi_ref, start, block, group) + p_ref[:, lanes].astype(F32)
+        total = inverse_y(z_scr, yi_ref, group) + p_ref[:, lanes].astype(F32)
         out_ref[:, lanes] = total.astype(BF16)
 
 
@@ -228,7 +219,9 @@
     count = modes_here // 2
     cells = 2 * NX
     rows = 2 * x_rows * modes_here
-    slot = lax.broadcasted_iota(jnp.int32, (C, 128), 1) // 32
+    lane = lax.broadcasted_iota(jnp.int32, (C, 128), 1)
+    odd_slot = lane // 32 % 2 == 1
+    upper = lane >= 64
 
     @pl.when(step == 0)
     def _():
@@ -241,14 +234,14 @@
             tiles = [in_scr[tile, pl.ds(mode, cells, stride=modes_here), :] for tile in range(4)]
             block = jnp.concatenate(tiles, axis=1).astype(BF16)
             cols = lax.dot_general(block, gx_ref[...], (((0,), (0,)), ((), ())), preferred_element_type=F32)
-            for part in range(2):
-                here = 2 * (mode % 2) + part
-                o_scr[here] = cols[:, 128 * part : 128 * part + 128]
-                for a in range(6):
-                    piece = o_scr[here, pl.ds(4 * a, C, stride=MY), :]
-                    for r in range(1, 4):
-                        piece = jnp.where(slot == r, o_scr[here, pl.ds(4 * a + r, C, stride=MY), :], piece)
-                    ut_scr[half, pair, part, :C, 128 * a : 128 * a + 128] = piece
+            o_scr[half] = cols
+            for a in range(6):
+                pieces = [o_scr[half, pl.ds(4 * a + r, C, stride=MY), :] for r in range(4)]
+                first = jnp.where(odd_slot, pieces[1], pieces[0])
+                second = jnp.where(odd_slot, pieces[3], pieces[2])
+                lanes = slice(128 * a, 128 * a + 128)
+                ut_scr[half, pair, 0, :C, lanes] = jnp.where(upper, pltpu.roll(second, 64, 1), first)
+                ut_scr[half, pair, 1, :C, lanes] = jnp.where(upper, second, pltpu.roll(first, 64, 1))
         even = dot32(ut_scr[0].reshape(count * 48, 768).astype(BF16), perm_ref[0])
         odd = dot32(ut_scr[1].reshape(count * 48, 768).astype(BF16), perm_ref[1])
         even = even.reshape(count, 2, 24, 640)
@@ -290,14 +283,18 @@
         o_scr[...] = jnp.zeros_like(o_scr)
         for mode in range(modes_here):
             pair, half = mode // 2, mode % 2
-            for part in range(2):
-                here = 2 * half + part
-                for a in range(6):
-                    values = ut_scr[half, pair, part, :C, 128 * a : 128 * a + 128]
-                    for r in range(4):
-                        o_scr[here, pl.ds(4 * a + r, C, stride=MY), :] = jnp.where(slot == r, values, 0.0)
-            cols = jnp.concatenate([o_scr[2 * half], o_scr[2 * half + 1]], axis=1).astype(BF16)
-            back = lax.dot_general(gx_ref[...], cols, (((1,), (1,)), ((), ())), preferred_element_type=F32)
+            for a in range(6):
+                lanes = slice(128 * a, 128 * a + 128)
+                real = ut_scr[half, pair, 0, :C, lanes]
+                imag = ut_scr[half, pair, 1, :C, lanes]
+                first = jnp.where(upper, pltpu.roll(imag, 64, 1), real)
+                second = jnp.where(upper, imag, pltpu.roll(real, 64, 1))
+                for r, values in enumerate((first, first, second, second)):
+                    kept = odd_slot if r % 2 else jnp.logical_not(odd_slot)
+                    o_scr[half, pl.ds(4 * a + r, C, stride=MY), :] = jnp.where(kept, values, 0.0)
+            back = lax.dot_general(
+                gx_ref[...], o_scr[half].astype(BF16), (((1,), (1,)), ((), ())), preferred_element_type=F32
+            )
             for tile in range(4):
                 out_scr[tile, pl.ds(mode, cells, stride=modes_here), :] = back[:, 128 * tile : 128 * tile + 128]
         for owner in range(owners):
@@ -331,13 +328,12 @@
     return pl.CostEstimate(flops=int(micros * 1e9), transcendentals=0, bytes_accessed=int(micros * 3e6))
 
 
-def whole(array):
-    zeros = (0,) * len(array.shape)
-    return pl.BlockSpec(array.shape, lambda i: zeros)
-
-
-def params():
-    return pltpu.CompilerParams(dimension_semantics=("arbitrary",), vmem_limit_bytes=VMEM_LIMIT)
+def whole(_):
+    return pl.BlockSpec(memory_space=pltpu.VMEM)
+
+
+def params(mebibytes=52):
+    return pltpu.CompilerParams(dimension_semantics=("arbitrary",), vmem_limit_bytes=mebibytes * MIB)
 
 
 def shape_of(shape, kind):
@@ -360,7 +356,7 @@
     yf_np, yi_np = y_tiles()
     perm_np, permt_np = lane_perms()
     zf_fwd, zf_inv = jnp.asarray(forward_np), jnp.asarray(inverse_np)
-    zi_fwd, zi_inv = jnp.asarray(forward_np.T.copy()), jnp.asarray(inverse_np.T.copy())
+    zi_fwd, zi_inv = jnp.asarray(forward_np.T.reshape(2, ZT, -1)), jnp.asarray(inverse_np.T.reshape(2, ZT, -1))
     yf, yi = jnp.asarray(yf_np), jnp.asarray(yi_np)
     perm, permt = jnp.asarray(perm_np), jnp.asarray(permt_np)
     gx = jnp.asarray(x_table(x_rows))
@@ -370,10 +366,12 @@
     sig = signal.reshape(rows_all, CY)
     cot = cotangent.reshape(rows_all, CY)
     payload = shape_of((owners, 2, x_rows, modes_here, LANES), BF16)
+    payload_spec = pl.BlockSpec(payload.shape, lambda i: (0, 0, 0, 0, 0))
+    zi_spec = pl.BlockSpec((2, depth_rows, 2 * MZT), lambda i: (0, i, 0))
     row_spec = pl.BlockSpec((block, CY), lambda i: (i, 0))
     y_scr = pltpu.VMEM((8, block, 128), F32)
     yt_scr = pltpu.VMEM((x_rows, 2 * ZT, LANES), BF16)
-    z_scr = pltpu.VMEM((8, rows_all, 128), F32)
+    z_scr = pltpu.VMEM((8, block, 128), F32)
     sizes = dict(x_rows=x_rows, depth_rows=depth_rows)
 
     def point_block(weights):
@@ -415,17 +413,17 @@
                 whole(perm),
                 whole(permt),
             ],
-            out_specs=(u_spec, whole(payload)),
+            out_specs=(u_spec, payload_spec),
             out_shape=(u_shape, payload),
             scratch_shapes=[
                 pltpu.VMEM((4, 2 * NX * modes_here, 128), F32),
                 pltpu.VMEM((4, 2 * NX * modes_here, 128), F32),
-                pltpu.VMEM((4, LANES, 128), F32),
+                pltpu.VMEM((2, LANES, 128), F32),
                 pltpu.VMEM((2, pairs, 2, 24, 768), F32),
                 pltpu.VMEM((pairs, 2, 24, KB), F32),
                 pltpu.VMEM((pairs, 2, 24, KB), F32),
             ],
-            compiler_params=params(), cost_estimate=cost(27),
+            compiler_params=params(46), cost_estimate=cost(27),
             name="modes",
         )(received, spec_weight, gx, perm, permt)
 
@@ -451,7 +449,7 @@
         functools.partial(analyse_kernel, **sizes),
         grid=(steps,),
         in_specs=[row_spec, whole(yf), whole(zf_fwd)],
-        out_specs=whole(payload),
+        out_specs=payload_spec,
         out_shape=payload,
         scratch_shapes=[y_scr, yt_scr],
         compiler_params=params(), cost_estimate=cost(14),
@@ -467,9 +465,9 @@
         functools.partial(middle_kernel, **sizes),
         grid=(steps,),
         in_specs=[
-            whole(payload), row_spec, row_spec, whole(bias_row), whole(zi_inv), whole(yi), whole(yf), whole(zf_inv),
+            whole(payload), row_spec, row_spec, whole(bias_row), zi_spec, whole(yi), whole(yf), whole(zf_inv),
         ],
-        out_specs=(row_spec, whole(payload)),
+        out_specs=(row_spec, payload_spec),
         out_shape=(shape_of((rows_all, CY), BF16), payload),
         scratch_shapes=[z_scr, y_scr, yt_scr],
         compiler_params=params(), cost_estimate=cost(32),
@@ -480,9 +478,9 @@
     g_hat, d_cells = modes_call(received, True)
     d_here = exchange(d_cells)
     grad_signal = pl.pallas_call(
-        functools.partial(final_kernel, **sizes),
+        functools.partial(final_kernel, x_rows=x_rows),
         grid=(steps,),
-        in_specs=[whole(payload), row_spec, whole(zi_fwd), whole(yi)],
+        in_specs=[whole(payload), row_spec, zi_spec, whole(yi)],
         out_specs=row_spec,
         out_shape=shape_of((rows_all, CY), BF16),
         scratch_shapes=[z_scr],

time: 341 us -> 334 us (0.979)
  Pallas kernels: 165 us -> 154 us
  waiting for transfers between devices: 97.6 us -> 103 us
  starting transfers between devices: 26.1 us -> 29.6 us
    pallas_call x2, Pallas kernels: 52.1 us -> 44.9 us  [modes_call(): pl.pallas_call(functools.partial(mode_kernel, backward=backward), grid=(p...]
    all_to_all x4, waiting for transfers between devices: 81.3 us -> 86.1 us  [exchange(): lax.all_to_all(values, 'space', split_axis=0, concat_axis=0, tiled=True)]
    unnamed x26 -> x34, local copies, waits for them, and re-layouts: 31.6 us -> 33.6 us
  transfers between devices with their start and end apart: 10 -> 10, of which waited for: 9 -> 9; matrix products, arithmetic and copies ran while one was open for 11% -> 10% of each run, Pallas kernels for 15% -> 15%
where the time goes in v4:
time: 334 us; the launch traced here: 330 us
  Pallas kernels  154 us (46%)
  waiting for transfers between devices  103 us (31%)
  local copies, waits for them, and re-layouts  33.8 us (10%)
  starting transfers between devices  29.6 us (9%)
  matrix products  5.42 us (2%)
    all_to_all x4, waiting for transfers between devices, exchange(): lax.all_to_all(values, 'space', split_axis=0, concat_axis=0, tiled=True)  86.1 us
    pallas_call x2, Pallas kernels, modes_call(): pl.pallas_call(functools.partial(mode_kernel, backward=backward), grid=(p...  44.9 us
    pallas_call x2, Pallas kernels, point(): pl.pallas_call(point_kernel, grid=(steps,), in_specs=[row_spec, whole(mat...  37.1 us
    unnamed x34, local copies, waits for them, and re-layouts  33.6 us
    pallas_call x1, Pallas kernels, local(): pl.pallas_call(functools.partial(middle_kernel, **sizes), grid=(steps,),...  32.2 us
    all_to_all x4, starting transfers between devices, exchange(): lax.all_to_all(values, 'space', split_axis=0, concat_axis=0, tiled=True)  20.3 us
    ppermute x6, waiting for transfers between devices, to_owners(): lax.ppermute(piece, 'dp', [(i, (i + shift) % dp_size) for i in range(dp_s...  17.4 us
    pallas_call x1, Pallas kernels, local(): pl.pallas_call(functools.partial(final_kernel, x_rows=x_rows), grid=(step...  13.8 us
  transfers between devices with their start and end apart: 10, of which 9 were waited for; matrix products, arithmetic and copies ran while one was open for 10% of the time, Pallas kernels for 15%

profile of v4, /device:TPU:0, one launch (start us, length us, event | category | flops | bytes accessed | tf_op | source)
XLA Modules:
  0.0 329.8 jit_solution(1472156042844433559)
XLA Ops:
  0.6 0.0 copy-start
  0.6 0.0 copy-start.7
  0.7 1.2 copy-done.7
  1.8 0.0 copy-start.11
  1.8 1.0 copy-done.11
  2.9 13.4 %analyse.1 = bf16[8,2,8,16,512]{4,3,2,1,0:T(8,128)(2,1)} custom-call(bf16[4096,1280]{1,0:T(8,128)(2,1)} %bitcast.26, bf16[7,256,256]{2,1,0:T(8,128)(2,1)S(1)} %copy-done.7, bf16[256,1024]{1,0:T(8,128)(2,1)S(1)} %copy-done.11), custom_call_target="tpu_custom_call" | custom-call | flops 14000000000 | bytes 42000000 | tf_op jit(solution)/shard_map/analyse/pallas_call | solution.py:448
  16.3 6.9 %all-to-all-start = ((bf16[8,2,8,16,512]{4,3,2,1,0:T(8,128)(2,1)}), bf16[8,2,8,16,512]{4,3,2,1,0:T(8,128)(2,1)}, u32[]{:S(2)}, u32[]{:S(2)}) async-start(bf16[8,2,8,16,512]{4,3,2,1,0:T(8,128)(2,1)} %analyse.1), calls=%async_computation | async-start | bytes 4194304 | tf_op jit(solution)/shard_map/all_to_all | solution.py:431
  23.2 0.0 copy-start.14
  23.2 13.3 %copy.17.w_ref = bf16[2,20,20,9216]{3,2,1,0:T(8,128)(2,1)} copy(bf16[2,20,20,9216]{3,0,2,1:T(2,128)(2,1)} %param.17) | data formatting | bytes 29491200 | tf_op args[2]
  36.6 0.0 copy-done
  36.6 0.0 copy-done.14
  36.6 2.7 fusion.b_ref
  39.3 0.0 copy-start.2
  39.3 0.0 copy-start.12
  39.3 18.6 %point.2.d_ref = bf16[4096,1280]{1,0:T(8,128)(2,1)} custom-call(bf16[4096,1280]{1,0:T(8,128)(2,1)} %bitcast.27, bf16[1280,1280]{1,0:T(8,128)(2,1)} %fusion.b_ref), custom_call_target="tpu_custom_call" | custom-call | flops 17999998976 | bytes 54000000 | tf_op jit(solution)/shard_map/point/pallas_call | solution.py:385
  57.9 14.4 %all-to-all-done.r_ref = bf16[8,2,8,16,512]{4,3,2,1,0:T(8,128)(2,1)} async-done(((bf16[8,2,8,16,512]{4,3,2,1,0:T(8,128)(2,1)}), bf16[8,2,8,16,512]{4,3,2,1,0:T(8,128)(2,1)}, u32[]{:S(2)}, u32[]{:S(2)}) %all-to-all-start) | async-done | bytes 2097184 | tf_op jit(solution)/shard_map/all_to_all | solution.py:431
  72.3 0.0 copy-done.2
  72.3 0.0 copy-done.12
  72.3 0.0 copy-start.4
  72.3 1.5 copy-done.4
  73.9 0.0 copy-start.13
  73.9 21.9 %modes.2 = (bf16[4,2,20,2304]{3,2,1,0:T(8,128)(2,1)S(1)}, bf16[8,2,8,16,512]{4,3,2,1,0:T(8,128)(2,1)}) custom-call(bf16[8,2,8,16,512]{4,3,2,1,0:T(8,128)(2,1)} %all-to-all-done.r_ref, bf16[2,20,20,9216]{3,2,1,0:T(8,128)(2,1)} %copy.17.w_ref, bf16[128,128]{1,0:T(8,128)(2,1)S(1)} %copy-done.12, bf16[2,768,640]{2,1,0:T(8,128)(2,1)S(1)} %copy-done.2, ...), custom_call_target="tpu_custom_call" | custom-call | flops 27000000512 | bytes 81000000 | tf_op jit(solution)/shard_map/modes/pallas_call | solution.py:406
  95.7 0.0 copy-start.6
  95.7 0.0 copy-start.9
  95.7 4.5 %all-to-all-start.1 = ((bf16[8,2,8,16,512]{4,3,2,1,0:T(8,128)(2,1)}), bf16[8,2,8,16,512]{4,3,2,1,0:T(8,128)(2,1)}, u32[]{:S(2)}, u32[]{:S(2)}) async-start(bf16[8,2,8,16,512]{4,3,2,1,0:T(8,128)(2,1)} %get-tuple-element.18), calls=%async_computation.1 | async-start | bytes 4194304 | tf_op jit(solution)/shard_map/all_to_all | solution.py:431
  100.3 0.8 dynamic-slice_bitcast_fusion.4
  101.1 1.6 collective-permute-start
  102.7 1.5 collective-permute-start.1
  104.2 1.4 collective-permute-start.2
  105.7 0.0 copy-done.13
  105.7 0.1 broadcast_in_dim.9
  105.7 0.1 reshape_reshape.3.bias_ref
  105.8 4.6 %collective-permute-done = bf16[2,20,2304]{2,1,0:T(8,128)(2,1)S(1)} collective-permute-done((bf16[2,20,2304]{2,1,0:T(8,128)(2,1)S(1)}, bf16[2,20,2304]{2,1,0:T(8,128)(2,1)S(1)}, u32[]{:S(2)}, u32[]{:S(2)}) %collective-permute-start) | collective-permute-done | bytes 184352 | tf_op jit(solution)/shard_map/ppermute | solution.py:444
  110.4 4.1 %collective-permute-done.1 = bf16[2,20,2304]{2,1,0:T(8,128)(2,1)S(1)} collective-permute-done((bf16[2,20,2304]{2,1,0:T(8,128)(2,1)}, bf16[2,20,2304]{2,1,0:T(8,128)(2,1)S(1)}, u32[]{:S(2)}, u32[]{:S(2)}) %collective-permute-start.1) | collective-permute-done | bytes 184352 | tf_op jit(solution)/shard_map/ppermute | solution.py:444
  114.5 0.8 convert_element_type.35.refs_4_
  115.3 0.0 collective-permute-done.2
  115.3 0.8 convert_element_type.36.refs_6_
  116.1 33.2 %all-to-all-done.1.q_ref = bf16[8,2,8,16,512]{4,3,2,1,0:T(8,128)(2,1)} async-done(((bf16[8,2,8,16,512]{4,3,2,1,0:T(8,128)(2,1)}), bf16[8,2,8,16,512]{4,3,2,1,0:T(8,128)(2,1)}, u32[]{:S(2)}, u32[]{:S(2)}) %all-to-all-start.1) | async-done | bytes 2097184 | tf_op jit(solution)/shard_map/all_to_all | solution.py:431
  149.3 0.0 copy-done.6
  149.3 0.0 copy-done.9
  149.3 1.0 copy-done.10
  150.3 32.2 %middle.1 = (bf16[4096,1280]{1,0:T(8,128)(2,1)}, bf16[8,2,8,16,512]{4,3,2,1,0:T(8,128)(2,1)}) custom-call(bf16[8,2,8,16,512]{4,3,2,1,0:T(8,128)(2,1)} %all-to-all-done.1.q_ref, bf16[4096,1280]{1,0:T(8,128)(2,1)} %point.2.d_ref, bf16[4096,1280]{1,0:T(8,128)(2,1)} %bitcast.28, f32[1,1280]{1,0:T(1,128)S(1)} %reshape_reshape.3.bias_ref, ...), custom_call_target="tpu_custom_call" | custom-call | flops 32000000000 | bytes 96000000 | tf_op jit(solution)/shard_map/middle/pallas_call | solution.py:464
  182.6 4.6 %all-to-all-start.2 = ((bf16[8,2,8,16,512]{4,3,2,1,0:T(8,128)(2,1)}), bf16[8,2,8,16,512]{4,3,2,1,0:T(8,128)(2,1)}, u32[]{:S(2)}, u32[]{:S(2)}) async-start(bf16[8,2,8,16,512]{4,3,2,1,0:T(8,128)(2,1)} %get-tuple-element.22), calls=%async_computation.2 | async-start | bytes 4194304 | tf_op jit(solution)/shard_map/all_to_all | solution.py:431
  187.2 0.0 copy-done.15
  187.2 2.7 fusion.1.b_ref
  189.9 18.5 %point.3.p_ref = bf16[4096,1280]{1,0:T(8,128)(2,1)} custom-call(bf16[4096,1280]{1,0:T(8,128)(2,1)} %get-tuple-element.23.s_ref, bf16[1280,1280]{1,0:T(8,128)(2,1)} %fusion.1.b_ref), custom_call_target="tpu_custom_call" | custom-call | flops 17999998976 | bytes 54000000 | tf_op jit(solution)/shard_map/point/pallas_call | solution.py:385
  208.3 27.9 %all-to-all-done.2.r_ref = bf16[8,2,8,16,512]{4,3,2,1,0:T(8,128)(2,1)} async-done(((bf16[8,2,8,16,512]{4,3,2,1,0:T(8,128)(2,1)}), bf16[8,2,8,16,512]{4,3,2,1,0:T(8,128)(2,1)}, u32[]{:S(2)}, u32[]{:S(2)}) %all-to-all-start.2) | async-done | bytes 2097184 | tf_op jit(solution)/shard_map/all_to_all | solution.py:431
  236.2 1.5 copy-done.3
  237.8 1.5 copy-done.5
  239.3 23.0 %modes.3 = (bf16[4,2,20,2304]{3,2,1,0:T(8,128)(2,1)S(1)}, bf16[8,2,8,16,512]{4,3,2,1,0:T(8,128)(2,1)}) custom-call(bf16[8,2,8,16,512]{4,3,2,1,0:T(8,128)(2,1)} %all-to-all-done.2.r_ref, bf16[2,20,20,9216]{3,2,1,0:T(8,128)(2,1)} %copy.17.w_ref, bf16[128,128]{1,0:T(8,128)(2,1)S(1)} %copy-done.12, bf16[2,768,640]{2,1,0:T(8,128)(2,1)S(1)} %copy-done.3, ...), custom_call_target="tpu_custom_call" | custom-call | flops 27000000512 | bytes 81000000 | tf_op jit(solution)/shard_map/modes/pallas_call | solution.py:406
  262.3 4.3 %all-to-all-start.3 = ((bf16[8,2,8,16,512]{4,3,2,1,0:T(8,128)(2,1)}), bf16[8,2,8,16,512]{4,3,2,1,0:T(8,128)(2,1)}, u32[]{:S(2)}, u32[]{:S(2)}) async-start(bf16[8,2,8,16,512]{4,3,2,1,0:T(8,128)(2,1)} %get-tuple-element.25), calls=%async_computation.3 | async-start | bytes 4194304 | tf_op jit(solution)/shard_map/all_to_all | solution.py:431
  266.7 0.1 dynamic-slice_bitcast_fusion
  266.7 1.6 collective-permute-start.3
  268.3 1.5 collective-permute-start.4
  269.8 1.7 collective-permute-start.5
  271.5 4.5 %collective-permute-done.3.refs_3_ = bf16[2,20,2304]{2,1,0:T(8,128)(2,1)S(1)} collective-permute-done((bf16[2,20,2304]{2,1,0:T(8,128)(2,1)S(1)}, bf16[2,20,2304]{2,1,0:T(8,128)(2,1)S(1)}, u32[]{:S(2)}, u32[]{:S(2)}) %collective-permute-start.3) | collective-permute-done | bytes 184352 | tf_op jit(solution)/shard_map/ppermute | solution.py:444
  276.0 4.1 %collective-permute-done.4.refs_5_ = bf16[2,20,2304]{2,1,0:T(8,128)(2,1)S(1)} collective-permute-done((bf16[2,20,2304]{2,1,0:T(8,128)(2,1)S(1)}, bf16[2,20,2304]{2,1,0:T(8,128)(2,1)S(1)}, u32[]{:S(2)}, u32[]{:S(2)}) %collective-permute-start.4) | collective-permute-done | bytes 184352 | tf_op jit(solution)/shard_map/ppermute | solution.py:444
  280.1 0.1 collective-permute-done.5.refs_7_
  280.2 12.5 %weight.1 = f32[2,20,20,2304]{3,2,1,0:T(8,128)} custom-call(f32[2,20,2304]{2,1,0:T(8,128)S(1)} %get-tuple-element.27.refs_0_, bf16[2,20,2304]{2,1,0:T(8,128)(2,1)S(1)} %get-tuple-element.37.refs_1_, f32[2,20,2304]{2,1,0:T(8,128)S(1)} %convert_element_type.34.refs_2_, bf16[2,20,2304]{2,1,0:T(8,128)(2,1)S(1)} %collective-permute-done.3.refs_3_, ...), custom_call_target="tpu_custom_call" | custom-call | flops 12999999488 | bytes 39000000 | tf_op jit(solution)/shard_map/weight/pallas_call | solution.py:491
  292.8 12.3 %copy.19 = f32[2,20,20,2304]{3,0,2,1:T(2,128)} copy(f32[2,20,20,2304]{3,2,1,0:T(8,128)} %weight.1) | data formatting | bytes 14745600
  305.1 10.6 %all-to-all-done.3.q_ref = bf16[8,2,8,16,512]{4,3,2,1,0:T(8,128)(2,1)} async-done(((bf16[8,2,8,16,512]{4,3,2,1,0:T(8,128)(2,1)}), bf16[8,2,8,16,512]{4,3,2,1,0:T(8,128)(2,1)}, u32[]{:S(2)}, u32[]{:S(2)}) %all-to-all-start.3) | async-done | bytes 2097184 | tf_op jit(solution)/shard_map/all_to_all | solution.py:431
  315.7 0.0 copy-done.8
  315.7 13.8 %final.1 = bf16[4096,1280]{1,0:T(8,128)(2,1)} custom-call(bf16[8,2,8,16,512]{4,3,2,1,0:T(8,128)(2,1)} %all-to-all-done.3.q_ref, bf16[4096,1280]{1,0:T(8,128)(2,1)} %point.3.p_ref, bf16[2,512,256]{2,1,0:T(8,128)(2,1)S(1)} %copy-done.8, bf16[7,256,256]{2,1,0:T(8,128)(2,1)S(1)} %copy-done.6), custom_call_target="tpu_custom_call" | custom-call | flops 16000000000 | bytes 48000000 | tf_op jit(solution)/shard_map/final/pallas_call | solution.py:480
  329.5 0.0 copy-done.1
  (9 shorter events, 0.0 us)
Async XLA Ops:
  0.6 35.9 %copy-start = (bf16[20,20]{1,0:T(8,128)(2,1)S(1)}, bf16[20,20]{1,0:T(8,128)(2,1)}, u32[]{:S(2)}) copy-start(bf16[20,20]{1,0:T(8,128)(2,1)} %param.18) | copy-start | bytes 2404
  0.6 1.2 copy-start.7
  1.8 1.0 copy-start.11
  16.3 56.0 %all-to-all-start = ((bf16[8,2,8,16,512]{4,3,2,1,0:T(8,128)(2,1)}), bf16[8,2,8,16,512]{4,3,2,1,0:T(8,128)(2,1)}, u32[]{:S(2)}, u32[]{:S(2)}) async-start(bf16[8,2,8,16,512]{4,3,2,1,0:T(8,128)(2,1)} %analyse.1), calls=%async_computation | async-start | bytes 4194304 | tf_op jit(solution)/shard_map/all_to_all | solution.py:431
  23.2 13.4 %copy-start.14 = (bf16[1280,20]{1,0:T(8,128)(2,1)S(1)}, bf16[1280,20]{1,0:T(8,128)(2,1)}, u32[]{:S(2)}) copy-start(bf16[1280,20]{1,0:T(8,128)(2,1)} %constant.116.clone) | copy-start | bytes 153604
  39.3 33.0 %copy-start.2 = (bf16[2,768,640]{2,1,0:T(8,128)(2,1)S(1)}, bf16[2,768,640]{2,1,0:T(8,128)(2,1)}, u32[]{:S(2)}) copy-start(bf16[2,768,640]{2,1,0:T(8,128)(2,1)} %constant.113.clone.perm_ref) | copy-start | bytes 5898244
  39.3 33.0 %copy-start.12 = (bf16[128,128]{1,0:T(8,128)(2,1)S(1)}, bf16[128,128]{1,0:T(8,128)(2,1)}, u32[]{:S(2)}) copy-start(bf16[128,128]{1,0:T(8,128)(2,1)} %constant.115.clone.gx_ref) | copy-start | bytes 98308
  72.3 1.5 copy-start.4
  73.9 31.8 %copy-start.13 = (bf16[20]{0:T(256)(128)(2,1)S(1)}, bf16[20]{0:T(256)(128)(2,1)}, u32[]{:S(2)}) copy-start(bf16[20]{0:T(256)(128)(2,1)} %param.19) | copy-start | bytes 124
  95.7 53.6 %copy-start.6 = (bf16[7,256,256]{2,1,0:T(8,128)(2,1)S(1)}, bf16[7,256,256]{2,1,0:T(8,128)(2,1)}, u32[]{:S(2)}) copy-start(bf16[7,256,256]{2,1,0:T(8,128)(2,1)} %constant.112.clone.yi_ref) | copy-start | bytes 2752516
  95.7 53.6 %copy-start.9 = (bf16[2,512,256]{2,1,0:T(8,128)(2,1)S(1)}, bf16[2,512,256]{2,1,0:T(8,128)(2,1)}, u32[]{:S(2)}) copy-start(bf16[2,512,256]{2,1,0:T(8,128)(2,1)} %constant.110.clone.zi_ref) | copy-start | bytes 1572868
  95.7 53.5 %all-to-all-start.1 = ((bf16[8,2,8,16,512]{4,3,2,1,0:T(8,128)(2,1)}), bf16[8,2,8,16,512]{4,3,2,1,0:T(8,128)(2,1)}, u32[]{:S(2)}, u32[]{:S(2)}) async-start(bf16[8,2,8,16,512]{4,3,2,1,0:T(8,128)(2,1)} %get-tuple-element.18), calls=%async_computation.1 | async-start | bytes 4194304 | tf_op jit(solution)/shard_map/all_to_all | solution.py:431
  101.1 9.3 %collective-permute-start = (bf16[2,20,2304]{2,1,0:T(8,128)(2,1)S(1)}, bf16[2,20,2304]{2,1,0:T(8,128)(2,1)S(1)}, u32[]{:S(2)}, u32[]{:S(2)}) collective-permute-start(bf16[2,20,2304]{2,1,0:T(8,128)(2,1)S(1)} %get-tuple-element.40), channel_id=1, source_target_pairs={{0,8},{8,16},{16,24},{24,0},{1,9},{9,17},{17,25},{25,1},{2,10},{10... | collective-permute-start | bytes 552968 | tf_op jit(solution)/shard_map/ppermute | solution.py:444
  102.7 11.8 %collective-permute-start.1 = (bf16[2,20,2304]{2,1,0:T(8,128)(2,1)}, bf16[2,20,2304]{2,1,0:T(8,128)(2,1)S(1)}, u32[]{:S(2)}, u32[]{:S(2)}) collective-permute-start(bf16[2,20,2304]{2,1,0:T(8,128)(2,1)} %get-tuple-element.39), channel_id=1, source_target_pairs={{0,16},{8,24},{16,0},{24,8},{1,17},{9,25},{17,1},{25,9},{2,18},{10... | collective-permute-start | bytes 552968 | tf_op jit(solution)/shard_map/ppermute | solution.py:444
  104.2 11.1 %collective-permute-start.2 = (bf16[2,20,2304]{2,1,0:T(8,128)(2,1)S(1)}, bf16[2,20,2304]{2,1,0:T(8,128)(2,1)S(1)}, u32[]{:S(2)}, u32[]{:S(2)}) collective-permute-start(bf16[2,20,2304]{2,1,0:T(8,128)(2,1)S(1)} %get-tuple-element.38), channel_id=1, source_target_pairs={{0,24},{8,0},{16,8},{24,16},{1,25},{9,1},{17,9},{25,17},{2,26},{10... | collective-permute-start | bytes 552968 | tf_op jit(solution)/shard_map/ppermute | solution.py:444
  149.3 1.0 copy-start.10
  150.3 36.8 %copy-start.15 = (bf16[1280,20]{1,0:T(8,128)(2,1)S(1)}, bf16[1280,20]{1,0:T(8,128)(2,1)}, u32[]{:S(2)}) copy-start(bf16[1280,20]{1,0:T(8,128)(2,1)} %constant.116.clone) | copy-start | bytes 153604
  182.6 53.6 %all-to-all-start.2 = ((bf16[8,2,8,16,512]{4,3,2,1,0:T(8,128)(2,1)}), bf16[8,2,8,16,512]{4,3,2,1,0:T(8,128)(2,1)}, u32[]{:S(2)}, u32[]{:S(2)}) async-start(bf16[8,2,8,16,512]{4,3,2,1,0:T(8,128)(2,1)} %get-tuple-element.22), calls=%async_computation.2 | async-start | bytes 4194304 | tf_op jit(solution)/shard_map/all_to_all | solution.py:431
  236.2 1.5 copy-start.3
  237.8 1.5 copy-start.5
  262.3 53.4 %all-to-all-start.3 = ((bf16[8,2,8,16,512]{4,3,2,1,0:T(8,128)(2,1)}), bf16[8,2,8,16,512]{4,3,2,1,0:T(8,128)(2,1)}, u32[]{:S(2)}, u32[]{:S(2)}) async-start(bf16[8,2,8,16,512]{4,3,2,1,0:T(8,128)(2,1)} %get-tuple-element.25), calls=%async_computation.3 | async-start | bytes 4194304 | tf_op jit(solution)/shard_map/all_to_all | solution.py:431
  266.7 9.3 %collective-permute-start.3 = (bf16[2,20,2304]{2,1,0:T(8,128)(2,1)S(1)}, bf16[2,20,2304]{2,1,0:T(8,128)(2,1)S(1)}, u32[]{:S(2)}, u32[]{:S(2)}) collective-permute-start(bf16[2,20,2304]{2,1,0:T(8,128)(2,1)S(1)} %get-tuple-element.36), channel_id=1, source_target_pairs={{0,8},{8,16},{16,24},{24,0},{1,9},{9,17},{17,25},{25,1},{2,10},{10... | collective-permute-start | bytes 552968 | tf_op jit(solution)/shard_map/ppermute | solution.py:444
  268.3 11.8 %collective-permute-start.4 = (bf16[2,20,2304]{2,1,0:T(8,128)(2,1)S(1)}, bf16[2,20,2304]{2,1,0:T(8,128)(2,1)S(1)}, u32[]{:S(2)}, u32[]{:S(2)}) collective-permute-start(bf16[2,20,2304]{2,1,0:T(8,128)(2,1)S(1)} %get-tuple-element.35), channel_id=1, source_target_pairs={{0,16},{8,24},{16,0},{24,8},{1,17},{9,25},{17,1},{25,9},{2,18},{10... | collective-permute-start | bytes 552968 | tf_op jit(solution)/shard_map/ppermute | solution.py:444
  269.8 10.4 %collective-permute-start.5 = (bf16[2,20,2304]{2,1,0:T(8,128)(2,1)S(1)}, bf16[2,20,2304]{2,1,0:T(8,128)(2,1)S(1)}, u32[]{:S(2)}, u32[]{:S(2)}) collective-permute-start(bf16[2,20,2304]{2,1,0:T(8,128)(2,1)S(1)} %get-tuple-element.34), channel_id=1, source_target_pairs={{0,24},{8,0},{16,8},{24,16},{1,25},{9,1},{17,9},{25,17},{2,26},{10... | collective-permute-start | bytes 552968 | tf_op jit(solution)/shard_map/ppermute | solution.py:444
  292.8 23.0 %copy-start.8 = (bf16[2,512,256]{2,1,0:T(8,128)(2,1)S(1)}, bf16[2,512,256]{2,1,0:T(8,128)(2,1)}, u32[]{:S(2)}) copy-start(bf16[2,512,256]{2,1,0:T(8,128)(2,1)} %constant.109.clone.zi_ref) | copy-start | bytes 1572868
  315.7 13.8 %copy-start.1 = (bf16[20,20]{1,0:T(8,128)(2,1)S(1)}, bf16[20,20]{1,0:T(8,128)(2,1)}, u32[]{:S(2)}) copy-start(bf16[20,20]{1,0:T(8,128)(2,1)} %param.18) | copy-start | bytes 2404

commit v5 on v4

--- a/solution.py
+++ b/solution.py
@@ -23,6 +23,7 @@
 MZT = 128
 CY = C * NY
 LANES = 512
+CJ = C * MY
 KM = MX * MY
 KB = 2 * KM
 BF = ml_dtypes.bfloat16
@@ -95,7 +96,7 @@
         for j in range(MY):
             perm[:, 128 * (j // 4) + 32 * (j % 4) + i, i * MY + j] = 1.0
     perm[1] = np.roll(perm[1], 64, axis=1)
-    return perm.astype(BF), perm.transpose(0, 2, 1).astype(BF)
+    return perm.astype(BF)
 
 
 def dot32(left, right):
@@ -123,22 +124,27 @@
 
 
 def forward_depth(zf_ref, yt_scr, out_ref, x_rows):
-    owners = out_ref.shape[0]
-    modes_here = MZT // owners
+    owners, _, x_groups, modes_here, _ = out_ref.shape
+    joined = x_rows // x_groups
     for x in range(x_rows):
         coeffs = dot32(zf_ref[...], yt_scr[x]).astype(BF16)
+        lane = CJ * (x % joined)
         for owner in range(owners):
             for part in range(2):
                 row = part * MZT + owner * modes_here
-                out_ref[owner, part, x] = coeffs[row : row + modes_here]
+                out_ref[owner, part, x // joined, :, lane : lane + CJ] = coeffs[row : row + modes_here, :CJ]
 
 
 def inverse_depth(q_ref, zi_ref, z_scr, x_rows):
-    owners = q_ref.shape[0]
+    owners, _, x_groups, _, _ = q_ref.shape
+    joined = x_rows // x_groups
     depth_rows = zi_ref.shape[1]
+    margin = jnp.zeros((2 * MZT, LANES - CJ), BF16)
     table = jnp.concatenate([zi_ref[0], zi_ref[1]], axis=0)
     for x in range(x_rows):
-        rows = jnp.concatenate([q_ref[owner, part, x] for part in range(2) for owner in range(owners)], axis=0)
+        group, lanes = x // joined, slice(CJ * (x % joined), CJ * (x % joined) + CJ)
+        rows = [q_ref[owner, part, group, :, lanes] for part in range(2) for owner in range(owners)]
+        rows = jnp.concatenate([jnp.concatenate(rows, axis=0), margin], axis=1)
         grid_rows = dot32(table, rows)
         for part in range(2):
             for tile in range(4):
@@ -157,10 +163,10 @@
     return total
 
 
-def gelu_slope(pre_act):
-    cumulative = 0.5 * (1.0 + lax.erf(pre_act * math.sqrt(0.5)))
-    density = jnp.exp(-0.5 * pre_act * pre_act) * (1.0 / math.sqrt(2.0 * math.pi))
-    return cumulative + pre_act * density
+def twice_slope(pre_act):
+    scaled = pre_act * math.sqrt(0.5)
+    gauss = jnp.exp2(scaled * scaled * -math.log2(math.e))
+    return (1.0 + lax.erf(scaled)) + (2.0 / math.sqrt(math.pi)) * scaled * gauss
 
 
 def analyse_kernel(s_ref, yf_ref, zf_ref, out_ref, y_scr, yt_scr, *, x_rows, depth_rows):
@@ -187,7 +193,7 @@
         for first in range(0, block, 64):
             rows = slice(first, first + 64)
             pre_act = total[rows] + d_ref[rows, lanes].astype(F32) + bias_ref[:, lanes]
-            hidden = cot_ref[rows, lanes].astype(F32) * gelu_slope(pre_act)
+            hidden = (0.5 * cot_ref[rows, lanes].astype(F32)) * twice_slope(pre_act)
             h_ref[rows, lanes] = hidden.astype(BF16)
     forward_y(h_ref[...], yf_ref, y_scr)
     spread_x(y_scr, yt_scr, step, x_rows, depth_rows)
@@ -210,25 +216,29 @@
 
 
 def mode_kernel(
-    r_ref, w_ref, gx_ref, perm_ref, permt_ref, u_ref, q_ref,
+    r_ref, w_ref, gx_ref, perm_ref, u_ref, q_ref,
     in_scr, out_scr, o_scr, ut_scr, u_scr, v_scr, *, backward,
 ):
     step = pl.program_id(0)
     pairs = pl.num_programs(0)
-    owners, _, x_rows, modes_here, _ = r_ref.shape
+    owners, _, x_groups, modes_here, width = r_ref.shape
+    joined = width // CJ
+    blocks = [(o, p, g, k) for o in range(owners) for p in range(2) for g in range(x_groups) for k in range(joined)]
     count = modes_here // 2
     cells = 2 * NX
-    rows = 2 * x_rows * modes_here
     lane = lax.broadcasted_iota(jnp.int32, (C, 128), 1)
     odd_slot = lane // 32 % 2 == 1
     upper = lane >= 64
 
     @pl.when(step == 0)
     def _():
-        for owner in range(owners):
-            values = r_ref[owner].reshape(rows, LANES).astype(F32)
+        for index, (owner, part, group, k) in enumerate(blocks):
+            values = r_ref[owner, part, group, :, CJ * k : CJ * k + CJ].astype(F32)
             for tile in range(4):
-                in_scr[tile, owner * rows : (owner + 1) * rows, :] = values[:, 128 * tile : 128 * tile + 128]
+                end = min(128 * tile + 128, CJ)
+                in_scr[tile, index * modes_here : (index + 1) * modes_here, : end - 128 * tile] = values[
+                    :, 128 * tile : end
+                ]
         for mode in range(modes_here):
             pair, half = mode // 2, mode % 2
             tiles = [in_scr[tile, pl.ds(mode, cells, stride=modes_here), :] for tile in range(4)]
@@ -279,7 +289,8 @@
     def _():
         for half in range(2):
             values = v_scr[:, :, :, 512 * half : 512 * half + 640].reshape(count * 48, 640).astype(BF16)
-            ut_scr[half] = dot32(values, permt_ref[half]).reshape(count, 2, 24, 768)
+            moved = lax.dot_general(values, perm_ref[half], (((1,), (1,)), ((), ())), preferred_element_type=F32)
+            ut_scr[half] = moved.reshape(count, 2, 24, 768)
         o_scr[...] = jnp.zeros_like(o_scr)
         for mode in range(modes_here):
             pair, half = mode // 2, mode % 2
@@ -297,10 +308,10 @@
             )
             for tile in range(4):
                 out_scr[tile, pl.ds(mode, cells, stride=modes_here), :] = back[:, 128 * tile : 128 * tile + 128]
-        for owner in range(owners):
-            for tile in range(4):
-                values = out_scr[tile, owner * rows : (owner + 1) * rows, :].astype(BF16)
-                q_ref[owner, :, :, :, 128 * tile : 128 * tile + 128] = values.reshape(2, x_rows, modes_here, 128)
+        for index, (owner, part, group, k) in enumerate(blocks):
+            rows = slice(index * modes_here, (index + 1) * modes_here)
+            values = jnp.concatenate([out_scr[tile, rows, :] for tile in range(4)], axis=1)
+            q_ref[owner, part, group, :, CJ * k : CJ * k + CJ] = values[:, :CJ].astype(BF16)
 
 
 def weight_kernel(*refs):
@@ -332,6 +343,11 @@
     return pl.BlockSpec(memory_space=pltpu.VMEM)
 
 
+def fixed(array):
+    zeros = (0,) * len(array.shape)
+    return pl.BlockSpec(array.shape, lambda i: zeros)
+
+
 def params(mebibytes=52):
     return pltpu.CompilerParams(dimension_semantics=("arbitrary",), vmem_limit_bytes=mebibytes * MIB)
 
@@ -354,18 +370,18 @@
 
     forward_np, inverse_np = depth_tables()
     yf_np, yi_np = y_tiles()
-    perm_np, permt_np = lane_perms()
     zf_fwd, zf_inv = jnp.asarray(forward_np), jnp.asarray(inverse_np)
     zi_fwd, zi_inv = jnp.asarray(forward_np.T.reshape(2, ZT, -1)), jnp.asarray(inverse_np.T.reshape(2, ZT, -1))
     yf, yi = jnp.asarray(yf_np), jnp.asarray(yi_np)
-    perm, permt = jnp.asarray(perm_np), jnp.asarray(permt_np)
+    perm = jnp.asarray(lane_perms())
     gx = jnp.asarray(x_table(x_rows))
     spread = jnp.asarray((np.arange(CY)[:, None] // NY == np.arange(C)[None, :]).astype(BF))
     same_y = jnp.asarray(np.arange(NY)[:, None] == np.arange(NY)[None, :])
 
     sig = signal.reshape(rows_all, CY)
     cot = cotangent.reshape(rows_all, CY)
-    payload = shape_of((owners, 2, x_rows, modes_here, LANES), BF16)
+    joined = math.gcd(x_rows, 4)
+    payload = shape_of((owners, 2, x_rows // joined, modes_here, joined * CJ), BF16)
     payload_spec = pl.BlockSpec(payload.shape, lambda i: (0, 0, 0, 0, 0))
     zi_spec = pl.BlockSpec((2, depth_rows, 2 * MZT), lambda i: (0, i, 0))
     row_spec = pl.BlockSpec((block, CY), lambda i: (i, 0))
@@ -411,7 +427,6 @@
                 pl.BlockSpec((2, C, C, KB), lambda i: (0, 0, 0, i)),
                 whole(gx),
                 whole(perm),
-                whole(permt),
             ],
             out_specs=(u_spec, payload_spec),
             out_shape=(u_shape, payload),
@@ -425,7 +440,7 @@
             ],
             compiler_params=params(46), cost_estimate=cost(27),
             name="modes",
-        )(received, spec_weight, gx, perm, permt)
+        )(received, spec_weight, gx, perm)
 
     def exchange(values):
         return lax.all_to_all(values, "space", split_axis=0, concat_axis=0, tiled=True)
@@ -448,7 +463,7 @@
     coeffs = pl.pallas_call(
         functools.partial(analyse_kernel, **sizes),
         grid=(steps,),
-        in_specs=[row_spec, whole(yf), whole(zf_fwd)],
+        in_specs=[row_spec, fixed(yf), fixed(zf_fwd)],
         out_specs=payload_spec,
         out_shape=payload,
         scratch_shapes=[y_scr, yt_scr],
@@ -465,7 +480,7 @@
         functools.partial(middle_kernel, **sizes),
         grid=(steps,),
         in_specs=[
-            whole(payload), row_spec, row_spec, whole(bias_row), zi_spec, whole(yi), whole(yf), whole(zf_inv),
+            whole(payload), row_spec, row_spec, whole(bias_row), zi_spec, whole(yi), whole(yf), fixed(zf_inv),
         ],
         out_specs=(row_spec, payload_spec),
         out_shape=(shape_of((rows_all, CY), BF16), payload),

time: 334 us -> 316 us (0.946)
  waiting for transfers between devices: 103 us -> 90.5 us
  Pallas kernels: 154 us -> 150 us
    all_to_all x4, waiting for transfers between devices: 86.1 us -> 74.5 us  [exchange(): lax.all_to_all(values, 'space', split_axis=0, concat_axis=0, tiled=True)]
    unnamed x34 -> x44, local copies, waits for them, and re-layouts: 33.6 us -> 33.1 us
  transfers between devices with their start and end apart: 10 -> 10, of which waited for: 9 -> 9; matrix products, arithmetic and copies ran while one was open for 10% -> 11% of each run, Pallas kernels for 15% -> 16%
where the time goes in v5:
time: 316 us; the launch traced here: 312 us
  Pallas kernels  150 us (47%)
  waiting for transfers between devices  90.5 us (29%)
  local copies, waits for them, and re-layouts  34 us (11%)
  starting transfers between devices  28.7 us (9%)
  matrix products  5.44 us (2%)
    all_to_all x4, waiting for transfers between devices, exchange(): lax.all_to_all(values, 'space', split_axis=0, concat_axis=0, tiled=True)  74.5 us
    pallas_call x2, Pallas kernels, modes_call(): pl.pallas_call(functools.partial(mode_kernel, backward=backward), grid=(p...  44.2 us
    pallas_call x2, Pallas kernels, point(): pl.pallas_call(point_kernel, grid=(steps,), in_specs=[row_spec, whole(mat...  36.9 us
    unnamed x44, local copies, waits for them, and re-layouts  33.1 us
    pallas_call x1, Pallas kernels, local(): pl.pallas_call(functools.partial(middle_kernel, **sizes), grid=(steps,),...  29.7 us
    all_to_all x4, starting transfers between devices, exchange(): lax.all_to_all(values, 'space', split_axis=0, concat_axis=0, tiled=True)  19.6 us
    ppermute x6, waiting for transfers between devices, to_owners(): lax.ppermute(piece, 'dp', [(i, (i + shift) % dp_size) for i in range(dp_s...  16 us
    pallas_call x1, Pallas kernels, local(): pl.pallas_call(functools.partial(analyse_kernel, **sizes), grid=(steps,),...  13.4 us
  transfers between devices with their start and end apart: 10, of which 9 were waited for; matrix products, arithmetic and copies ran while one was open for 11% of the time, Pallas kernels for 16%

profile of v5, /device:TPU:0, one launch (start us, length us, event | category | flops | bytes accessed | tf_op | source)
XLA Modules:
  0.0 311.9 jit_solution(10378207044329459872)
XLA Ops:
  0.6 0.0 copy-start
  0.6 0.0 copy-start.7
  0.7 1.2 copy-done.7
  1.8 1.0 copy-done.11
  2.9 13.4 %analyse.1 = bf16[8,2,2,16,1920]{4,3,2,1,0:T(8,128)(2,1)} custom-call(bf16[4096,1280]{1,0:T(8,128)(2,1)} %bitcast.26, bf16[7,256,256]{2,1,0:T(8,128)(2,1)S(1)} %copy-done.7, bf16[256,1024]{1,0:T(8,128)(2,1)S(1)} %copy-done.11), custom_call_target="tpu_custom_call" | custom-call | flops 14000000000 | bytes 42000000 | tf_op jit(solution)/shard_map/analyse/pallas_call | solution.py:463
  16.3 6.5 %all-to-all-start = ((bf16[8,2,2,16,1920]{4,3,2,1,0:T(8,128)(2,1)}), bf16[8,2,2,16,1920]{4,3,2,1,0:T(8,128)(2,1)S(1)}, u32[]{:S(2)}, u32[]{:S(2)}) async-start(bf16[8,2,2,16,1920]{4,3,2,1,0:T(8,128)(2,1)} %analyse.1), calls=%async_computation | async-start | bytes 3932160 | tf_op jit(solution)/shard_map/all_to_all | solution.py:446
  22.8 0.0 copy-start.19
  22.8 13.3 %copy.16.w_ref = bf16[2,20,20,9216]{3,2,1,0:T(8,128)(2,1)} copy(bf16[2,20,20,9216]{3,0,2,1:T(2,128)(2,1)} %param.16) | data formatting | bytes 29491200 | tf_op args[2]
  36.1 0.0 copy-start.13
  36.2 0.0 copy-start.15
  36.2 0.0 copy-done
  36.2 0.0 copy-done.19
  36.2 2.7 fusion.b_ref
  38.9 18.5 %point.2.d_ref = bf16[4096,1280]{1,0:T(8,128)(2,1)} custom-call(bf16[4096,1280]{1,0:T(8,128)(2,1)} %bitcast.27, bf16[1280,1280]{1,0:T(8,128)(2,1)} %fusion.b_ref), custom_call_target="tpu_custom_call" | custom-call | flops 17999998976 | bytes 54000000 | tf_op jit(solution)/shard_map/point/pallas_call | solution.py:401
  57.4 0.0 copy-done.17
  57.4 0.0 copy-done.13
  57.4 0.0 copy-done.15
  57.4 11.6 %all-to-all-done.r_ref = bf16[8,2,2,16,1920]{4,3,2,1,0:T(8,128)(2,1)S(1)} async-done(((bf16[8,2,2,16,1920]{4,3,2,1,0:T(8,128)(2,1)}), bf16[8,2,2,16,1920]{4,3,2,1,0:T(8,128)(2,1)S(1)}, u32[]{:S(2)}, u32[]{:S(2)}) %all-to-all-start) | async-done | bytes 1966112 | tf_op jit(solution)/shard_map/all_to_all | solution.py:446
  69.0 0.0 copy-done.12
  69.0 1.5 copy-done.3
  70.6 21.5 %modes.2 = (bf16[4,2,20,2304]{3,2,1,0:T(8,128)(2,1)S(1)}, bf16[8,2,2,16,1920]{4,3,2,1,0:T(8,128)(2,1)}) custom-call(bf16[8,2,2,16,1920]{4,3,2,1,0:T(8,128)(2,1)S(1)} %all-to-all-done.r_ref, bf16[2,20,20,9216]{3,2,1,0:T(8,128)(2,1)} %copy.16.w_ref, bf16[128,128]{1,0:T(8,128)(2,1)S(1)} %copy-done.12, bf16[2,768,640]{2,1,0:T(8,128)(2,1)S(1)} %copy-done.3), custom_call_target="tpu_custom_call" | custom-call | flops 27000000512 | bytes 81000000 | tf_op jit(solution)/shard_map/modes/pallas_call | solution.py:422
  92.1 4.7 %all-to-all-start.1 = ((bf16[8,2,2,16,1920]{4,3,2,1,0:T(8,128)(2,1)}), bf16[8,2,2,16,1920]{4,3,2,1,0:T(8,128)(2,1)}, u32[]{:S(2)}, u32[]{:S(2)}) async-start(bf16[8,2,2,16,1920]{4,3,2,1,0:T(8,128)(2,1)} %get-tuple-element.18), calls=%async_computation.1 | async-start | bytes 3932160 | tf_op jit(solution)/shard_map/all_to_all | solution.py:446
  96.8 0.1 dynamic-slice_bitcast_fusion.4
  96.9 1.6 collective-permute-start
  98.5 1.5 collective-permute-start.1
  100.0 1.4 collective-permute-start.2
  101.4 0.7 broadcast_in_dim.9
  102.2 0.1 reshape_reshape.3.bias_ref
  102.3 3.9 %collective-permute-done = bf16[2,20,2304]{2,1,0:T(8,128)(2,1)S(1)} collective-permute-done((bf16[2,20,2304]{2,1,0:T(8,128)(2,1)S(1)}, bf16[2,20,2304]{2,1,0:T(8,128)(2,1)S(1)}, u32[]{:S(2)}, u32[]{:S(2)}) %collective-permute-start) | collective-permute-done | bytes 184352 | tf_op jit(solution)/shard_map/ppermute | solution.py:459
  106.2 0.8 convert_element_type.34.refs_2_
  107.0 3.3 %collective-permute-done.1 = bf16[2,20,2304]{2,1,0:T(8,128)(2,1)S(1)} collective-permute-done((bf16[2,20,2304]{2,1,0:T(8,128)(2,1)S(1)}, bf16[2,20,2304]{2,1,0:T(8,128)(2,1)S(1)}, u32[]{:S(2)}, u32[]{:S(2)}) %collective-permute-start.1) | collective-permute-done | bytes 184352 | tf_op jit(solution)/shard_map/ppermute | solution.py:459
  110.3 0.8 convert_element_type.35.refs_4_
  111.1 0.0 collective-permute-done.2
  111.1 0.8 convert_element_type.36.refs_6_
  111.9 31.1 %all-to-all-done.1.q_ref = bf16[8,2,2,16,1920]{4,3,2,1,0:T(8,128)(2,1)} async-done(((bf16[8,2,2,16,1920]{4,3,2,1,0:T(8,128)(2,1)}), bf16[8,2,2,16,1920]{4,3,2,1,0:T(8,128)(2,1)}, u32[]{:S(2)}, u32[]{:S(2)}) %all-to-all-start.1) | async-done | bytes 1966112 | tf_op jit(solution)/shard_map/all_to_all | solution.py:446
  143.0 0.0 copy-done.5
  143.1 0.0 copy-done.9
  143.1 1.0 copy-done.10
  144.1 29.7 %middle.1 = (bf16[4096,1280]{1,0:T(8,128)(2,1)}, bf16[8,2,2,16,1920]{4,3,2,1,0:T(8,128)(2,1)}) custom-call(bf16[8,2,2,16,1920]{4,3,2,1,0:T(8,128)(2,1)} %all-to-all-done.1.q_ref, bf16[4096,1280]{1,0:T(8,128)(2,1)} %point.2.d_ref, bf16[4096,1280]{1,0:T(8,128)(2,1)} %bitcast.28, f32[1,1280]{1,0:T(1,128)S(1)} %reshape_reshape.3.bias_ref, ...), custom_call_target="tpu_custom_call" | custom-call | flops 32000000000 | bytes 96000000 | tf_op jit(solution)/shard_map/middle/pallas_call | solution.py:479
  173.8 4.0 %all-to-all-start.2 = ((bf16[8,2,2,16,1920]{4,3,2,1,0:T(8,128)(2,1)}), bf16[8,2,2,16,1920]{4,3,2,1,0:T(8,128)(2,1)S(1)}, u32[]{:S(2)}, u32[]{:S(2)}) async-start(bf16[8,2,2,16,1920]{4,3,2,1,0:T(8,128)(2,1)} %get-tuple-element.22), calls=%async_computation.2 | async-start | bytes 3932160 | tf_op jit(solution)/shard_map/all_to_all | solution.py:446
  177.9 0.0 copy-done.14
  177.9 0.0 copy-done.16
  177.9 0.0 copy-done.18
  177.9 0.0 copy-done.20
  177.9 2.7 fusion.1.b_ref
  180.6 18.5 %point.3.p_ref = bf16[4096,1280]{1,0:T(8,128)(2,1)} custom-call(bf16[4096,1280]{1,0:T(8,128)(2,1)} %get-tuple-element.23.s_ref, bf16[1280,1280]{1,0:T(8,128)(2,1)} %fusion.1.b_ref), custom_call_target="tpu_custom_call" | custom-call | flops 17999998976 | bytes 54000000 | tf_op jit(solution)/shard_map/point/pallas_call | solution.py:401
  199.1 25.0 %all-to-all-done.2.r_ref = bf16[8,2,2,16,1920]{4,3,2,1,0:T(8,128)(2,1)S(1)} async-done(((bf16[8,2,2,16,1920]{4,3,2,1,0:T(8,128)(2,1)}), bf16[8,2,2,16,1920]{4,3,2,1,0:T(8,128)(2,1)S(1)}, u32[]{:S(2)}, u32[]{:S(2)}) %all-to-all-start.2) | async-done | bytes 1966112 | tf_op jit(solution)/shard_map/all_to_all | solution.py:446
  224.0 1.5 copy-done.4
  225.6 22.7 %modes.3 = (bf16[4,2,20,2304]{3,2,1,0:T(8,128)(2,1)S(1)}, bf16[8,2,2,16,1920]{4,3,2,1,0:T(8,128)(2,1)}) custom-call(bf16[8,2,2,16,1920]{4,3,2,1,0:T(8,128)(2,1)S(1)} %all-to-all-done.2.r_ref, bf16[2,20,20,9216]{3,2,1,0:T(8,128)(2,1)} %copy.16.w_ref, bf16[128,128]{1,0:T(8,128)(2,1)S(1)} %copy-done.12, bf16[2,768,640]{2,1,0:T(8,128)(2,1)S(1)} %copy-done.4), custom_call_target="tpu_custom_call" | custom-call | flops 27000000512 | bytes 81000000 | tf_op jit(solution)/shard_map/modes/pallas_call | solution.py:422
  248.3 4.3 %all-to-all-start.3 = ((bf16[8,2,2,16,1920]{4,3,2,1,0:T(8,128)(2,1)}), bf16[8,2,2,16,1920]{4,3,2,1,0:T(8,128)(2,1)}, u32[]{:S(2)}, u32[]{:S(2)}) async-start(bf16[8,2,2,16,1920]{4,3,2,1,0:T(8,128)(2,1)} %get-tuple-element.25), calls=%async_computation.3 | async-start | bytes 3932160 | tf_op jit(solution)/shard_map/all_to_all | solution.py:446
  252.6 0.1 dynamic-slice_bitcast_fusion
  252.7 1.6 collective-permute-start.3
  254.3 1.5 collective-permute-start.4
  255.8 1.6 collective-permute-start.5
  257.4 4.6 %collective-permute-done.3.refs_3_ = bf16[2,20,2304]{2,1,0:T(8,128)(2,1)S(1)} collective-permute-done((bf16[2,20,2304]{2,1,0:T(8,128)(2,1)S(1)}, bf16[2,20,2304]{2,1,0:T(8,128)(2,1)S(1)}, u32[]{:S(2)}, u32[]{:S(2)}) %collective-permute-start.3) | collective-permute-done | bytes 184352 | tf_op jit(solution)/shard_map/ppermute | solution.py:459
  262.0 4.1 %collective-permute-done.4.refs_5_ = bf16[2,20,2304]{2,1,0:T(8,128)(2,1)S(1)} collective-permute-done((bf16[2,20,2304]{2,1,0:T(8,128)(2,1)S(1)}, bf16[2,20,2304]{2,1,0:T(8,128)(2,1)S(1)}, u32[]{:S(2)}, u32[]{:S(2)}) %collective-permute-start.4) | collective-permute-done | bytes 184352 | tf_op jit(solution)/shard_map/ppermute | solution.py:459
  266.1 0.1 collective-permute-done.5.refs_7_
  266.2 1.0 copy-done.2
  267.2 12.5 %weight.1 = f32[2,20,20,2304]{3,2,1,0:T(8,128)} custom-call(f32[2,20,2304]{2,1,0:T(8,128)S(1)} %get-tuple-element.27.refs_0_, bf16[2,20,2304]{2,1,0:T(8,128)(2,1)S(1)} %get-tuple-element.37.refs_1_, f32[2,20,2304]{2,1,0:T(8,128)S(1)} %copy-done.2, bf16[2,20,2304]{2,1,0:T(8,128)(2,1)S(1)} %collective-permute-done.3.refs_3_, ...), custom_call_target="tpu_custom_call" | custom-call | flops 12999999488 | bytes 39000000 | tf_op jit(solution)/shard_map/weight/pallas_call | solution.py:506
  279.7 12.4 %copy.18 = f32[2,20,20,2304]{3,0,2,1:T(2,128)} copy(f32[2,20,20,2304]{3,2,1,0:T(8,128)} %weight.1) | data formatting | bytes 14745600
  292.1 6.8 %all-to-all-done.3.q_ref = bf16[8,2,2,16,1920]{4,3,2,1,0:T(8,128)(2,1)} async-done(((bf16[8,2,2,16,1920]{4,3,2,1,0:T(8,128)(2,1)}), bf16[8,2,2,16,1920]{4,3,2,1,0:T(8,128)(2,1)}, u32[]{:S(2)}, u32[]{:S(2)}) %all-to-all-start.3) | async-done | bytes 1966112 | tf_op jit(solution)/shard_map/all_to_all | solution.py:446
  298.9 0.0 copy-done.6
  298.9 12.8 %final.1 = bf16[4096,1280]{1,0:T(8,128)(2,1)} custom-call(bf16[8,2,2,16,1920]{4,3,2,1,0:T(8,128)(2,1)} %all-to-all-done.3.q_ref, bf16[4096,1280]{1,0:T(8,128)(2,1)} %point.3.p_ref, bf16[2,512,256]{2,1,0:T(8,128)(2,1)S(1)} %copy-done.8, bf16[7,256,256]{2,1,0:T(8,128)(2,1)S(1)} %copy-done.6), custom_call_target="tpu_custom_call" | custom-call | flops 16000000000 | bytes 48000000 | tf_op jit(solution)/shard_map/final/pallas_call | solution.py:495
  311.7 0.0 copy-done.1
  (19 shorter events, 0.0 us)
Async XLA Ops:
  0.6 35.5 %copy-start = (bf16[20,20]{1,0:T(8,128)(2,1)S(1)}, bf16[20,20]{1,0:T(8,128)(2,1)}, u32[]{:S(2)}) copy-start(bf16[20,20]{1,0:T(8,128)(2,1)} %param.17) | copy-start | bytes 2404
  0.6 1.2 copy-start.7
  1.8 1.0 copy-start.11
  16.3 52.7 %all-to-all-start = ((bf16[8,2,2,16,1920]{4,3,2,1,0:T(8,128)(2,1)}), bf16[8,2,2,16,1920]{4,3,2,1,0:T(8,128)(2,1)S(1)}, u32[]{:S(2)}, u32[]{:S(2)}) async-start(bf16[8,2,2,16,1920]{4,3,2,1,0:T(8,128)(2,1)} %analyse.1), calls=%async_computation | async-start | bytes 3932160 | tf_op jit(solution)/shard_map/all_to_all | solution.py:446
  22.8 13.4 %copy-start.19 = (bf16[1280,20]{1,0:T(8,128)(2,1)S(1)}, bf16[1280,20]{1,0:T(8,128)(2,1)}, u32[]{:S(2)}) copy-start(bf16[1280,20]{1,0:T(8,128)(2,1)} %constant.113.clone) | copy-start | bytes 153604
  36.1 21.3 %copy-start.17 = (pred[1280]{0:T(1024)(128)(4,1)}, pred[1280]{0:T(1024)(128)(4,1)S(1)}, u32[]{:S(2)}) copy-start(pred[1280]{0:T(1024)(128)(4,1)S(1)} %fusion.5) | copy-start | bytes 3844
  36.1 21.3 %copy-start.13 = (s32[1280]{0:T(1024)}, s32[1280]{0:T(1024)S(1)}, u32[]{:S(2)}) copy-start(s32[1280]{0:T(1024)S(1)} %get-tuple-element.42) | copy-start | bytes 15364
  36.2 21.3 %copy-start.15 = (s32[1280]{0:T(1024)}, s32[1280]{0:T(1024)S(1)}, u32[]{:S(2)}) copy-start(s32[1280]{0:T(1024)S(1)} %get-tuple-element.43) | copy-start | bytes 15364
  38.9 30.1 %copy-start.12 = (bf16[128,128]{1,0:T(8,128)(2,1)S(1)}, bf16[128,128]{1,0:T(8,128)(2,1)}, u32[]{:S(2)}) copy-start(bf16[128,128]{1,0:T(8,128)(2,1)} %constant.112.clone.gx_ref) | copy-start | bytes 98308
  69.0 1.5 copy-start.3
  92.1 51.0 %copy-start.5 = (bf16[7,256,256]{2,1,0:T(8,128)(2,1)S(1)}, bf16[7,256,256]{2,1,0:T(8,128)(2,1)}, u32[]{:S(2)}) copy-start(bf16[7,256,256]{2,1,0:T(8,128)(2,1)} %constant.110.clone.yi_ref) | copy-start | bytes 2752516
  92.1 51.0 %copy-start.9 = (bf16[2,512,256]{2,1,0:T(8,128)(2,1)S(1)}, bf16[2,512,256]{2,1,0:T(8,128)(2,1)}, u32[]{:S(2)}) copy-start(bf16[2,512,256]{2,1,0:T(8,128)(2,1)} %constant.108.clone.zi_ref) | copy-start | bytes 1572868
  92.1 51.0 %all-to-all-start.1 = ((bf16[8,2,2,16,1920]{4,3,2,1,0:T(8,128)(2,1)}), bf16[8,2,2,16,1920]{4,3,2,1,0:T(8,128)(2,1)}, u32[]{:S(2)}, u32[]{:S(2)}) async-start(bf16[8,2,2,16,1920]{4,3,2,1,0:T(8,128)(2,1)} %get-tuple-element.18), calls=%async_computation.1 | async-start | bytes 3932160 | tf_op jit(solution)/shard_map/all_to_all | solution.py:446
  96.9 9.2 %collective-permute-start = (bf16[2,20,2304]{2,1,0:T(8,128)(2,1)S(1)}, bf16[2,20,2304]{2,1,0:T(8,128)(2,1)S(1)}, u32[]{:S(2)}, u32[]{:S(2)}) collective-permute-start(bf16[2,20,2304]{2,1,0:T(8,128)(2,1)S(1)} %get-tuple-element.40), channel_id=1, source_target_pairs={{0,8},{8,16},{16,24},{24,0},{1,9},{9,17},{17,25},{25,1},{2,10},{10... | collective-permute-start | bytes 552968 | tf_op jit(solution)/shard_map/ppermute | solution.py:459
  98.5 11.8 %collective-permute-start.1 = (bf16[2,20,2304]{2,1,0:T(8,128)(2,1)S(1)}, bf16[2,20,2304]{2,1,0:T(8,128)(2,1)S(1)}, u32[]{:S(2)}, u32[]{:S(2)}) collective-permute-start(bf16[2,20,2304]{2,1,0:T(8,128)(2,1)S(1)} %get-tuple-element.39), channel_id=1, source_target_pairs={{0,16},{8,24},{16,0},{24,8},{1,17},{9,25},{17,1},{25,9},{2,18},{10... | collective-permute-start | bytes 552968 | tf_op jit(solution)/shard_map/ppermute | solution.py:459
  100.0 11.1 %collective-permute-start.2 = (bf16[2,20,2304]{2,1,0:T(8,128)(2,1)S(1)}, bf16[2,20,2304]{2,1,0:T(8,128)(2,1)S(1)}, u32[]{:S(2)}, u32[]{:S(2)}) collective-permute-start(bf16[2,20,2304]{2,1,0:T(8,128)(2,1)S(1)} %get-tuple-element.38), channel_id=1, source_target_pairs={{0,24},{8,0},{16,8},{24,16},{1,25},{9,1},{17,9},{25,17},{2,26},{10... | collective-permute-start | bytes 552968 | tf_op jit(solution)/shard_map/ppermute | solution.py:459
  143.1 1.0 copy-start.10
  144.1 33.8 %copy-start.14 = (s32[1280]{0:T(1024)S(1)}, s32[1280]{0:T(1024)}, u32[]{:S(2)}) copy-start(s32[1280]{0:T(1024)} %copy-done.13) | copy-start | bytes 15364
  144.1 33.8 %copy-start.16 = (s32[1280]{0:T(1024)S(1)}, s32[1280]{0:T(1024)}, u32[]{:S(2)}) copy-start(s32[1280]{0:T(1024)} %copy-done.15) | copy-start | bytes 15364
  144.1 33.8 %copy-start.18 = (pred[1280]{0:T(1024)(128)(4,1)S(1)}, pred[1280]{0:T(1024)(128)(4,1)}, u32[]{:S(2)}) copy-start(pred[1280]{0:T(1024)(128)(4,1)} %copy-done.17) | copy-start | bytes 3844
  144.1 33.8 %copy-start.20 = (bf16[1280,20]{1,0:T(8,128)(2,1)S(1)}, bf16[1280,20]{1,0:T(8,128)(2,1)}, u32[]{:S(2)}) copy-start(bf16[1280,20]{1,0:T(8,128)(2,1)} %constant.113.clone) | copy-start | bytes 153604
  173.8 50.2 %all-to-all-start.2 = ((bf16[8,2,2,16,1920]{4,3,2,1,0:T(8,128)(2,1)}), bf16[8,2,2,16,1920]{4,3,2,1,0:T(8,128)(2,1)S(1)}, u32[]{:S(2)}, u32[]{:S(2)}) async-start(bf16[8,2,2,16,1920]{4,3,2,1,0:T(8,128)(2,1)} %get-tuple-element.22), calls=%async_computation.2 | async-start | bytes 3932160 | tf_op jit(solution)/shard_map/all_to_all | solution.py:446
  224.0 1.5 copy-start.4
  248.3 50.6 %all-to-all-start.3 = ((bf16[8,2,2,16,1920]{4,3,2,1,0:T(8,128)(2,1)}), bf16[8,2,2,16,1920]{4,3,2,1,0:T(8,128)(2,1)}, u32[]{:S(2)}, u32[]{:S(2)}) async-start(bf16[8,2,2,16,1920]{4,3,2,1,0:T(8,128)(2,1)} %get-tuple-element.25), calls=%async_computation.3 | async-start | bytes 3932160 | tf_op jit(solution)/shard_map/all_to_all | solution.py:446
  252.7 9.3 %collective-permute-start.3 = (bf16[2,20,2304]{2,1,0:T(8,128)(2,1)S(1)}, bf16[2,20,2304]{2,1,0:T(8,128)(2,1)S(1)}, u32[]{:S(2)}, u32[]{:S(2)}) collective-permute-start(bf16[2,20,2304]{2,1,0:T(8,128)(2,1)S(1)} %get-tuple-element.36), channel_id=1, source_target_pairs={{0,8},{8,16},{16,24},{24,0},{1,9},{9,17},{17,25},{25,1},{2,10},{10... | collective-permute-start | bytes 552968 | tf_op jit(solution)/shard_map/ppermute | solution.py:459
  254.3 11.8 %collective-permute-start.4 = (bf16[2,20,2304]{2,1,0:T(8,128)(2,1)S(1)}, bf16[2,20,2304]{2,1,0:T(8,128)(2,1)S(1)}, u32[]{:S(2)}, u32[]{:S(2)}) collective-permute-start(bf16[2,20,2304]{2,1,0:T(8,128)(2,1)S(1)} %get-tuple-element.35), channel_id=1, source_target_pairs={{0,16},{8,24},{16,0},{24,8},{1,17},{9,25},{17,1},{25,9},{2,18},{10... | collective-permute-start | bytes 552968 | tf_op jit(solution)/shard_map/ppermute | solution.py:459
  255.8 10.4 %collective-permute-start.5 = (bf16[2,20,2304]{2,1,0:T(8,128)(2,1)S(1)}, bf16[2,20,2304]{2,1,0:T(8,128)(2,1)S(1)}, u32[]{:S(2)}, u32[]{:S(2)}) collective-permute-start(bf16[2,20,2304]{2,1,0:T(8,128)(2,1)S(1)} %get-tuple-element.34), channel_id=1, source_target_pairs={{0,24},{8,0},{16,8},{24,16},{1,25},{9,1},{17,9},{25,17},{2,26},{10... | collective-permute-start | bytes 552968 | tf_op jit(solution)/shard_map/ppermute | solution.py:459
  266.2 1.0 copy-start.2
  279.7 19.2 %copy-start.6 = (bf16[7,256,256]{2,1,0:T(8,128)(2,1)S(1)}, bf16[7,256,256]{2,1,0:T(8,128)(2,1)}, u32[]{:S(2)}) copy-start(bf16[7,256,256]{2,1,0:T(8,128)(2,1)} %constant.110.clone.yi_ref) | copy-start | bytes 2752516
  279.7 19.2 %copy-start.8 = (bf16[2,512,256]{2,1,0:T(8,128)(2,1)S(1)}, bf16[2,512,256]{2,1,0:T(8,128)(2,1)}, u32[]{:S(2)}) copy-start(bf16[2,512,256]{2,1,0:T(8,128)(2,1)} %constant.107.clone.zi_ref) | copy-start | bytes 1572868
  298.9 12.8 %copy-start.1 = (bf16[20,20]{1,0:T(8,128)(2,1)S(1)}, bf16[20,20]{1,0:T(8,128)(2,1)}, u32[]{:S(2)}) copy-start(bf16[20,20]{1,0:T(8,128)(2,1)} %param.17) | copy-start | bytes 2404
